TPU v7x, 128 devices: a whole 4x4x4 slice. The times are simulated.
128 devices in a mesh: comp: 32 (over x, z_hi, y), band: 4 (over z_lo, core).
Axes of the slice: x: 4, y: 4, z: 4 (z_hi: 2, z_lo: 2; z = z_hi * 2 + z_lo), core: 2. Of those that a mesh axis runs over, the one named last changes fastest.
Arguments:
- spectrum: float32 [1152, 384, 256], P('comp', 'band'), as said below
- wet_mask: int32 [384, 256], P('band'), may hold values 0 or 1
- quad_matrix: bfloat16 [1152, 1152], replicated, may hold values from -0.1875 to 0.1875
- dissipation: float32 [1152], replicated, may hold values from 0.2 to 2
- circulation: float32 [3, 32, 4096], P(None, 'band', 'comp'), may hold values from -3 to 3
- source_points: int32 [3, 32, 4096], P(None, 'band', 'comp'), may hold values from 0 to 24575
Outputs:
- spectrum_out: float32 [1152, 384, 256], P('comp', 'band')
- circulation_out: float32 [3, 32, 4096], P(None, 'band', 'comp')
Inputs may be any that keep to these rules, and one draw needn't show every extreme that they name: `spectrum`: every entry is positive. `source_points`: each entry numbers a wave point of the band that holds the cell's row, row by row within the band.
All inputs are finite; a program needn't handle non-finite values. No bound on the sum of `wet_mask` on one device may be relied on, other than what follows from the above.
Results may differ from a plain program's by a relative error of at most 0.007.
Values may be sent and summed in bfloat16 or wider, within the bound.
No kernel may reach another device: no remote copies, remote signals or barrier semaphores. Data moves between devices by JAX's collectives and lax.ppermute only.
A program may use at most 128 MiB of HBM per device.

v0:
```python
import math

import jax
import jax.numpy as jnp
from jax import lax
from jax.sharding import PartitionSpec as P

NF = 36
ND = 32
SUBSTEPS = 4
SRC_STEPS = 4
SW_STEPS = 8


step_source = 0.1
wave_speed = 0.35
friction = 0.05
forcing_gain = 0.15


def extended_2(cells, sides, width):
    for axis, dim in sides:
        count = lax.axis_size(axis)
        ends = count - 1
        head = lax.slice_in_dim(cells, 0, width, axis=dim)
        tail = lax.slice_in_dim(cells, cells.shape[dim] - width, cells.shape[dim], axis=dim)
        cells = jnp.concatenate(
            [
                lax.ppermute(tail, axis, [(i, (i + 1) % count) for i in range(ends)]),
                cells,
                lax.ppermute(head, axis, [((i + 1) % count, i) for i in range(ends)]),
            ],
            axis=dim,
        )
    return cells


def from_everyone(shard, axis):
    size = lax.axis_size(axis)
    return lax.all_to_all(
        jnp.broadcast_to(shard[None], (size, *shard.shape)), axis, 0, 0, tiled=True
    )


def joined_along(blocks, dim):
    lengths = list(blocks.shape[1:])
    lengths[dim] *= blocks.shape[0]
    return jnp.moveaxis(blocks, 0, dim).reshape(lengths)


def gather_directly(shard, axis, dim):
    blocks = from_everyone(shard, axis)
    return joined_along(blocks, dim)


def side_by_side(arrays, axis, dim, along):
    ends, at = ([], 0)
    for a in arrays[:-1]:
        at += a.shape[along]
        ends.append(at)
    both = jnp.concatenate(arrays, axis=along)
    return tuple(jnp.split(lax.all_gather(both, axis, axis=dim, tiled=True), ends, axis=along))


def component_tables(offset, local_count, freqs, headings):
    indices = offset + jnp.arange(local_count, dtype=jnp.int32)
    frequency = (indices // headings).astype(jnp.float32)
    heading = (indices % headings).astype(jnp.float32)
    heading_angle = 2.0 * math.pi * (heading + 0.5) / headings
    fraction = (frequency + 0.5) / freqs
    group_speed = 0.25 + 0.4 * fraction
    wave_ratio = 0.5 + 0.5 * fraction
    cosine = jnp.cos(heading_angle)
    sine_part = jnp.sin(heading_angle)
    speed_east = group_speed * cosine
    speed_north = group_speed * sine_part
    stress_coef = jnp.stack(
        [
            wave_ratio * (1.0 + cosine * cosine) - 0.5,
            wave_ratio * sine_part * cosine,
            wave_ratio * (1.0 + sine_part * sine_part) - 0.5,
        ]
    )
    return (speed_east, speed_north, stress_coef)


def upwind(extended, speed_east, speed_north, wet_rows):
    middle = extended[:, 1:-1, :]
    west_cells = extended[:, :-2, :]
    east_cells = extended[:, 2:, :]
    padded = jnp.pad(middle, ((0, 0), (0, 0), (1, 1)))
    south_cells = padded[:, :, :-2]
    north_cells = padded[:, :, 2:]
    along_rows = speed_east[:, None, None]
    along_cols = speed_north[:, None, None]
    flux_rows = jnp.maximum(along_rows, 0.0) * (middle - west_cells) + jnp.minimum(
        along_rows, 0.0
    ) * (east_cells - middle)
    flux_cols = jnp.maximum(along_cols, 0.0) * (middle - south_cells) + jnp.minimum(
        along_cols, 0.0
    ) * (north_cells - middle)
    return (middle - flux_rows - flux_cols) * wet_rows


def sources(base, quad_matrix, dissipation):
    current = base
    for repeat in range(SRC_STEPS):
        product = jnp.dot(
            quad_matrix, current.astype(jnp.bfloat16), preferred_element_type=jnp.float32
        )
        energy_level = jnp.mean(current, axis=0, keepdims=True)
        current = current + step_source * current * (product - dissipation[:, None] * energy_level)
    return current


def diff_rows(extended):
    return 0.5 * (extended[2:, 1:-1] - extended[:-2, 1:-1])


def diff_cols(extended):
    return 0.5 * (extended[1:-1, 2:] - extended[1:-1, :-2])


def on_device(spectrum, wet_mask, quad_matrix, dissipation, circulation, source_points):
    local_count = spectrum.shape[0]
    row_count = spectrum.shape[1]
    columns = spectrum.shape[2]
    groups = lax.axis_size("comp")
    component_total = local_count * groups
    offset = lax.axis_index("comp") * local_count
    speed_east, speed_north, stress_coef = component_tables(offset, local_count, NF, ND)
    wetness = wet_mask.astype(jnp.float32)[None]
    density = spectrum
    deep_field, deep_wet = (
        extended_2(density, (("band", 1),), SUBSTEPS),
        extended_2(wetness, (("band", 1),), SUBSTEPS),
    )
    for substep in range(SUBSTEPS):
        margin = substep + 1
        deep_field = upwind(
            deep_field, speed_east, speed_north, deep_wet[:, margin : deep_wet.shape[1] - margin, :]
        )
    density = deep_field
    sent_block = lax.optimization_barrier(density.astype(jnp.bfloat16)).reshape(
        local_count, groups, -1
    )
    base = lax.all_to_all(sent_block, "comp", split_axis=1, concat_axis=0, tiled=True)[
        :, 0, :
    ].astype(jnp.float32)
    current = sources(base, quad_matrix, dissipation)
    increment = (current - base).astype(jnp.bfloat16)
    returned = lax.all_to_all(
        increment[:, None, :], "comp", split_axis=0, concat_axis=1, tiled=True
    )
    full_coef = component_tables(0, component_total, NF, ND)[2]
    coupled = base + increment.astype(jnp.float32)
    stress_here = jnp.dot(full_coef, coupled, precision=lax.Precision.HIGHEST) / component_total
    outcome = (returned, stress_here[:, None, :])
    returned, stress_part = outcome
    band_stress = gather_directly(stress_part, "comp", 1).reshape(3, -1)
    increment_back = returned.reshape(local_count, row_count, columns).astype(jnp.float32)
    new_spectrum = density + increment_back
    tile_rows = circulation.shape[1]
    tile_cols = circulation.shape[2]
    picked = jnp.take(band_stress, source_points.reshape(-1), axis=1).reshape(
        3, 3, tile_rows, tile_cols
    )
    cell_stress = 0.5 * picked[:, 0] + 0.3 * picked[:, 1] + 0.2 * picked[:, 2]
    margin_cols = 2 * SW_STEPS + 1
    whole_state, whole_stress = side_by_side((circulation, cell_stress), "band", 1, 0)
    wide_state, wide_stress = (
        extended_2(whole_state, (("comp", 2),), margin_cols),
        extended_2(whole_stress, (("comp", 2),), margin_cols),
    )
    wide_cols = wide_state.shape[2]
    global_col = (
        lax.axis_index("comp") * tile_cols - margin_cols + jnp.arange(wide_cols, dtype=jnp.int32)
    )
    inside = ((global_col >= 0) & (global_col < tile_cols * groups)).astype(jnp.float32)[None, :]
    rimmed = jnp.pad(wide_stress, ((0, 0), (1, 1), (1, 1)))
    force_down = -(diff_rows(rimmed[0]) + diff_cols(rimmed[1]))
    force_across = -(diff_rows(rimmed[1]) + diff_cols(rimmed[2]))
    height = wide_state[0]
    flow_down = wide_state[1]
    flow_across = wide_state[2]
    for repeat in range(SW_STEPS):
        down_ext = jnp.pad(flow_down, 1)
        across_ext = jnp.pad(flow_across, 1)
        height = (height - wave_speed * (diff_rows(down_ext) + diff_cols(across_ext))) * inside
        height_ext = jnp.pad(height, 1)
        flow_down = (
            (1.0 - friction) * flow_down
            - wave_speed * diff_rows(height_ext)
            + forcing_gain * force_down
        ) * inside
        flow_across = (
            (1.0 - friction) * flow_across
            - wave_speed * diff_cols(height_ext)
            + forcing_gain * force_across
        ) * inside
    stacked = jnp.stack([height, flow_down, flow_across])
    row_start = lax.axis_index("band") * tile_rows
    own_rows = lax.dynamic_slice_in_dim(stacked, row_start, tile_rows, 1)
    return (new_spectrum, own_rows[:, :, margin_cols : margin_cols + tile_cols])


def solution(mesh):
    in_specs = (
        P("comp", "band", None),
        P("band", None),
        P(),
        P(),
        P(None, "band", "comp"),
        P(None, "band", "comp"),
    )
    out_specs = (P("comp", "band", None), P(None, "band", "comp"))
    return jax.shard_map(
        on_device, mesh=mesh, in_specs=in_specs, out_specs=out_specs, check_vma=False
    )
```

profile of v0, /device:TPU:6, one launch (start us, length us, event | category | flops | bytes accessed | tf_op | source)
XLA Modules:
  0.0 229.5 jit_solution(7555750817525466782)
XLA Ops:
  0.6 1.3 fusion.230
  1.9 1.3 collective-permute-start.1
  3.2 3.0 %collective-permute-start = (f32[36,4,256]{2,1,0:T(4,128)S(1)}, f32[36,4,256]{2,1,0:T(4,128)S(1)}, u32[]{:S(2)}, u32[]{:S(2)}) collective-permute-start(f32[36,4,256]{2,1,0:T(4,128)S(1)} %get-tuple-element.8), channel_id=1, source_target_pairs={{0,1},{1,2},{2,3},{4,5},{5,6},{6,7},{8,9},{9,10},{10,11},{12,13},{... | collective-permute-start | bytes 442376 | tf_op jit(solution)/shard_map/ppermute | solution.py:29
  6.3 0.9 convert_bitcast_fusion.1
  7.2 1.3 collective-permute-start.3
  8.5 4.1 %collective-permute-start.2 = (f32[1,4,256]{2,1,0:T(4,128)S(1)}, f32[1,4,256]{2,1,0:T(4,128)S(1)}, u32[]{:S(2)}, u32[]{:S(2)}) collective-permute-start(f32[1,4,256]{2,1,0:T(4,128)S(1)} %get-tuple-element.23), channel_id=1, source_target_pairs={{0,1},{1,2},{2,3},{4,5},{5,6},{6,7},{8,9},{9,10},{10,11},{12,13},{... | collective-permute-start | bytes 12296 | tf_op jit(solution)/shard_map/ppermute | solution.py:29
  12.7 0.7 collective-permute-done.2
  13.5 2.3 %pad_maximum_fusion = f32[36,104,256]{2,1,0:T(8,128)S(1)} fusion(f32[36,4,256]{2,1,0:T(4,128)S(1)} %collective-permute-done.1, f32[36,96,256]{2,1,0:T(8,128)} %param.6, f32[36,4,256]{2,1,0:T(4,128)S(1)} %collective-permute-done), kind=kLoop, calls=%fused_computation.53 | loop fusion | flops 1916928 | bytes 7667712 | tf_op jit(solution)/shard_map/concatenate | solution.py:27
  15.8 0.3 slice.459
  16.1 4.2 %fusion.4 = f32[36,102,256]{2,1,0:T(8,128)S(1)} fusion(f32[36,102,256]{2,1,0:T(8,128)S(1)} %slice.459, f32[36,104,256]{2,1,0:T(8,128)S(1)} %pad_maximum_fusion, f32[102,256]{1,0:T(8,128)S(1)} %slice_bitcast_fusion.2, f32[36]{0:T(128)S(1)} %get-tuple-element.47, f32[36]{0:T(128)S(1)} %get-tuple-element.48, f32[36]{0:T(128)S(1)} %get-tuple-element.49, ...), kind=kLoop, calls=%fused_computation.18 | loop fusion | flops 12220416 | bytes 15145536 | tf_op jit(solution)/shard_map/mul | solution.py:102
  20.3 0.3 slice.465
  20.6 4.2 %fusion.11 = f32[36,100,256]{2,1,0:T(8,128)S(1)} fusion(f32[36,100,256]{2,1,0:T(8,128)S(1)} %slice.465, f32[36,102,256]{2,1,0:T(8,128)S(1)} %fusion.4, f32[100,256]{1,0:T(8,128)S(1)} %slice_bitcast_fusion.1, f32[36]{0:T(128)S(1)} %get-tuple-element.47, f32[36]{0:T(128)S(1)} %get-tuple-element.48, f32[36]{0:T(128)S(1)} %get-tuple-element.49, ...), kind=kLoop, calls=%fused_computation.25 | loop fusion | flops 11980800 | bytes 14848576 | tf_op jit(solution)/shard_map/mul | solution.py:102
  24.8 0.3 slice.469
  25.1 4.2 %fusion.18 = f32[36,98,256]{2,1,0:T(8,128)S(1)} fusion(f32[36,98,256]{2,1,0:T(8,128)S(1)} %slice.469, f32[36,100,256]{2,1,0:T(8,128)S(1)} %fusion.11, f32[98,256]{1,0:T(8,128)S(1)} %slice_bitcast_fusion, f32[36]{0:T(128)S(1)} %get-tuple-element.47, f32[36]{0:T(128)S(1)} %get-tuple-element.48, f32[36]{0:T(128)S(1)} %get-tuple-element.49, ...), kind=kLoop, calls=%fused_computation.32 | loop fusion | flops 11741184 | bytes 14551616 | tf_op jit(solution)/shard_map/mul | solution.py:102
  29.3 0.5 slice.473
  29.8 5.6 %fusion.228 = (bf16[36,96,256]{2,1,0:T(8,128)(2,1)}, f32[36,96,256]{2,1,0:T(8,128)}) fusion(f32[96,256]{1,0:T(8,128)S(1)} %get-tuple-element.26, f32[36,96,256]{2,1,0:T(8,128)S(1)} %slice.473, f32[36]{0:T(128)S(1)} %get-tuple-element.47, f32[36]{0:T(128)S(1)} %get-tuple-element.48, f32[36,98,256]{2,1,0:T(8,128)S(1)} %fusion.18, ...), kind=kLoop, calls=%fused_computation.378 | loop fusion | flops 12386304 | bytes 16024128 | tf_op jit(solution)/shard_map/convert_element_type | solution.py:144
  35.5 3.8 %reshape.257 = bf16[36,32,768]{2,1,0:T(8,128)(2,1)} reshape(bf16[36,96,256]{2,1,0:T(8,128)(2,1)} %get-tuple-element.6) | data formatting | bytes 3538944 | tf_op jit(solution)/shard_map/reshape | solution.py:144
  39.3 3.7 %copy.23 = bf16[36,32,768]{2,0,1:T(8,128)(2,1)} copy(bf16[36,32,768]{2,1,0:T(8,128)(2,1)} %reshape.257) | data formatting | bytes 3538944 | tf_op jit(solution)/shard_map/reshape | solution.py:144
  43.0 10.7 %all-to-all-start = ((bf16[36,32,768]{2,0,1:T(8,128)(2,1)}), bf16[36,32,768]{2,0,1:T(8,128)(2,1)}, u32[]{:S(2)}, u32[]{:S(2)}) async-start(bf16[36,32,768]{2,0,1:T(8,128)(2,1)} %copy.23), calls=%async_computation | async-start | bytes 3932160 | tf_op jit(solution)/shard_map/all_to_all | solution.py:147
  53.7 0.2 multiply_add_fusion.1
  53.9 0.2 multiply_add_fusion
  54.1 27.1 %all-to-all-done = bf16[36,32,768]{2,0,1:T(8,128)(2,1)} async-done(((bf16[36,32,768]{2,0,1:T(8,128)(2,1)}), bf16[36,32,768]{2,0,1:T(8,128)(2,1)}, u32[]{:S(2)}, u32[]{:S(2)}) %all-to-all-start) | async-done | bytes 1769504 | tf_op jit(solution)/shard_map/all_to_all | solution.py:147
  81.2 3.6 %squeeze.25 = bf16[1152,768]{1,0:T(8,128)(2,1)} reshape(bf16[32,36,1,768]{3,1,0,2:T(8,128)(2,1)} %bitcast.5) | data formatting | bytes 3538944 | tf_op jit(solution)/shard_map/squeeze | solution.py:147
  84.9 3.9 %copy.24 = bf16[1152,768]{0,1:T(8,128)(2,1)} copy(bf16[1152,768]{1,0:T(8,128)(2,1)} %squeeze.25) | data formatting | bytes 3538944 | tf_op jit(solution)/shard_map/squeeze | solution.py:147
  88.8 1.9 convert_reduce_fusion
  90.7 5.4 %fusion.234 = (f32[768]{0:T(1024)S(1)}, f32[1152,768]{0,1:T(8,128)S(1)}) fusion(f32[768]{0:T(1024)S(1)} %broadcast_multiply_fusion.3, f32[1152]{0:T(1024)S(1)} %copy-done.5, bf16[1152,768]{1,0:T(8,128)(2,1)} %squeeze.25, bf16[1152,1152]{1,0:T(8,128)(2,1)S(1)} %copy-done, bf16[1152,768]{0,1:T(8,128)(2,1)} %copy.24), kind=kOutput, calls=%fused_computation.383 | convolution fusion | flops 2044624128 | bytes 9742848 | tf_op jit(solution)/shard_map/dot_general | solution.py:108
  96.2 3.0 %fusion.235 = (f32[768]{0:T(1024)S(1)}, f32[1152,768]{0,1:T(8,128)S(1)}) fusion(f32[1152,768]{0,1:T(8,128)S(1)} %get-tuple-element.42, f32[768]{0:T(1024)S(1)} %broadcast_multiply_fusion.2, f32[1152]{0:T(1024)S(1)} %copy-done.5, bf16[1152,1152]{1,0:T(8,128)(2,1)S(1)} %copy-done), kind=kOutput, calls=%fused_computation.384 | convolution fusion | flops 2044624128 | bytes 9742848 | tf_op jit(solution)/shard_map/dot_general | solution.py:108
  99.1 2.9 %fusion.236 = (f32[768]{0:T(1024)S(1)}, f32[1152,768]{0,1:T(8,128)S(1)}) fusion(f32[1152,768]{0,1:T(8,128)S(1)} %get-tuple-element.44, f32[768]{0:T(1024)S(1)} %broadcast_multiply_fusion.1, f32[1152]{0:T(1024)S(1)} %copy-done.5, bf16[1152,1152]{1,0:T(8,128)(2,1)S(1)} %copy-done), kind=kOutput, calls=%fused_computation.385 | convolution fusion | flops 2044624128 | bytes 9742848 | tf_op jit(solution)/shard_map/dot_general | solution.py:108
  102.1 3.0 %fusion.57 = bf16[1152,768]{0,1:T(8,128)(2,1)S(1)} fusion(bf16[1152,768]{0,1:T(8,128)(2,1)S(1)} %copy-done.1, f32[1152,768]{0,1:T(8,128)S(1)} %get-tuple-element.46, bf16[1152,1152]{1,0:T(8,128)(2,1)S(1)} %copy-done, f32[768]{0:T(1024)S(1)} %broadcast_multiply_fusion, f32[1152]{0:T(1024)S(1)} %copy-done.5), kind=kOutput, calls=%fused_computation.85 | convolution fusion | flops 2046394368 | bytes 9739776 | tf_op jit(solution)/shard_map/dot_general | solution.py:108
  105.1 3.2 %fusion.61 = f32[3,768]{1,0:T(4,128)S(1)} fusion(bf16[1152,768]{0,1:T(8,128)(2,1)S(1)} %copy-done.1, bf16[1152,768]{0,1:T(8,128)(2,1)S(1)} %fusion.57, f32[1,1152]{1,0:T(1,128)S(1)} %get-tuple-element.51, f32[1,1152]{1,0:T(1,128)S(1)} %get-tuple-element.52, f32[1,1152]{1,0:T(1,128)S(1)} %multiply_add_fusion.1), kind=kOutput, calls=%fused_computation.89 | convolution fusion | flops 34513920 | bytes 3561984 | tf_op jit(solution)/shard_map/dot_general | solution.py:157
  108.3 0.9 broadcast_in_dim.16
  109.2 8.7 %all-to-all-start.2 = ((f32[32,3,1,768]{3,2,1,0:T(1,128)}), f32[32,3,1,768]{3,2,1,0:T(1,128)S(1)}, u32[]{:S(2)}, u32[]{:S(2)}) async-start(f32[32,3,1,768]{3,2,1,0:T(1,128)} %broadcast_in_dim.16), calls=%async_computation.2 | async-start | bytes 589824 | tf_op jit(solution)/shard_map/all_to_all | solution.py:40
  117.9 0.5 broadcast.839
  118.4 4.1 %reduce.1 = bf16[1152,768]{0,1:T(8,128)(2,1)} reduce(bf16[1152,1,768]{0,2,1:T(8,128)(2,1)} %bitcast.98, bf16[]{:T(256)} %broadcast.839), dimensions={1}, to_apply=%copy.25.reduce_sub_computation | reduce | bytes 3538946 | tf_op jit(solution)/shard_map/broadcast_in_dim | solution.py:153
  122.6 3.9 %copy.29 = bf16[1152,768]{1,0:T(8,128)(2,1)} copy(bf16[1152,768]{0,1:T(8,128)(2,1)} %reduce.1) | data formatting | bytes 3538944
  126.4 4.8 %reshape.269 = bf16[32,2,13824]{2,1,0:T(2,128)(2,1)} reshape(bf16[1152,768]{1,0:T(8,128)(2,1)} %copy.29) | data formatting | bytes 3538944
  131.2 9.8 %all-to-all-start.1 = ((bf16[32,2,13824]{2,1,0:T(2,128)(2,1)}), bf16[32,2,13824]{2,1,0:T(2,128)(2,1)}, u32[]{:S(2)}, u32[]{:S(2)}) async-start(bf16[32,2,13824]{2,1,0:T(2,128)(2,1)} %reshape.269), calls=%async_computation.1 | async-start | bytes 3538944 | tf_op jit(solution)/shard_map/all_to_all | solution.py:152
  141.1 6.7 %copy.27 = f32[3,32,1,768]{0,3,1,2:T(8,128)} copy(f32[3,32,1,768]{3,2,0,1:T(1,128)S(1)} %bitcast.100) | data formatting | bytes 589824 | tf_op jit(solution)/shard_map/transpose | solution.py:48
  147.8 15.4 %gather_fusion = f32[3072,3]{1,0:T(8,128)} fusion(f32[3,24576]{0,1:T(8,128)} %bitcast.97, s32[3072]{0:T(1024)S(1)} %broadcast_clamp_fusion), kind=kCustom, calls=%fused_computation | custom fusion | bytes 86016 | tf_op jit(solution)/shard_map/jit(_take)/gather | solution.py:165
  163.1 1.9 copy.28
  165.1 5.3 %all_gather.3 = f32[6,32,128]{2,1,0:T(8,128)S(1)} all-gather(f32[6,8,128]{2,1,0:T(8,128)S(1)} %pad_maximum_fusion.3), channel_id=1, replica_groups=mesh['comp'=32,'band'=4] {'band'}, dimensions={1}, use_global_device_ids=true | all-gather | bytes 122880 | tf_op jit(solution)/shard_map/all_gather | solution.py:62
  170.5 7.3 %collective-permute-start.5 = (f32[3,32,17]{2,1,0:T(8,128)S(1)}, f32[3,32,17]{2,1,0:T(8,128)S(1)}, u32[]{:S(2)}, u32[]{:S(2)}) collective-permute-start(f32[3,32,17]{2,1,0:T(8,128)S(1)} %get-tuple-element.17), channel_id=1, source_target_pairs={{4,0},{8,4},{12,8},{16,12},{20,16},{24,20},{28,24},{32,28},{36,32}... | collective-permute-start | bytes 19592 | tf_op jit(solution)/shard_map/ppermute | solution.py:31
  177.8 1.9 collective-permute-start.4
  179.7 8.4 %collective-permute-start.7 = (f32[3,32,17]{2,1,0:T(8,128)S(1)}, f32[3,32,17]{2,1,0:T(8,128)S(1)}, u32[]{:S(2)}, u32[]{:S(2)}) collective-permute-start(f32[3,32,17]{2,1,0:T(8,128)S(1)} %get-tuple-element.16), channel_id=1, source_target_pairs={{4,0},{8,4},{12,8},{16,12},{20,16},{24,20},{28,24},{32,28},{36,32}... | collective-permute-start | bytes 19592 | tf_op jit(solution)/shard_map/ppermute | solution.py:31
  188.2 1.9 collective-permute-start.6
  190.1 0.1 pad_maximum_fusion.2
  190.2 8.4 %collective-permute-done.6 = f32[3,32,17]{2,1,0:T(8,128)S(1)} collective-permute-done((f32[3,32,17]{2,1,0:T(8,128)S(1)}, f32[3,32,17]{2,1,0:T(8,128)S(1)}, u32[]{:S(2)}, u32[]{:S(2)}) %collective-permute-start.6) | collective-permute-done | bytes 6560 | tf_op jit(solution)/shard_map/ppermute | solution.py:29
  198.7 0.1 select_maximum_fusion
  198.9 0.1 fusion.122
  199.2 0.1 fusion.132
  199.3 0.1 fusion.81
  199.3 0.1 fusion.142
  199.5 0.1 fusion.152
  199.6 0.1 fusion.93
  199.7 0.1 fusion.162
  199.9 0.1 fusion.172
  200.1 0.1 fusion.182
  200.3 0.1 fusion.194
  200.4 0.7 fusion.209
  201.1 10.1 %reshape.270 = bf16[1152,1,768]{2,1,0:T(2,128)(2,1)} reshape(bf16[32,2,13824]{2,1,0:T(2,128)(2,1)} %all-to-all-done.1) | data formatting | bytes 3538944
  211.1 5.6 %convert_bitcast_fusion = f32[36,32,1,768]{3,2,0,1:T(1,128)S(1)} fusion(bf16[32,36,1,768]{3,2,1,0:T(2,128)(2,1)} %bitcast.96), kind=kLoop, calls=%fused_computation.83 | loop fusion | flops 884736 | bytes 5308416 | tf_op jit(solution)/shard_map/convert_element_type | solution.py:161
  216.8 2.4 %copy.26 = f32[36,32,1,768]{3,1,0,2:T(8,128)} copy(f32[36,32,1,768]{3,2,0,1:T(1,128)S(1)} %convert_bitcast_fusion) | data formatting | bytes 7077888 | tf_op jit(solution)/shard_map/convert_element_type | solution.py:161
  219.2 4.8 %reshape.259 = f32[36,96,256]{2,1,0:T(8,128)} reshape(f32[36,32,1,768]{3,1,0,2:T(8,128)} %copy.26) | data formatting | bytes 7077888 | tf_op jit(solution)/shard_map/convert_element_type | solution.py:161
  224.0 5.5 %add.483 = f32[36,96,256]{2,1,0:T(8,128)} add(f32[36,96,256]{2,1,0:T(8,128)} %get-tuple-element.7, f32[36,96,256]{2,1,0:T(8,128)} %reshape.259) | non-fusion elementwise | flops 884736 | bytes 10616832 | tf_op jit(solution)/shard_map/add | solution.py:162
  (48 shorter events, 0.9 us)
Async XLA Ops:
  0.6 90.1 %copy-start = (bf16[1152,1152]{1,0:T(8,128)(2,1)S(1)}, bf16[1152,1152]{1,0:T(8,128)(2,1)}, u32[]{:S(2)}) copy-start(bf16[1152,1152]{1,0:T(8,128)(2,1)} %param.8) | copy-start | bytes 7962628
  1.9 11.5 %collective-permute-start.1 = (f32[36,4,256]{2,1,0:T(4,128)S(1)}, f32[36,4,256]{2,1,0:T(4,128)S(1)}, u32[]{:S(2)}, u32[]{:S(2)}) collective-permute-start(f32[36,4,256]{2,1,0:T(4,128)S(1)} %get-tuple-element.9), channel_id=1, source_target_pairs={{1,0},{2,1},{3,2},{5,4},{6,5},{7,6},{9,8},{10,9},{11,10},{13,12},{... | collective-permute-start | bytes 442376 | tf_op jit(solution)/shard_map/ppermute | solution.py:31
  3.2 10.2 %collective-permute-start = (f32[36,4,256]{2,1,0:T(4,128)S(1)}, f32[36,4,256]{2,1,0:T(4,128)S(1)}, u32[]{:S(2)}, u32[]{:S(2)}) collective-permute-start(f32[36,4,256]{2,1,0:T(4,128)S(1)} %get-tuple-element.8), channel_id=1, source_target_pairs={{0,1},{1,2},{2,3},{4,5},{5,6},{6,7},{8,9},{9,10},{10,11},{12,13},{... | collective-permute-start | bytes 442376 | tf_op jit(solution)/shard_map/ppermute | solution.py:29
  7.2 5.5 %collective-permute-start.3 = (f32[1,4,256]{2,1,0:T(4,128)S(1)}, f32[1,4,256]{2,1,0:T(4,128)S(1)}, u32[]{:S(2)}, u32[]{:S(2)}) collective-permute-start(f32[1,4,256]{2,1,0:T(4,128)S(1)} %get-tuple-element.24), channel_id=1, source_target_pairs={{1,0},{2,1},{3,2},{5,4},{6,5},{7,6},{9,8},{10,9},{11,10},{13,12},{... | collective-permute-start | bytes 12296 | tf_op jit(solution)/shard_map/ppermute | solution.py:31
  8.5 4.9 %collective-permute-start.2 = (f32[1,4,256]{2,1,0:T(4,128)S(1)}, f32[1,4,256]{2,1,0:T(4,128)S(1)}, u32[]{:S(2)}, u32[]{:S(2)}) collective-permute-start(f32[1,4,256]{2,1,0:T(4,128)S(1)} %get-tuple-element.23), channel_id=1, source_target_pairs={{0,1},{1,2},{2,3},{4,5},{5,6},{6,7},{8,9},{9,10},{10,11},{12,13},{... | collective-permute-start | bytes 12296 | tf_op jit(solution)/shard_map/ppermute | solution.py:29
  39.3 14.6 %copy-start.3 = (s32[3,8,128]{2,1,0:T(8,128)S(1)}, s32[3,8,128]{2,1,0:T(8,128)}, u32[]{:S(2)}) copy-start(s32[3,8,128]{2,1,0:T(8,128)} %param.11) | copy-start | bytes 36868
  43.0 38.2 %all-to-all-start = ((bf16[36,32,768]{2,0,1:T(8,128)(2,1)}), bf16[36,32,768]{2,0,1:T(8,128)(2,1)}, u32[]{:S(2)}, u32[]{:S(2)}) async-start(bf16[36,32,768]{2,0,1:T(8,128)(2,1)} %copy.23), calls=%async_computation | async-start | bytes 3932160 | tf_op jit(solution)/shard_map/all_to_all | solution.py:147
  84.9 5.8 %copy-start.5 = (f32[1152]{0:T(1024)S(1)}, f32[1152]{0:T(1024)}, u32[]{:S(2)}) copy-start(f32[1152]{0:T(1024)} %param.9) | copy-start | bytes 13828
  99.1 3.0 %copy-start.1 = (bf16[1152,768]{0,1:T(8,128)(2,1)S(1)}, bf16[1152,768]{0,1:T(8,128)(2,1)}, u32[]{:S(2)}) copy-start(bf16[1152,768]{0,1:T(8,128)(2,1)} %copy.24) | copy-start | bytes 5308420
  105.1 3.2 %copy-start.2 = (bf16[1152,768]{0,1:T(8,128)(2,1)}, bf16[1152,768]{0,1:T(8,128)(2,1)S(1)}, u32[]{:S(2)}) copy-start(bf16[1152,768]{0,1:T(8,128)(2,1)S(1)} %fusion.57) | copy-start | bytes 5308420
  109.2 22.0 %all-to-all-start.2 = ((f32[32,3,1,768]{3,2,1,0:T(1,128)}), f32[32,3,1,768]{3,2,1,0:T(1,128)S(1)}, u32[]{:S(2)}, u32[]{:S(2)}) async-start(f32[32,3,1,768]{3,2,1,0:T(1,128)} %broadcast_in_dim.16), calls=%async_computation.2 | async-start | bytes 589824 | tf_op jit(solution)/shard_map/all_to_all | solution.py:40
  131.2 69.9 %all-to-all-start.1 = ((bf16[32,2,13824]{2,1,0:T(2,128)(2,1)}), bf16[32,2,13824]{2,1,0:T(2,128)(2,1)}, u32[]{:S(2)}, u32[]{:S(2)}) async-start(bf16[32,2,13824]{2,1,0:T(2,128)(2,1)} %reshape.269), calls=%async_computation.1 | async-start | bytes 3538944 | tf_op jit(solution)/shard_map/all_to_all | solution.py:152
  141.1 24.0 %copy-start.4 = (f32[3,8,128]{2,1,0:T(8,128)S(1)}, f32[3,8,128]{2,1,0:T(8,128)}, u32[]{:S(2)}) copy-start(f32[3,8,128]{2,1,0:T(8,128)} %param.10) | copy-start | bytes 36868
  170.5 19.6 %collective-permute-start.5 = (f32[3,32,17]{2,1,0:T(8,128)S(1)}, f32[3,32,17]{2,1,0:T(8,128)S(1)}, u32[]{:S(2)}, u32[]{:S(2)}) collective-permute-start(f32[3,32,17]{2,1,0:T(8,128)S(1)} %get-tuple-element.17), channel_id=1, source_target_pairs={{4,0},{8,4},{12,8},{16,12},{20,16},{24,20},{28,24},{32,28},{36,32}... | collective-permute-start | bytes 19592 | tf_op jit(solution)/shard_map/ppermute | solution.py:31
  177.8 12.3 %collective-permute-start.4 = (f32[3,32,17]{2,1,0:T(8,128)S(1)}, f32[3,32,17]{2,1,0:T(8,128)S(1)}, u32[]{:S(2)}, u32[]{:S(2)}) collective-permute-start(f32[3,32,17]{2,1,0:T(8,128)S(1)} %get-tuple-element.18), channel_id=1, source_target_pairs={{0,4},{4,8},{8,12},{12,16},{16,20},{20,24},{24,28},{28,32},{32,36}... | collective-permute-start | bytes 19592 | tf_op jit(solution)/shard_map/ppermute | solution.py:29
  179.7 10.5 %collective-permute-start.7 = (f32[3,32,17]{2,1,0:T(8,128)S(1)}, f32[3,32,17]{2,1,0:T(8,128)S(1)}, u32[]{:S(2)}, u32[]{:S(2)}) collective-permute-start(f32[3,32,17]{2,1,0:T(8,128)S(1)} %get-tuple-element.16), channel_id=1, source_target_pairs={{4,0},{8,4},{12,8},{16,12},{20,16},{24,20},{28,24},{32,28},{36,32}... | collective-permute-start | bytes 19592 | tf_op jit(solution)/shard_map/ppermute | solution.py:31
  188.2 10.5 %collective-permute-start.6 = (f32[3,32,17]{2,1,0:T(8,128)S(1)}, f32[3,32,17]{2,1,0:T(8,128)S(1)}, u32[]{:S(2)}, u32[]{:S(2)}) collective-permute-start(f32[3,32,17]{2,1,0:T(8,128)S(1)} %get-tuple-element.15), channel_id=1, source_target_pairs={{0,4},{4,8},{8,12},{12,16},{16,20},{20,24},{24,28},{28,32},{32,36}... | collective-permute-start | bytes 19592 | tf_op jit(solution)/shard_map/ppermute | solution.py:29
where the time goes:
time: 231 us; the launch traced here: 229 us
  local copies, waits for them, and re-layouts  69.1 us (30%)
  starting transfers between devices  58.4 us (25%)
  other arithmetic  41.7 us (18%)
  waiting for transfers between devices  36.2 us (16%)
  matrix products  17.5 us (8%)
  blocking collectives  5.33 us (2%)
    all_to_all x1, waiting for transfers between devices, on_device(): lax.all_to_all(sent_block, 'comp', split_axis=1, concat_axis=0, tiled=True)  27.1 us
    unnamed x15, local copies, waits for them, and re-layouts  18.7 us
    ppermute x4, starting transfers between devices, extended_2(): lax.ppermute(head, axis, [((i + 1) % count, i) for i in range(ends)])  18.3 us
    gather x2, local copies, waits for them, and re-layouts, on_device(): jnp.take(band_stress, source_points.reshape(-1), axis=1)  17.3 us
    dot_general x4, matrix products, sources(): jnp.dot(quad_matrix, current.astype(jnp.bfloat16), preferred_element_type...  14.3 us
    mul x3, other arithmetic, upwind(): return (middle - flux_rows - flux_cols) * wet_rows  12.7 us
    ppermute x4, starting transfers between devices, extended_2(): lax.ppermute(tail, axis, [(i, (i + 1) % count) for i in range(ends)])  10.9 us
    all_to_all x1, starting transfers between devices, on_device(): lax.all_to_all(sent_block, 'comp', split_axis=1, concat_axis=0, tiled=True)  10.7 us
  transfers between devices with their start and end apart: 11, of which 3 were waited for; matrix products, arithmetic and copies ran while one was open for 18% of the time, Pallas kernels for 0%

commit v1 on v0

v1 whole, which is shorter than its diff:
```python
import functools
import math

import jax
import jax.numpy as jnp
from jax import lax
from jax.experimental import pallas as pl
from jax.experimental.pallas import tpu as pltpu
from jax.sharding import PartitionSpec as P

NF = 36
ND = 32
K = NF * ND
SUBSTEPS = 4
SRC_STEPS = 4
SW_STEPS = 8

step_source = 0.1
wave_speed = 0.35
friction = 0.05
forcing_gain = 0.15

LOCAL = 36
ROWS = 96
OWNERS = 32
GROUP = 16
RUN = 6
HALO = 4
KB = 4
MARGIN = 2 * SW_STEPS
TILES = 10


def component_tables(offset, local_count):
    indices = offset + jnp.arange(local_count, dtype=jnp.int32)
    frequency = (indices // ND).astype(jnp.float32)
    heading = (indices % ND).astype(jnp.float32)
    heading_angle = 2.0 * math.pi * (heading + 0.5) / ND
    fraction = (frequency + 0.5) / NF
    group_speed = 0.25 + 0.4 * fraction
    wave_ratio = 0.5 + 0.5 * fraction
    cosine = jnp.cos(heading_angle)
    sine_part = jnp.sin(heading_angle)
    speed_east = group_speed * cosine
    speed_north = group_speed * sine_part
    stress_coef = jnp.stack(
        [
            wave_ratio * (1.0 + cosine * cosine) - 0.5,
            wave_ratio * sine_part * cosine,
            wave_ratio * (1.0 + sine_part * sine_part) - 0.5,
        ]
    )
    return speed_east, speed_north, stress_coef


def propagate_kernel(
    speeds, spec_ref, top_ref, bot_ref, wet_ref, wtop_ref, wbot_ref,
    prop_ref, sent_ref, field, wet, half0, half1,
):
    ext = ROWS + 2 * HALO
    step = pl.program_id(0)

    @pl.when(step == 0)
    def _():
        wet[0:ROWS, :] = wet_ref[...].astype(jnp.float32)
        wet[ROWS:ROWS + HALO, :] = wbot_ref[0]
        wet[ROWS + HALO:ext, :] = wtop_ref[0]

    lane = lax.broadcasted_iota(jnp.int32, (ext, 128), 1)

    def advance(k, east, north):
        a = jnp.abs(speeds[0, step * KB + k])
        b = jnp.abs(speeds[1, step * KB + k])
        c = 1.0 - a - b
        left, right = field[:, :128], field[:, 128:]
        wl, wr = wet[:, :128], wet[:, 128:]
        for _ in range(SUBSTEPS):
            row_shift = 1 if east else ext - 1
            ul = pltpu.roll(left, row_shift, 0)
            ur = pltpu.roll(right, row_shift, 0)
            if north:
                rl = pltpu.roll(left, 1, 1)
                rr = pltpu.roll(right, 1, 1)
                sl = jnp.where(lane == 0, 0.0, rl)
                sr = jnp.where(lane == 0, rl, rr)
            else:
                rl = pltpu.roll(left, 127, 1)
                rr = pltpu.roll(right, 127, 1)
                sl = jnp.where(lane == 127, rr, rl)
                sr = jnp.where(lane == 127, 0.0, rr)
            left = wl * (c * left + a * ul + b * sl)
            right = wr * (c * right + a * ur + b * sr)
        left, right = left[:ROWS], right[:ROWS]
        prop_ref[k, :, :128] = left
        prop_ref[k, :, 128:] = right
        half0[pl.ds(k * ROWS, ROWS), :] = left
        half1[pl.ds(k * ROWS, ROWS), :] = right

    def one(k, carry):
        field[0:ROWS, :] = spec_ref[k]
        field[ROWS:ROWS + HALO, :] = bot_ref[k]
        field[ROWS + HALO:ext, :] = top_ref[k]
        ax = speeds[0, step * KB + k]
        ay = speeds[1, step * KB + k]
        for east in (True, False):
            for north in (True, False):
                hit_x = ax >= 0.0 if east else ax < 0.0
                hit_y = ay >= 0.0 if north else ay < 0.0
                pl.when(hit_x & hit_y)(functools.partial(advance, k, east, north))
        return carry

    lax.fori_loop(0, KB, one, 0)
    for h, half in enumerate((half0, half1)):
        for g in range(GROUP):
            picked = half[pl.ds(g, KB * RUN, stride=GROUP), :]
            sent_ref[h * GROUP + g] = picked.astype(jnp.bfloat16)


def propagate(speeds, spectrum, top, bottom, wet_mask):
    cols = spectrum.shape[2]
    smem = pl.BlockSpec(memory_space=pltpu.SMEM)
    edge = pl.BlockSpec((KB, HALO, cols), lambda i: (i, 0, 0))
    wet_edge = pl.BlockSpec((1, HALO, cols), lambda i: (LOCAL, 0, 0))
    body = pl.BlockSpec((KB, ROWS, cols), lambda i: (i, 0, 0))
    return pl.pallas_call(
        propagate_kernel,
        grid=(LOCAL // KB,),
        in_specs=[
            smem, body, edge, edge,
            pl.BlockSpec((ROWS, cols), lambda i: (0, 0)),
            wet_edge, wet_edge,
        ],
        out_specs=[body, pl.BlockSpec((OWNERS, KB * RUN, 128), lambda i: (0, i, 0))],
        out_shape=[
            jax.ShapeDtypeStruct((LOCAL, ROWS, cols), jnp.float32),
            jax.ShapeDtypeStruct((OWNERS, LOCAL * RUN, 128), jnp.bfloat16),
        ],
        scratch_shapes=[
            pltpu.VMEM((ROWS + 2 * HALO, cols), jnp.float32),
            pltpu.VMEM((ROWS + 2 * HALO, cols), jnp.float32),
            pltpu.VMEM((KB * ROWS, 128), jnp.float32),
            pltpu.VMEM((KB * ROWS, 128), jnp.float32),
        ],
        name="propagate",
    )(speeds, spectrum, top, bottom, wet_mask, top, bottom)


MB = 384
NB = 256


def source_kernel(recv_ref, quad_ref, diss_ref, coef_ref, out_ref, stress_ref, flat, cur, xb, level):
    total = recv_ref.shape[0]
    chunk = 1152

    def widen(i, carry):
        flat[pl.ds(i * chunk, chunk), :] = recv_ref[pl.ds(i * chunk, chunk), :].astype(jnp.float32)
        return carry

    lax.fori_loop(0, total // chunk, widen, 0)
    for j in range(RUN):
        base = flat[pl.ds(j, K, stride=RUN), :]
        cols = slice(j * 128, (j + 1) * 128)
        cur[:, cols] = base
        xb[0, :, cols] = base.astype(jnp.bfloat16)
        level[0, :, cols] = jnp.sum(base, axis=0, keepdims=True)

    def step(s, carry):
        old = s % 2
        new = 1 - old
        for n in range(RUN * 128 // NB):
            cols = slice(n * NB, (n + 1) * NB)
            mean = level[old, :, cols] * (1.0 / K)
            sums = jnp.zeros((1, NB), jnp.float32)
            for m in range(K // MB):
                rows = slice(m * MB, (m + 1) * MB)
                product = jnp.dot(
                    quad_ref[rows, :], xb[old, :, cols], preferred_element_type=jnp.float32
                )
                rate = jnp.concatenate([diss_ref[rows, :]] * (NB // 128), axis=1)
                now = cur[rows, cols]
                now = now + step_source * now * (product - rate * mean)
                cur[rows, cols] = now
                xb[new, rows, cols] = now.astype(jnp.bfloat16)
                sums = sums + jnp.sum(now, axis=0, keepdims=True)
            level[new, :, cols] = sums
        return carry

    lax.fori_loop(0, SRC_STEPS, step, 0)
    for j in range(RUN):
        base = flat[pl.ds(j, K, stride=RUN), :]
        cols = slice(j * 128, (j + 1) * 128)
        gain = (cur[:, cols] - base).astype(jnp.bfloat16).astype(jnp.float32)
        flat[pl.ds(j, K, stride=RUN), :] = gain
        coupled = base + gain
        for c in range(3):
            row = jnp.sum(coef_ref[c] * coupled, axis=0, keepdims=True) * (1.0 / K)
            stress_ref[c * 8 + j:c * 8 + j + 1, :] = row
    for c in range(3):
        stress_ref[c * 8 + RUN:c * 8 + 8, :] = jnp.zeros((8 - RUN, 128), jnp.float32)

    def narrow(i, carry):
        out_ref[pl.ds(i * chunk, chunk), :] = flat[pl.ds(i * chunk, chunk), :].astype(jnp.bfloat16)
        return carry

    lax.fori_loop(0, total // chunk, narrow, 0)


def sources(received, quad_matrix, rate_wide, coef_wide):
    points = RUN * 128
    return pl.pallas_call(
        source_kernel,
        out_shape=[
            jax.ShapeDtypeStruct(received.shape, jnp.bfloat16),
            jax.ShapeDtypeStruct((24, 128), jnp.float32),
        ],
        scratch_shapes=[
            pltpu.VMEM((K * RUN, 128), jnp.float32),
            pltpu.VMEM((K, points), jnp.float32),
            pltpu.VMEM((2, K, points), jnp.bfloat16),
            pltpu.VMEM((2, 1, points), jnp.float32),
        ],
        name="sources",
    )(received, quad_matrix, rate_wide, coef_wide)


def pick_kernel(table_ref, points_ref, out_ref):
    pieces = []
    for c in range(3):
        rows = table_ref[:, c * 8:(c + 1) * 8, :].reshape(OWNERS * 8, 128)
        turned = rows.T
        high = turned.astype(jnp.bfloat16)
        pieces.append(high)
        pieces.append((turned - high.astype(jnp.float32)).astype(jnp.bfloat16))
    table = jnp.concatenate(pieces, axis=0)
    slot = lax.broadcasted_iota(jnp.int32, (OWNERS * 8, 128), 0)
    within = lax.broadcasted_iota(jnp.int32, (128, 128), 0)
    weights = (0.5, 0.3, 0.2)
    for t in range(TILES):
        hots, lows = [], []
        for m in range(3):
            p = points_ref[m * TILES + t:m * TILES + t + 1, :]
            row = p >> 8
            col = p & 255
            hi = (((col >> 7) * GROUP + (row & (GROUP - 1))) << 3) + (row >> 4)
            hots.append(jnp.where(slot == hi, 1.0, 0.0).astype(jnp.bfloat16))
            lows.append(col & 127)
        hot = jnp.concatenate(hots, axis=1)
        found = jnp.dot(table, hot, preferred_element_type=jnp.float32)
        for c in range(3):
            both = found[2 * c * 128:(2 * c + 1) * 128] + found[(2 * c + 1) * 128:(2 * c + 2) * 128]
            acc = jnp.zeros((128, 128), jnp.float32)
            for m in range(3):
                acc = acc + jnp.where(
                    within == lows[m], both[:, m * 128:(m + 1) * 128] * weights[m], 0.0
                )
            out_ref[c, t:t + 1, :] = jnp.sum(acc, axis=0, keepdims=True)


def pick(table, points):
    return pl.pallas_call(
        pick_kernel,
        out_shape=jax.ShapeDtypeStruct((3, TILES, 128), jnp.float32),
        name="pick",
    )(table, points)


def finish_kernel(back_ref, prop_ref, out_ref, half0, half1):
    for h, half in enumerate((half0, half1)):
        for g in range(GROUP):
            half[pl.ds(g, KB * RUN, stride=GROUP), :] = back_ref[h * GROUP + g].astype(jnp.float32)
    for k in range(KB):
        rows = slice(k * ROWS, (k + 1) * ROWS)
        out_ref[k, :, :128] = prop_ref[k, :, :128] + half0[rows, :]
        out_ref[k, :, 128:] = prop_ref[k, :, 128:] + half1[rows, :]


def finish(back, propagated):
    cols = propagated.shape[2]
    body = pl.BlockSpec((KB, ROWS, cols), lambda i: (i, 0, 0))
    return pl.pallas_call(
        finish_kernel,
        grid=(LOCAL // KB,),
        in_specs=[pl.BlockSpec((OWNERS, KB * RUN, 128), lambda i: (0, i, 0)), body],
        out_specs=body,
        out_shape=jax.ShapeDtypeStruct(propagated.shape, jnp.float32),
        scratch_shapes=[
            pltpu.VMEM((KB * ROWS, 128), jnp.float32),
            pltpu.VMEM((KB * ROWS, 128), jnp.float32),
        ],
        name="finish",
    )(back, propagated)


def from_neighbours(low, high, axis):
    count = lax.axis_size(axis)
    ends = count - 1
    before = lax.ppermute(high, axis, [(i, (i + 1) % count) for i in range(ends)])
    after = lax.ppermute(low, axis, [((i + 1) % count, i) for i in range(ends)])
    return before, after


def diff_rows(extended):
    return 0.5 * (extended[2:, 1:-1] - extended[:-2, 1:-1])


def diff_cols(extended):
    return 0.5 * (extended[1:-1, 2:] - extended[1:-1, :-2])


def shallow_water(wide_state, wide_stress, tile_cols, tile_rows):
    groups = lax.axis_size("comp")
    wide_cols = wide_state.shape[2]
    global_col = (
        lax.axis_index("comp") * tile_cols - MARGIN + jnp.arange(wide_cols, dtype=jnp.int32)
    )
    within = (global_col >= 0) & (global_col < tile_cols * groups)
    inside = within.astype(jnp.float32)[None, :]
    rimmed = jnp.pad(jnp.where(within, wide_stress, 0.0), ((0, 0), (1, 1), (1, 1)))
    force_down = -(diff_rows(rimmed[0]) + diff_cols(rimmed[1]))
    force_across = -(diff_rows(rimmed[1]) + diff_cols(rimmed[2]))
    height, flow_down, flow_across = wide_state
    for _ in range(SW_STEPS):
        down_ext = jnp.pad(flow_down, 1)
        across_ext = jnp.pad(flow_across, 1)
        height = (height - wave_speed * (diff_rows(down_ext) + diff_cols(across_ext))) * inside
        height_ext = jnp.pad(height, 1)
        flow_down = (
            (1.0 - friction) * flow_down
            - wave_speed * diff_rows(height_ext)
            + forcing_gain * force_down
        ) * inside
        flow_across = (
            (1.0 - friction) * flow_across
            - wave_speed * diff_cols(height_ext)
            + forcing_gain * force_across
        ) * inside
    stacked = jnp.stack([height, flow_down, flow_across])
    row_start = lax.axis_index("band") * tile_rows
    own_rows = lax.dynamic_slice_in_dim(stacked, row_start, tile_rows, 1)
    return own_rows[:, :, MARGIN:MARGIN + tile_cols]


def on_device(spectrum, wet_mask, quad_matrix, dissipation, circulation, source_points):
    offset = lax.axis_index("comp") * LOCAL
    speed_east, speed_north, _ = component_tables(offset, LOCAL)
    speeds = jnp.stack([speed_east, speed_north])
    wetness = wet_mask.astype(jnp.float32)[None]
    low = jnp.concatenate([spectrum[:, :HALO], wetness[:, :HALO]], axis=0)
    high = jnp.concatenate([spectrum[:, -HALO:], wetness[:, -HALO:]], axis=0)
    top, bottom = from_neighbours(low, high, "band")
    propagated, sent = propagate(speeds, spectrum, top, bottom, wet_mask)
    received = lax.all_to_all(sent, "comp", 0, 0, tiled=True)

    tile_rows = circulation.shape[1]
    tile_cols = circulation.shape[2]
    both = jnp.concatenate([circulation, source_points.astype(jnp.float32)], axis=0)
    before, after = from_neighbours(both[:, :, :MARGIN], both[:, :, -MARGIN:], "comp")
    wide = jnp.concatenate([before, both, after], axis=2)
    left_points = before[3:].astype(jnp.int32).reshape(3, 1, 128)
    right_points = after[3:].astype(jnp.int32).reshape(3, 1, 128)
    points = jnp.concatenate([source_points, left_points, right_points], axis=1)
    points = points.reshape(3 * TILES, 128)

    full_coef = component_tables(0, K)[2]
    coef_wide = jnp.broadcast_to(full_coef[:, :, None], (3, K, 128))
    rate_wide = jnp.broadcast_to(dissipation[:, None], (K, 128))
    increments, stress = sources(received.reshape(K * RUN, 128), quad_matrix, rate_wide, coef_wide)
    table = lax.all_to_all(
        jnp.broadcast_to(stress[None], (OWNERS, 24, 128)), "comp", 0, 0, tiled=True
    )
    returned = lax.all_to_all(
        increments.reshape(OWNERS, LOCAL * RUN, 128), "comp", 0, 0, tiled=True
    )
    cells = pick(table, points)
    own = cells[:, :tile_rows]
    left = cells[:, tile_rows].reshape(3, tile_rows, MARGIN)
    right = cells[:, tile_rows + 1].reshape(3, tile_rows, MARGIN)
    wide_cells = jnp.concatenate([left, own, right], axis=2)
    everything = lax.all_gather(
        jnp.concatenate([wide[:3], wide_cells], axis=0), "band", axis=1, tiled=True
    )
    circulation_out = shallow_water(everything[:3], everything[3:], tile_cols, tile_rows)
    spectrum_out = finish(returned, propagated)
    return spectrum_out, circulation_out


def solution(mesh):
    in_specs = (
        P("comp", "band", None),
        P("band", None),
        P(),
        P(),
        P(None, "band", "comp"),
        P(None, "band", "comp"),
    )
    out_specs = (P("comp", "band", None), P(None, "band", "comp"))
    return jax.shard_map(
        on_device, mesh=mesh, in_specs=in_specs, out_specs=out_specs, check_vma=False
    )
```

time: 231 us -> 147 us (0.64)
  local copies, waits for them, and re-layouts: 69.1 us -> 9.89 us
  Pallas kernels: 0 us -> 50.2 us
  other arithmetic: 41.7 us -> 4.33 us
  starting transfers between devices: 58.4 us -> 40.1 us
  matrix products: 17.5 us -> 0 us
  waiting for transfers between devices: 36.2 us -> 27.2 us
  blocking collectives: 5.33 us -> 12.4 us
    pallas_call x0 -> x4, Pallas kernels: none -> 50.2 us  [the longest x1 21.9 us: sources(): pl.pallas_call(source_kernel, out_shape=[jax.ShapeDtypeStruct(received.sh...]
    dot_general x5 -> x0, matrix products: 17.5 us -> none  [the longest x4 14.3 us: sources(): jnp.dot(quad_matrix, current.astype(jnp.bfloat16), preferred_element_type...]
    gather x2 -> x0, local copies, waits for them, and re-layouts: 17.3 us -> none  [on_device(): jnp.take(band_stress, source_points.reshape(-1), axis=1)]
    unnamed x15 -> x16, local copies, waits for them, and re-layouts: 18.7 us -> 1.92 us
    ppermute x8 -> x4, starting transfers between devices: 29.2 us -> 13.4 us  [the longest x2 8.27 us: from_neighbours(): after = lax.ppermute(low, axis, [((i + 1) % count, i) for i in range(ends)])]
    mul x18 -> x16, other arithmetic: 14.1 us -> 1.45 us  [the longest x8 0.7 us: shallow_water(): (height - wave_speed * (diff_rows(down_ext) + diff_cols(across_ext))) * i...]
    convert_element_type x3, other arithmetic: 11.3 us -> 0.01 us  [the longest x1 0.01 us: on_device(): left_points = before[3:].astype(jnp.int32).reshape(3, 1, 128)]
    squeeze x4 -> x1, local copies, waits for them, and re-layouts: 7.57 us -> 0.1 us  [shallow_water(): force_across = -(diff_rows(rimmed[1]) + diff_cols(rimmed[2]))]
  transfers between devices with their start and end apart: 11 -> 7, of which waited for: 3 -> 4; matrix products, arithmetic and copies ran while one was open for 18% -> 7% of each run, Pallas kernels for 0% -> 18%
where the time goes in v1:
time: 147 us; the launch traced here: 145 us
  Pallas kernels  50.2 us (34%)
  starting transfers between devices  40.1 us (27%)
  waiting for transfers between devices  27.2 us (19%)
  blocking collectives  12.4 us (8%)
  local copies, waits for them, and re-layouts  9.89 us (7%)
  other arithmetic  4.33 us (3%)
    pallas_call x1, Pallas kernels, sources(): pl.pallas_call(source_kernel, out_shape=[jax.ShapeDtypeStruct(received.sh...  21.9 us
    pallas_call x1, Pallas kernels, propagate(): pl.pallas_call(propagate_kernel, grid=(LOCAL // KB,), in_specs=[smem, bod...  16.3 us
    all_gather x1, blocking collectives, on_device(): lax.all_gather(jnp.concatenate([wide[:3], wide_cells], axis=0), 'band', a...  12.4 us
    all_to_all x1, waiting for transfers between devices, on_device(): received = lax.all_to_all(sent, 'comp', 0, 0, tiled=True)  11 us
    all_to_all x1, starting transfers between devices, on_device(): received = lax.all_to_all(sent, 'comp', 0, 0, tiled=True)  11 us
    all_to_all x1, waiting for transfers between devices, on_device(): lax.all_to_all(jnp.broadcast_to(stress[None], (OWNERS, 24, 128)), 'comp',...  9.94 us
    all_to_all x1, starting transfers between devices, on_device(): lax.all_to_all(jnp.broadcast_to(stress[None], (OWNERS, 24, 128)), 'comp',...  9.83 us
    ppermute x2, starting transfers between devices, from_neighbours(): after = lax.ppermute(low, axis, [((i + 1) % count, i) for i in range(ends)])  8.27 us
  transfers between devices with their start and end apart: 7, of which 4 were waited for; matrix products, arithmetic and copies ran while one was open for 7% of the time, Pallas kernels for 18%

profile of v1, /device:TPU:6, one launch (start us, length us, event | category | flops | bytes accessed | tf_op | source)
XLA Modules:
  0.0 144.9 jit_solution(3380421597797280132)
XLA Ops:
  0.6 1.1 fusion.161
  1.7 0.9 convert_bitcast_fusion
  2.7 1.7 %collective-permute-start = (f32[37,4,256]{2,1,0:T(4,128)S(1)}, f32[37,4,256]{2,1,0:T(4,128)S(1)}, u32[]{:S(2)}, u32[]{:S(2)}) collective-permute-start(f32[37,4,256]{2,1,0:T(4,128)S(1)} %pad_maximum_fusion), channel_id=1, source_target_pairs={{0,1},{1,2},{2,3},{4,5},{5,6},{6,7},{8,9},{9,10},{10,11},{12,13},{... | collective-permute-start | bytes 454664 | tf_op jit(solution)/shard_map/ppermute | solution.py:298
  4.5 1.3 collective-permute-start.1
  5.8 0.1 sine_multiply_fusion
  5.9 0.6 pad_maximum_fusion.4.speeds
  6.4 0.0 collective-permute-done.top_ref.wtop_ref
  6.4 3.0 %collective-permute-done.1.bot_ref.wbot_ref = f32[37,4,256]{2,1,0:T(4,128)S(1)} collective-permute-done((f32[37,4,256]{2,1,0:T(4,128)S(1)}, f32[37,4,256]{2,1,0:T(4,128)S(1)}, u32[]{:S(2)}, u32[]{:S(2)}) %collective-permute-start.1) | collective-permute-done | bytes 151584 | tf_op jit(solution)/shard_map/ppermute | solution.py:299
  9.5 0.0 copy-done.3
  9.5 0.6 copy-done.4
  10.1 16.3 %propagate.1 = (f32[36,96,256]{2,1,0:T(8,128)}, bf16[32,216,128]{2,1,0:T(8,128)(2,1)}) custom-call(f32[2,36]{1,0:T(2,128)} %pad_maximum_fusion.4.speeds, f32[36,96,256]{2,1,0:T(8,128)} %spec_ref.1, f32[37,4,256]{2,1,0:T(4,128)} %copy-done.3, f32[37,4,256]{2,1,0:T(4,128)} %copy-done.4, s32[96,256]{1,0:T(8,128)} %wet_ref.1, f32[37,4,256]{2,1,0:T(4,128)} %copy-done.3, ...), custom_call_target="tpu_custom_call" | custom-call | tf_op jit(solution)/shard_map/propagate/pallas_call | solution.py:125
  26.4 0.0 copy-start.7
  26.4 11.0 %all-to-all-start = ((bf16[32,216,128]{2,1,0:T(8,128)(2,1)}), bf16[32,216,128]{2,1,0:T(8,128)(2,1)S(1)}, u32[]{:S(2)}, u32[]{:S(2)}) async-start(bf16[32,216,128]{2,1,0:T(8,128)(2,1)} %get-tuple-element.6), calls=%async_computation | async-start | bytes 3538944 | tf_op jit(solution)/shard_map/all_to_all | solution.py:353
  37.4 0.0 copy-done.6
  37.4 0.0 copy-done.5
  37.4 0.1 slice_maximum_fusion
  37.5 3.4 %collective-permute-start.2 = (f32[6,8,16]{2,1,0:T(8,128)S(1)}, f32[6,8,16]{2,1,0:T(8,128)S(1)}, u32[]{:S(2)}, u32[]{:S(2)}) collective-permute-start(f32[6,8,16]{2,1,0:T(8,128)S(1)} %get-tuple-element.41), channel_id=1, source_target_pairs={{0,4},{4,8},{8,12},{12,16},{16,20},{20,24},{24,28},{28,32},{32,36}... | collective-permute-start | bytes 9224 | tf_op jit(solution)/shard_map/ppermute | solution.py:298
  40.9 7.0 %collective-permute-start.3 = (f32[6,8,16]{2,1,0:T(8,128)S(1)}, f32[6,8,16]{2,1,0:T(8,128)S(1)}, u32[]{:S(2)}, u32[]{:S(2)}) collective-permute-start(f32[6,8,16]{2,1,0:T(8,128)S(1)} %get-tuple-element.42), channel_id=1, source_target_pairs={{4,0},{8,4},{12,8},{16,12},{20,16},{24,20},{28,24},{32,28},{36,32}... | collective-permute-start | bytes 9224 | tf_op jit(solution)/shard_map/ppermute | solution.py:299
  47.9 0.2 multiply_add_fusion.1
  48.0 0.2 multiply_add_fusion
  48.2 11.0 %all-to-all-done = bf16[32,216,128]{2,1,0:T(8,128)(2,1)S(1)} async-done(((bf16[32,216,128]{2,1,0:T(8,128)(2,1)}), bf16[32,216,128]{2,1,0:T(8,128)(2,1)S(1)}, u32[]{:S(2)}, u32[]{:S(2)}) %all-to-all-start) | async-done | bytes 1769504 | tf_op jit(solution)/shard_map/all_to_all | solution.py:353
  59.3 1.8 %broadcast_in_dim.32.coef_ref = f32[3,1152,128]{2,1,0:T(8,128)} broadcast(f32[3,1152]{1,0:T(4,128)S(1)} %pad_maximum_fusion.3), dimensions={0,1} | broadcast | bytes 1783296 | tf_op jit(solution)/shard_map/broadcast_in_dim | solution.py:366
  61.1 0.0 copy-done.7
  61.1 1.0 broadcast_in_dim.15.diss_ref
  62.1 0.0 copy-done
  62.1 21.9 %sources.1 = (bf16[6912,128]{1,0:T(8,128)(2,1)}, f32[24,128]{1,0:T(8,128)}) custom-call(bf16[6912,128]{1,0:T(8,128)(2,1)} %bitcast.27, bf16[1152,1152]{1,0:T(8,128)(2,1)} %quad_ref.1, f32[1152,128]{1,0:T(8,128)} %broadcast_in_dim.15.diss_ref, f32[3,1152,128]{2,1,0:T(8,128)} %broadcast_in_dim.32.coef_ref), custom_call_target="tpu_custom_call" | custom-call | tf_op jit(solution)/shard_map/sources/pallas_call | solution.py:211
  84.1 1.5 %broadcast_in_dim.33 = f32[32,24,128]{2,1,0:T(8,128)} broadcast(f32[24,128]{1,0:T(8,128)} %get-tuple-element.9), dimensions={1,2} | broadcast | bytes 405504 | tf_op jit(solution)/shard_map/broadcast_in_dim | solution.py:370
  85.5 9.8 %all-to-all-start.2 = ((f32[32,24,128]{2,1,0:T(8,128)}), f32[32,24,128]{2,1,0:T(8,128)S(1)}, u32[]{:S(2)}, u32[]{:S(2)}) async-start(f32[32,24,128]{2,1,0:T(8,128)} %broadcast_in_dim.33), calls=%async_computation.2 | async-start | bytes 786432 | tf_op jit(solution)/shard_map/all_to_all | solution.py:369
  95.4 0.0 collective-permute-done.2
  95.4 0.1 reshape.248
  95.5 0.0 collective-permute-done.3
  95.5 0.1 reshape.249
  95.6 0.6 reshape.247.points_ref
  96.2 9.9 %all-to-all-done.2.table_ref = f32[32,24,128]{2,1,0:T(8,128)S(1)} async-done(((f32[32,24,128]{2,1,0:T(8,128)}), f32[32,24,128]{2,1,0:T(8,128)S(1)}, u32[]{:S(2)}, u32[]{:S(2)}) %all-to-all-start.2) | async-done | bytes 393248 | tf_op jit(solution)/shard_map/all_to_all | solution.py:369
  106.1 5.9 %all-to-all-start.1 = ((bf16[32,216,128]{2,1,0:T(8,128)(2,1)}), bf16[32,216,128]{2,1,0:T(8,128)(2,1)S(1)}, u32[]{:S(2)}, u32[]{:S(2)}) async-start(bf16[32,216,128]{2,1,0:T(8,128)(2,1)} %bitcast.28), calls=%async_computation.1 | async-start | bytes 3538944 | tf_op jit(solution)/shard_map/all_to_all | solution.py:372
  112.1 0.0 copy-done.2
  112.1 4.0 %pick.1 = f32[3,10,128]{2,1,0:T(8,128)} custom-call(f32[32,24,128]{2,1,0:T(8,128)} %copy-done.2, s32[30,128]{1,0:T(8,128)} %reshape.247.points_ref), custom_call_target="tpu_custom_call" | custom-call | tf_op jit(solution)/shard_map/pick/pallas_call | solution.py:261
  116.0 0.8 slice_reduce_fusion.1
  116.8 0.7 slice.368
  117.6 0.1 reshape_squeeze.6
  117.6 0.1 reshape_squeeze.7
  117.7 0.1 fusion
  117.8 12.4 %all_gather.3 = f32[6,32,160]{2,1,0:T(8,128)S(1)} all-gather(f32[6,8,160]{2,1,0:T(8,128)S(1)} %fusion), channel_id=1, replica_groups=mesh['comp'=32,'band'=4] {'band'}, dimensions={1}, use_global_device_ids=true | all-gather | bytes 153600 | tf_op jit(solution)/shard_map/all_gather | solution.py:380
  130.2 0.1 fusion.5
  130.3 0.1 fusion.10
  130.4 0.1 fusion.63
  130.6 0.1 fusion.16
  130.7 0.1 fusion.73
  130.7 0.1 fusion.22
  130.8 0.1 fusion.83
  130.9 0.1 fusion.28
  131.0 0.1 fusion.93
  131.1 0.1 fusion.34
  131.2 0.1 fusion.103
  131.3 0.1 fusion.40
  131.4 0.1 fusion.113
  131.5 0.1 fusion.46
  131.6 0.1 fusion.123
  131.7 0.1 fusion.52
  131.8 0.1 fusion.135
  131.9 0.7 fusion.145
  132.6 3.1 %all-to-all-done.1.back_ref = bf16[32,216,128]{2,1,0:T(8,128)(2,1)S(1)} async-done(((bf16[32,216,128]{2,1,0:T(8,128)(2,1)}), bf16[32,216,128]{2,1,0:T(8,128)(2,1)S(1)}, u32[]{:S(2)}, u32[]{:S(2)}) %all-to-all-start.1) | async-done | bytes 1769504 | tf_op jit(solution)/shard_map/all_to_all | solution.py:372
  135.7 1.2 copy-done.1
  137.0 8.0 %finish.1 = f32[36,96,256]{2,1,0:T(8,128)} custom-call(bf16[32,216,128]{2,1,0:T(8,128)(2,1)} %copy-done.1, f32[36,96,256]{2,1,0:T(8,128)} %get-tuple-element.8.prop_ref), custom_call_target="tpu_custom_call" | custom-call | tf_op jit(solution)/shard_map/finish/pallas_call | solution.py:281
  (18 shorter events, 0.2 us)
Async XLA Ops:
  2.7 3.7 %collective-permute-start = (f32[37,4,256]{2,1,0:T(4,128)S(1)}, f32[37,4,256]{2,1,0:T(4,128)S(1)}, u32[]{:S(2)}, u32[]{:S(2)}) collective-permute-start(f32[37,4,256]{2,1,0:T(4,128)S(1)} %pad_maximum_fusion), channel_id=1, source_target_pairs={{0,1},{1,2},{2,3},{4,5},{5,6},{6,7},{8,9},{9,10},{10,11},{12,13},{... | collective-permute-start | bytes 454664 | tf_op jit(solution)/shard_map/ppermute | solution.py:298
  4.5 5.0 %collective-permute-start.1 = (f32[37,4,256]{2,1,0:T(4,128)S(1)}, f32[37,4,256]{2,1,0:T(4,128)S(1)}, u32[]{:S(2)}, u32[]{:S(2)}) collective-permute-start(f32[37,4,256]{2,1,0:T(4,128)S(1)} %pad_maximum_fusion.1), channel_id=1, source_target_pairs={{1,0},{2,1},{3,2},{5,4},{6,5},{7,6},{9,8},{10,9},{11,10},{13,12},{... | collective-permute-start | bytes 454664 | tf_op jit(solution)/shard_map/ppermute | solution.py:299
  6.4 3.0 %copy-start.3 = (f32[37,4,256]{2,1,0:T(4,128)}, f32[37,4,256]{2,1,0:T(4,128)S(1)}, u32[]{:S(2)}) copy-start(f32[37,4,256]{2,1,0:T(4,128)S(1)} %collective-permute-done.top_ref.wtop_ref) | copy-start | bytes 454660
  9.5 0.6 copy-start.4
  26.4 11.0 %copy-start.6 = (s32[3,8,128]{2,1,0:T(8,128)S(1)}, s32[3,8,128]{2,1,0:T(8,128)}, u32[]{:S(2)}) copy-start(s32[3,8,128]{2,1,0:T(8,128)} %param.11) | copy-start | bytes 36868
  26.4 11.0 %copy-start.5 = (f32[3,8,128]{2,1,0:T(8,128)S(1)}, f32[3,8,128]{2,1,0:T(8,128)}, u32[]{:S(2)}) copy-start(f32[3,8,128]{2,1,0:T(8,128)} %param.10) | copy-start | bytes 36868
  26.4 34.7 %copy-start.7 = (f32[1152]{0:T(1024)S(1)}, f32[1152]{0:T(1024)}, u32[]{:S(2)}) copy-start(f32[1152]{0:T(1024)} %param.9) | copy-start | bytes 13828
  26.4 32.8 %all-to-all-start = ((bf16[32,216,128]{2,1,0:T(8,128)(2,1)}), bf16[32,216,128]{2,1,0:T(8,128)(2,1)S(1)}, u32[]{:S(2)}, u32[]{:S(2)}) async-start(bf16[32,216,128]{2,1,0:T(8,128)(2,1)} %get-tuple-element.6), calls=%async_computation | async-start | bytes 3538944 | tf_op jit(solution)/shard_map/all_to_all | solution.py:353
  37.5 57.9 %collective-permute-start.2 = (f32[6,8,16]{2,1,0:T(8,128)S(1)}, f32[6,8,16]{2,1,0:T(8,128)S(1)}, u32[]{:S(2)}, u32[]{:S(2)}) collective-permute-start(f32[6,8,16]{2,1,0:T(8,128)S(1)} %get-tuple-element.41), channel_id=1, source_target_pairs={{0,4},{4,8},{8,12},{12,16},{16,20},{20,24},{24,28},{28,32},{32,36}... | collective-permute-start | bytes 9224 | tf_op jit(solution)/shard_map/ppermute | solution.py:298
  40.9 54.6 %collective-permute-start.3 = (f32[6,8,16]{2,1,0:T(8,128)S(1)}, f32[6,8,16]{2,1,0:T(8,128)S(1)}, u32[]{:S(2)}, u32[]{:S(2)}) collective-permute-start(f32[6,8,16]{2,1,0:T(8,128)S(1)} %get-tuple-element.42), channel_id=1, source_target_pairs={{4,0},{8,4},{12,8},{16,12},{20,16},{24,20},{28,24},{32,28},{36,32}... | collective-permute-start | bytes 9224 | tf_op jit(solution)/shard_map/ppermute | solution.py:299
  59.3 2.9 %copy-start = (bf16[32,216,128]{2,1,0:T(8,128)(2,1)}, bf16[32,216,128]{2,1,0:T(8,128)(2,1)S(1)}, u32[]{:S(2)}) copy-start(bf16[32,216,128]{2,1,0:T(8,128)(2,1)S(1)} %all-to-all-done) | copy-start | bytes 5308420
  85.5 20.6 %all-to-all-start.2 = ((f32[32,24,128]{2,1,0:T(8,128)}), f32[32,24,128]{2,1,0:T(8,128)S(1)}, u32[]{:S(2)}, u32[]{:S(2)}) async-start(f32[32,24,128]{2,1,0:T(8,128)} %broadcast_in_dim.33), calls=%async_computation.2 | async-start | bytes 786432 | tf_op jit(solution)/shard_map/all_to_all | solution.py:369
  106.1 5.9 %copy-start.2 = (f32[32,24,128]{2,1,0:T(8,128)}, f32[32,24,128]{2,1,0:T(8,128)S(1)}, u32[]{:S(2)}) copy-start(f32[32,24,128]{2,1,0:T(8,128)S(1)} %all-to-all-done.2.table_ref) | copy-start | bytes 1179652
  106.1 29.6 %all-to-all-start.1 = ((bf16[32,216,128]{2,1,0:T(8,128)(2,1)}), bf16[32,216,128]{2,1,0:T(8,128)(2,1)S(1)}, u32[]{:S(2)}, u32[]{:S(2)}) async-start(bf16[32,216,128]{2,1,0:T(8,128)(2,1)} %bitcast.28), calls=%async_computation.1 | async-start | bytes 3538944 | tf_op jit(solution)/shard_map/all_to_all | solution.py:372
  135.7 1.2 copy-start.1

commit v2 on v1

v2 whole, which is shorter than its diff:
```python
import math

import jax
import jax.numpy as jnp
from jax import lax
from jax.experimental import pallas as pl
from jax.experimental.pallas import tpu as pltpu
from jax.sharding import PartitionSpec as P


NF = 36
ND = 32
K = NF * ND
SUBSTEPS = 4
SRC_STEPS = 4
SW_STEPS = 8

step_source = 0.1
wave_speed = 0.35
friction = 0.05
forcing_gain = 0.15

LOCAL = 36
ROWS = 96
OWNERS = 32
GROUP = 16
RUN = 6
HALO = 4
KB = 4
MARGIN = 2 * SW_STEPS
TILES = 10


def component_tables(offset, local_count):
    indices = offset + jnp.arange(local_count, dtype=jnp.int32)
    frequency = (indices // ND).astype(jnp.float32)
    heading = (indices % ND).astype(jnp.float32)
    heading_angle = 2.0 * math.pi * (heading + 0.5) / ND
    fraction = (frequency + 0.5) / NF
    group_speed = 0.25 + 0.4 * fraction
    wave_ratio = 0.5 + 0.5 * fraction
    cosine = jnp.cos(heading_angle)
    sine_part = jnp.sin(heading_angle)
    speed_east = group_speed * cosine
    speed_north = group_speed * sine_part
    stress_coef = jnp.stack(
        [
            wave_ratio * (1.0 + cosine * cosine) - 0.5,
            wave_ratio * sine_part * cosine,
            wave_ratio * (1.0 + sine_part * sine_part) - 0.5,
        ]
    )
    return speed_east, speed_north, stress_coef


def in_hbm(array):
    return pltpu.with_memory_space_constraint(array, pltpu.HBM)


def in_vmem(array):
    return pltpu.with_memory_space_constraint(array, pltpu.VMEM)


def propagate_kernel(
    speeds, spec_hbm, top_ref, bot_ref, wet_ref, prop0_hbm, prop1_hbm, sent_hbm,
    spec_ref, load_sems, prop0, prop1, sent_ref, wet, left_a, right_a, left_b, right_b, keep_sems, sent_sems,
):
    ext = ROWS + 2 * HALO

    def keep(i):
        part = pl.ds(i * KB * ROWS, KB * ROWS)
        return [
            pltpu.make_async_copy(prop.at[part], hbm.at[part], keep_sems.at[h, i])
            for h, (prop, hbm) in enumerate(((prop0, prop0_hbm), (prop1, prop1_hbm)))
        ]

    def give(o):
        return pltpu.make_async_copy(sent_ref.at[o], sent_hbm.at[o], sent_sems.at[o])

    def load(i):
        part = pl.ds(i * KB, KB)
        return pltpu.make_async_copy(spec_hbm.at[part], spec_ref.at[part], load_sems.at[i])

    def start_load(i, carry):
        load(i).start()
        return carry

    lax.fori_loop(0, LOCAL // KB, start_load, 0)
    wet[0:ROWS, :] = wet_ref[...]
    wet[ROWS:ROWS + HALO, :] = bot_ref[LOCAL]
    wet[ROWS + HALO:ext, :] = top_ref[LOCAL]
    lane = lax.broadcasted_iota(jnp.int32, (ext, 128), 1)

    def advance(k, ahead, a, b, north):
        c = 1.0 - a - b
        edge = 0 if north else 127
        turn = 1 if north else 127
        side = jnp.where(lane == edge, 0.0, b)
        fields = ((left_a, right_a), (left_b, right_b))
        for s in range(SUBSTEPS):
            left_ref, right_ref = fields[s % 2]
            left, right = left_ref[8:8 + ext, :], right_ref[8:8 + ext, :]
            ul = left_ref[pl.ds(8 + ahead, ext), :]
            ur = right_ref[pl.ds(8 + ahead, ext), :]
            rl = pltpu.roll(left, turn, 1)
            rr = pltpu.roll(right, turn, 1)
            if north:
                across_l = side * rl
                across_r = b * jnp.where(lane == 0, rl, rr)
            else:
                across_l = b * jnp.where(lane == 127, rr, rl)
                across_r = side * rr
            left = wet[:, :128] * (c * left + a * ul + across_l)
            right = wet[:, 128:] * (c * right + a * ur + across_r)
            if s + 1 < SUBSTEPS:
                left_ref, right_ref = fields[(s + 1) % 2]
                for ref, value in ((left_ref, left), (right_ref, right)):
                    ref[8:8 + ext, :] = value
                    ref[7:8, :] = value[ext - 1:]
                    ref[8 + ext:9 + ext, :] = value[0:1]
        prop0[pl.ds(k * ROWS, ROWS), :] = left[:ROWS]
        prop1[pl.ds(k * ROWS, ROWS), :] = right[:ROWS]

    def one(k, carry):
        for h, ref in enumerate((left_a, right_a)):
            cols = slice(h * 128, (h + 1) * 128)
            top = top_ref[k, :, cols]
            ref[8:8 + ROWS, :] = spec_ref[k, :, cols]
            ref[8 + ROWS:8 + ROWS + HALO, :] = bot_ref[k, :, cols]
            ref[8 + ROWS + HALO:8 + ext, :] = top
            ref[7:8, :] = top[HALO - 1:]
            ref[8 + ext:9 + ext, :] = spec_ref[k, 0:1, cols]
        ax = speeds[0, k]
        ay = speeds[1, k]
        ahead = jnp.where(ax >= 0.0, -1, 1)
        a = jnp.abs(ax)
        b = jnp.abs(ay)

        @pl.when(ay >= 0.0)
        def _():
            advance(k, ahead, a, b, True)

        @pl.when(ay < 0.0)
        def _():
            advance(k, ahead, a, b, False)

        return carry

    def block(i, carry):
        load(i).wait()
        lax.fori_loop(i * KB, (i + 1) * KB, one, 0)
        for copy in keep(i):
            copy.start()
        return carry

    lax.fori_loop(0, LOCAL // KB, block, 0)

    def regroup(g, carry):
        for h, prop in enumerate((prop0, prop1)):
            o = h * GROUP + g
            picked = prop[pl.ds(g, LOCAL * RUN, stride=GROUP), :]
            sent_ref[o] = picked.astype(jnp.bfloat16)
            give(o).start()
        return carry

    lax.fori_loop(0, GROUP, regroup, 0)

    def settle_keep(i, carry):
        for copy in keep(i):
            copy.wait()
        return carry

    def settle_give(o, carry):
        give(o).wait()
        return carry

    lax.fori_loop(0, LOCAL // KB, settle_keep, 0)
    lax.fori_loop(0, OWNERS, settle_give, 0)


def propagate(speeds, spectrum, top, bottom, wetness):
    cols = spectrum.shape[2]
    ext = ROWS + 2 * HALO
    vmem = pl.BlockSpec(memory_space=pltpu.VMEM)
    hbm = pl.BlockSpec(memory_space=pltpu.HBM)
    return pl.pallas_call(
        propagate_kernel,
        in_specs=[pl.BlockSpec(memory_space=pltpu.SMEM), hbm] + [vmem] * 3,
        out_specs=[hbm] * 3,
        out_shape=[
            pltpu.HBM((LOCAL * ROWS, 128), jnp.float32),
            pltpu.HBM((LOCAL * ROWS, 128), jnp.float32),
            pltpu.HBM((OWNERS, LOCAL * RUN, 128), jnp.bfloat16),
        ],
        scratch_shapes=[
            pltpu.VMEM((LOCAL, ROWS, cols), jnp.float32),
            pltpu.SemaphoreType.DMA((LOCAL // KB,)),
            pltpu.VMEM((LOCAL * ROWS, 128), jnp.float32),
            pltpu.VMEM((LOCAL * ROWS, 128), jnp.float32),
            pltpu.VMEM((OWNERS, LOCAL * RUN, 128), jnp.bfloat16),
            pltpu.VMEM((ext, cols), jnp.float32),
        ]
        + [pltpu.VMEM((ext + 16, 128), jnp.float32)] * 4
        + [pltpu.SemaphoreType.DMA((2, LOCAL // KB)), pltpu.SemaphoreType.DMA((OWNERS,))],
        compiler_params=pltpu.CompilerParams(vmem_limit_bytes=16 << 20),
        name="propagate",
    )(speeds, in_hbm(spectrum), *map(in_vmem, (top, bottom, wetness)))


MB = 384
NB = 256
FIRST = 2
FIRST_ROWS = FIRST * LOCAL
REST = RUN - FIRST
PIECES = 6
BLOCKS = RUN * 128 // NB


def source_kernel(
    recv_ref, quad_hbm, diss_ref, coef_ref, points_ref, first_hbm, rest_hbm,
    quad_ref, first_ref, rest_ref, flat, cur, xa, xb, rate, level, flat_first, flat_rest,
    quad_sem, out_sems,
):
    chunk = K
    fetch = pltpu.make_async_copy(quad_hbm, quad_ref, quad_sem)
    fetch.start()

    def give(o):
        return (
            pltpu.make_async_copy(first_ref.at[o], first_hbm.at[o], out_sems.at[0, o]),
            pltpu.make_async_copy(rest_ref.at[o], rest_hbm.at[o], out_sems.at[1, o]),
        )

    def widen(i, carry):
        flat[pl.ds(i * chunk, chunk), :] = recv_ref[pl.ds(i * chunk, chunk), :].astype(jnp.float32)
        return carry

    lax.fori_loop(0, RUN, widen, 0)
    for i in range(K // 128):
        rate[i * 128:(i + 1) * 128, :] = jnp.broadcast_to(diss_ref[i:i + 1, :], (128, 128)).T
    for j in range(RUN):
        base = flat[pl.ds(j, K, stride=RUN), :]
        cols = slice(j * 128, (j + 1) * 128)
        cur[:, cols] = base
        xa[:, cols] = base.astype(jnp.bfloat16)
        level[:, cols] = jnp.sum(base, axis=0, keepdims=True)

    coef = coef_ref[...]
    stress = [
        jnp.dot(coef, xa[:, n * NB:(n + 1) * NB], preferred_element_type=jnp.float32)
        for n in range(BLOCKS)
    ]

    fetch.wait()

    def step(old, new):
        for n in range(BLOCKS):
            cols = slice(n * NB, (n + 1) * NB)
            mean = level[:, cols] * (1.0 / K)
            sums = jnp.zeros((1, NB), jnp.float32)
            for m in range(K // MB):
                rows = slice(m * MB, (m + 1) * MB)
                product = jnp.dot(
                    quad_ref[rows, :], old[:, cols], preferred_element_type=jnp.float32
                )
                each = jnp.concatenate([rate[rows, :]] * (NB // 128), axis=1)
                now = cur[rows, cols]
                now = now + step_source * now * (product - each * mean)
                cur[rows, cols] = now
                new[rows, cols] = now.astype(jnp.bfloat16)
                sums = sums + jnp.sum(now, axis=0, keepdims=True)
            level[:, cols] = sums

    def two_steps(i, carry):
        step(xa, xb)
        step(xb, xa)
        return carry

    lax.fori_loop(0, SRC_STEPS // 2, two_steps, 0)
    for j in range(RUN):
        base = flat[pl.ds(j, K, stride=RUN), :]
        cols = slice(j * 128, (j + 1) * 128)
        gain = (cur[:, cols] - base).astype(jnp.bfloat16)
        xb[:, cols] = gain
        if j < FIRST:
            flat_first[pl.ds(j, K, stride=FIRST), :] = gain.astype(jnp.float32)
        else:
            flat_rest[pl.ds(j - FIRST, K, stride=REST), :] = gain.astype(jnp.float32)
    parts = []
    for n in range(BLOCKS):
        both = stress[n] + jnp.dot(
            coef, xb[:, n * NB:(n + 1) * NB], preferred_element_type=jnp.float32
        )
        rows = [both[c:c + 1] + both[3 + c:4 + c] + both[6 + c:7 + c] for c in range(3)]
        parts.append(jnp.concatenate(rows, axis=0) * (1.0 / K))
    pieces = []
    for c in range(3):
        rows = [parts[j * 128 // NB][c:c + 1, j * 128 % NB:j * 128 % NB + 128] for j in range(RUN)]
        whole = jnp.concatenate(rows + [jnp.zeros((8 - RUN, 128), jnp.float32)], axis=0)
        high = whole.astype(jnp.bfloat16).astype(jnp.float32)
        pieces += [high, whole - high]
    shared = jnp.concatenate(pieces, axis=0).astype(jnp.bfloat16)

    def narrow(o, carry):
        gain = flat_first[pl.ds(o * FIRST_ROWS, FIRST_ROWS), :].astype(jnp.bfloat16)
        first_ref[o, 0:FIRST_ROWS, :] = gain
        first_ref[o, FIRST_ROWS:FIRST_ROWS + 8 * PIECES, :] = shared
        rows = LOCAL * REST
        rest_ref[o] = flat_rest[pl.ds(o * rows, rows), :].astype(jnp.bfloat16)
        for copy in give(o):
            copy.start()
        return carry

    def settle(o, carry):
        for copy in give(o):
            copy.wait()
        return carry

    lax.fori_loop(0, OWNERS, narrow, 0)
    lax.fori_loop(0, OWNERS, settle, 0)


def sources(received, quad_matrix, rates, coef, points_list):
    points = RUN * 128
    vmem = pl.BlockSpec(memory_space=pltpu.VMEM)
    hbm = pl.BlockSpec(memory_space=pltpu.HBM)
    return pl.pallas_call(
        source_kernel,
        in_specs=[vmem, hbm, vmem, vmem, hbm],
        out_specs=[hbm] * 2,
        out_shape=[
            pltpu.HBM((OWNERS, FIRST_ROWS + 8 * PIECES, 128), jnp.bfloat16),
            pltpu.HBM((OWNERS, LOCAL * REST, 128), jnp.bfloat16),
        ],
        scratch_shapes=[
            pltpu.VMEM((K, K), jnp.bfloat16),
            pltpu.VMEM((OWNERS, FIRST_ROWS + 8 * PIECES, 128), jnp.bfloat16),
            pltpu.VMEM((OWNERS, LOCAL * REST, 128), jnp.bfloat16),
            pltpu.VMEM((K * RUN, 128), jnp.float32),
            pltpu.VMEM((K, points), jnp.float32),
            pltpu.VMEM((K, points), jnp.bfloat16),
            pltpu.VMEM((K, points), jnp.bfloat16),
            pltpu.VMEM((K, 128), jnp.float32),
            pltpu.VMEM((1, points), jnp.float32),
            pltpu.VMEM((K * FIRST, 128), jnp.float32),
            pltpu.VMEM((K * REST, 128), jnp.float32),
            pltpu.SemaphoreType.DMA(()),
            pltpu.SemaphoreType.DMA((2, OWNERS)),
        ],
        compiler_params=pltpu.CompilerParams(vmem_limit_bytes=30 << 20),
        name="sources",
    )(in_vmem(received), in_hbm(quad_matrix), in_vmem(rates), in_vmem(coef), in_hbm(points_list))


def pick_kernel(first_ref, points_ref, out_ref):
    pieces = []
    for i in range(PIECES):
        at = FIRST_ROWS + 8 * i
        rows = first_ref[:, at:at + 8, :].astype(jnp.float32).reshape(OWNERS * 8, 128)
        pieces.append(rows.T.astype(jnp.bfloat16))
    table = jnp.concatenate(pieces, axis=0)
    slot = lax.broadcasted_iota(jnp.int32, (OWNERS * 8, 128), 0)
    within = lax.broadcasted_iota(jnp.int32, (128, 128), 0)
    weights = (0.5, 0.3, 0.2)
    for t in range(TILES):
        hots, lows = [], []
        for m in range(3):
            p = points_ref[m * TILES + t:m * TILES + t + 1, :]
            row = p >> 8
            col = p & 255
            hi = (((col >> 7) * GROUP + (row & (GROUP - 1))) << 3) + (row >> 4)
            hots.append(jnp.where(slot == hi, 1.0, 0.0).astype(jnp.bfloat16))
            lows.append(col & 127)
        hot = jnp.concatenate(hots, axis=1)
        found = jnp.dot(table, hot, preferred_element_type=jnp.float32)
        for c in range(3):
            both = found[2 * c * 128:(2 * c + 1) * 128] + found[(2 * c + 1) * 128:(2 * c + 2) * 128]
            acc = jnp.zeros((128, 128), jnp.float32)
            for m in range(3):
                acc = acc + jnp.where(
                    within == lows[m], both[:, m * 128:(m + 1) * 128] * weights[m], 0.0
                )
            out_ref[c, t:t + 1, :] = jnp.sum(acc, axis=0, keepdims=True)


def pick(first, points):
    vmem = pl.BlockSpec(memory_space=pltpu.VMEM)
    return pl.pallas_call(
        pick_kernel,
        in_specs=[vmem] * 2,
        out_specs=vmem,
        out_shape=pltpu.VMEM((3, TILES, 128), jnp.float32),
        compiler_params=pltpu.CompilerParams(vmem_limit_bytes=10 << 20),
        name="pick",
    )(in_vmem(first), in_vmem(points))


def finish_kernel(
    first_ref, rest_ref, prop0_hbm, prop1_hbm, out_hbm,
    prop0, prop1, spread_first, spread_rest, out, sems, keep_sems,
):
    def keep(i):
        part = pl.ds(i * KB * ROWS, KB * ROWS)
        return [
            pltpu.make_async_copy(hbm.at[part], prop.at[part], keep_sems.at[h, i])
            for h, (prop, hbm) in enumerate(((prop0, prop0_hbm), (prop1, prop1_hbm)))
        ]

    def load(i, carry):
        for copy in keep(i):
            copy.start()
        return carry

    lax.fori_loop(0, LOCAL // KB, load, 0)

    def spread(g, carry):
        for h in range(2):
            o = h * GROUP + g
            spread_first[h, pl.ds(g, FIRST_ROWS, stride=GROUP), :] = first_ref[
                o, 0:FIRST_ROWS, :
            ].astype(jnp.float32)
            spread_rest[h, pl.ds(g, LOCAL * REST, stride=GROUP), :] = rest_ref[o].astype(
                jnp.float32
            )
        return carry

    lax.fori_loop(0, GROUP, spread, 0)
    cut = FIRST * GROUP

    def copy(i):
        part = pl.ds(i * KB, KB)
        return pltpu.make_async_copy(out.at[part], out_hbm.at[part], sems.at[i])

    def add(i, carry):
        for copy_in in keep(i):
            copy_in.wait()
        for kk in range(KB):
            k = i * KB + kk
            for h, prop in enumerate((prop0, prop1)):
                cols = slice(h * 128, (h + 1) * 128)
                out[k, 0:cut, cols] = (
                    prop[pl.ds(k * ROWS, cut), :] + spread_first[h, pl.ds(k * cut, cut), :]
                )
                tail = ROWS - cut
                out[k, cut:ROWS, cols] = (
                    prop[pl.ds(k * ROWS + cut, tail), :] + spread_rest[h, pl.ds(k * tail, tail), :]
                )
        copy(i).start()
        return carry

    lax.fori_loop(0, LOCAL // KB, add, 0)

    def settle(i, carry):
        copy(i).wait()
        return carry

    lax.fori_loop(0, LOCAL // KB, settle, 0)


def finish(first, rest, prop0, prop1):
    vmem = pl.BlockSpec(memory_space=pltpu.VMEM)
    hbm = pl.BlockSpec(memory_space=pltpu.HBM)
    shape = (LOCAL, ROWS, 256)
    return pl.pallas_call(
        finish_kernel,
        in_specs=[vmem, vmem, hbm, hbm],
        out_specs=hbm,
        out_shape=pltpu.HBM(shape, jnp.float32),
        scratch_shapes=[
            pltpu.VMEM((LOCAL * ROWS, 128), jnp.float32),
            pltpu.VMEM((LOCAL * ROWS, 128), jnp.float32),
            pltpu.VMEM((2, LOCAL * FIRST * GROUP, 128), jnp.float32),
            pltpu.VMEM((2, LOCAL * REST * GROUP, 128), jnp.float32),
            pltpu.VMEM(shape, jnp.float32),
            pltpu.SemaphoreType.DMA((LOCAL // KB,)),
            pltpu.SemaphoreType.DMA((2, LOCAL // KB)),
        ],
        compiler_params=pltpu.CompilerParams(vmem_limit_bytes=16 << 20),
        name="finish",
    )(in_vmem(first), in_vmem(rest), in_hbm(prop0), in_hbm(prop1))


def from_neighbours(low, high, axis):
    count = lax.axis_size(axis)
    ends = count - 1
    before = lax.ppermute(high, axis, [(i, (i + 1) % count) for i in range(ends)])
    after = lax.ppermute(low, axis, [((i + 1) % count, i) for i in range(ends)])
    return before, after


def diff_rows(extended):
    return 0.5 * (extended[2:, 1:-1] - extended[:-2, 1:-1])


def diff_cols(extended):
    return 0.5 * (extended[1:-1, 2:] - extended[1:-1, :-2])


def shallow_water(wide_state, wide_stress, tile_cols, tile_rows):
    groups = lax.axis_size("comp")
    wide_cols = wide_state.shape[2]
    global_col = (
        lax.axis_index("comp") * tile_cols - MARGIN + jnp.arange(wide_cols, dtype=jnp.int32)
    )
    within = (global_col >= 0) & (global_col < tile_cols * groups)
    inside = within.astype(jnp.float32)[None, :]
    rimmed = jnp.pad(jnp.where(within, wide_stress, 0.0), ((0, 0), (1, 1), (1, 1)))
    force_down = -(diff_rows(rimmed[0]) + diff_cols(rimmed[1]))
    force_across = -(diff_rows(rimmed[1]) + diff_cols(rimmed[2]))
    height, flow_down, flow_across = wide_state
    for _ in range(SW_STEPS):
        down_ext = jnp.pad(flow_down, 1)
        across_ext = jnp.pad(flow_across, 1)
        height = (height - wave_speed * (diff_rows(down_ext) + diff_cols(across_ext))) * inside
        height_ext = jnp.pad(height, 1)
        flow_down = (
            (1.0 - friction) * flow_down
            - wave_speed * diff_rows(height_ext)
            + forcing_gain * force_down
        ) * inside
        flow_across = (
            (1.0 - friction) * flow_across
            - wave_speed * diff_cols(height_ext)
            + forcing_gain * force_across
        ) * inside
    stacked = jnp.stack([height, flow_down, flow_across])
    row_start = lax.axis_index("band") * tile_rows
    own_rows = lax.dynamic_slice_in_dim(stacked, row_start, tile_rows, 1)
    return own_rows[:, :, MARGIN:MARGIN + tile_cols]


def window(spectrum, wet_mask, quad_matrix, dissipation, circulation, source_points):
    offset = lax.axis_index("comp") * LOCAL
    speed_east, speed_north, _ = component_tables(offset, LOCAL)
    speeds = jnp.stack([speed_east, speed_north])
    wetness = wet_mask.astype(jnp.float32)[None]
    low = jnp.concatenate([spectrum[:, :HALO], wetness[:, :HALO]], axis=0)
    high = jnp.concatenate([spectrum[:, -HALO:], wetness[:, -HALO:]], axis=0)
    top, bottom = from_neighbours(low, high, "band")
    prop0, prop1, sent = propagate(speeds, spectrum, top, bottom, wetness[0])
    received = lax.all_to_all(sent, "comp", 0, 0, tiled=True)

    tile_rows = circulation.shape[1]
    tile_cols = circulation.shape[2]
    both = jnp.concatenate([circulation, source_points.astype(jnp.float32)], axis=0)
    before, after = from_neighbours(both[:, :, :MARGIN], both[:, :, -MARGIN:], "comp")
    wide = jnp.concatenate([before, both, after], axis=2)
    left_points = before[3:].astype(jnp.int32).reshape(3, 1, 128)
    right_points = after[3:].astype(jnp.int32).reshape(3, 1, 128)
    points = jnp.concatenate([source_points, left_points, right_points], axis=1)
    points = points.reshape(3 * TILES, 128)

    full_coef = component_tables(0, K)[2]
    coef_high = full_coef.astype(jnp.bfloat16).astype(jnp.float32)
    coef_mid = (full_coef - coef_high).astype(jnp.bfloat16).astype(jnp.float32)
    coef_low = full_coef - coef_high - coef_mid
    spare = jnp.zeros((7, K), jnp.float32)
    coef = jnp.concatenate([coef_high, coef_mid, coef_low, spare]).astype(jnp.bfloat16)
    first, rest = sources(
        received.reshape(K * RUN, 128), quad_matrix, dissipation.reshape(K // 128, 128), coef, points
    )
    first = lax.all_to_all(first, "comp", 0, 0, tiled=True)
    rest = lax.all_to_all(rest, "comp", 0, 0, tiled=True)
    cells = pick(first, points)
    own = cells[:, :tile_rows]
    left = cells[:, tile_rows].reshape(3, tile_rows, MARGIN)
    right = cells[:, tile_rows + 1].reshape(3, tile_rows, MARGIN)
    wide_cells = jnp.concatenate([left, own, right], axis=2)
    everything = lax.all_gather(
        jnp.concatenate([wide[:3], wide_cells], axis=0), "band", axis=1, tiled=True
    )
    circulation_out = shallow_water(everything[:3], everything[3:], tile_cols, tile_rows)
    spectrum_out = finish(first, rest, prop0, prop1)
    return spectrum_out, circulation_out


def solution(mesh):
    in_specs = (
        P("comp", "band", None),
        P("band", None),
        P(),
        P(),
        P(None, "band", "comp"),
        P(None, "band", "comp"),
    )
    out_specs = (P("comp", "band", None), P(None, "band", "comp"))
    return jax.shard_map(window, mesh=mesh, in_specs=in_specs, out_specs=out_specs, check_vma=False)
```

time: 147 us -> 135 us (0.918)
  Pallas kernels: 50.2 us -> 38.2 us
  waiting for transfers between devices: 27.2 us -> 39 us
  local copies, waits for them, and re-layouts: 9.89 us -> 2.26 us
  starting transfers between devices: 40.1 us -> 35.1 us
    all_to_all x3, waiting for transfers between devices: 24.1 us -> 39 us  [the longest x1 22.4 us: window(): received = lax.all_to_all(sent, 'comp', 0, 0, tiled=True)]
    pallas_call x4, Pallas kernels: 50.2 us -> 38.2 us  [the longest x1 16.8 us: propagate(): pl.pallas_call(propagate_kernel, in_specs=[pl.BlockSpec(memory_space=pltp...]
    all_to_all x3, starting transfers between devices: 26.7 us -> 21.7 us  [the longest x1 8.48 us: window(): first = lax.all_to_all(first, 'comp', 0, 0, tiled=True)]
    broadcast_in_dim x3 -> x1, local copies, waits for them, and re-layouts: 4.33 us -> 0.01 us  [window(): spare = jnp.zeros((7, K), jnp.float32)]
    ppermute x2, waiting for transfers between devices: 3.02 us -> 0.01 us  [from_neighbours(): after = lax.ppermute(low, axis, [((i + 1) % count, i) for i in range(ends)])]
    unnamed x16 -> x8, local copies, waits for them, and re-layouts: 1.92 us -> 0.02 us
    convert_element_type x3 -> x6, other arithmetic: 0.01 us -> 1.68 us  [the longest x1 0.91 us: window(): wetness = wet_mask.astype(jnp.float32)[None]]
    slice x4, local copies, waits for them, and re-layouts: 2.62 us -> 1.14 us  [the longest x2 1.11 us: window(): low = jnp.concatenate([spectrum[:, :HALO], wetness[:, :HALO]], axis=0)]
  transfers between devices with their start and end apart: 7 -> 7, of which waited for: 4 -> 3; matrix products, arithmetic and copies ran while one was open for 7% -> 4% of each run, Pallas kernels for 18% -> 14%
where the time goes in v2:
time: 135 us; the launch traced here: 133 us
  waiting for transfers between devices  39 us (29%)
  Pallas kernels  38.2 us (28%)
  starting transfers between devices  35.1 us (26%)
  blocking collectives  12.3 us (9%)
  other arithmetic  5.36 us (4%)
  local copies, waits for them, and re-layouts  2.26 us (2%)
    all_to_all x1, waiting for transfers between devices, window(): received = lax.all_to_all(sent, 'comp', 0, 0, tiled=True)  22.4 us
    pallas_call x1, Pallas kernels, propagate(): pl.pallas_call(propagate_kernel, in_specs=[pl.BlockSpec(memory_space=pltp...  16.8 us
    all_to_all x1, waiting for transfers between devices, window(): first = lax.all_to_all(first, 'comp', 0, 0, tiled=True)  16 us
    pallas_call x1, Pallas kernels, sources(): pl.pallas_call(source_kernel, in_specs=[vmem, hbm, vmem, vmem, hbm], out_...  15.1 us
    all_gather x1, blocking collectives, window(): lax.all_gather(jnp.concatenate([wide[:3], wide_cells], axis=0), 'band', a...  12.3 us
    all_to_all x1, starting transfers between devices, window(): first = lax.all_to_all(first, 'comp', 0, 0, tiled=True)  8.48 us
    ppermute x2, starting transfers between devices, from_neighbours(): after = lax.ppermute(low, axis, [((i + 1) % count, i) for i in range(ends)])  8.23 us
    all_to_all x1, starting transfers between devices, window(): received = lax.all_to_all(sent, 'comp', 0, 0, tiled=True)  7.39 us
  transfers between devices with their start and end apart: 7, of which 3 were waited for; matrix products, arithmetic and copies ran while one was open for 4% of the time, Pallas kernels for 14%

profile of v2, /device:TPU:6, one launch (start us, length us, event | category | flops | bytes accessed | tf_op | source)
XLA Modules:
  0.0 133.2 jit_solution(6215052925678893447)
XLA Ops:
  0.6 0.9 fusion.164
  1.6 1.1 fusion.163
  2.7 1.7 %collective-permute-start = (f32[37,4,256]{2,1,0:T(4,128)S(1)}, f32[37,4,256]{2,1,0:T(4,128)S(1)}, u32[]{:S(2)}, u32[]{:S(2)}) collective-permute-start(f32[37,4,256]{2,1,0:T(4,128)S(1)} %pad_maximum_fusion), channel_id=1, source_target_pairs={{0,1},{1,2},{2,3},{4,5},{5,6},{6,7},{8,9},{9,10},{10,11},{12,13},{... | collective-permute-start | bytes 454664 | tf_op jit(solution)/shard_map/ppermute | solution.py:486
  4.5 1.3 collective-permute-start.1
  5.8 0.7 convert_element_type.140
  6.5 0.9 slice_maximum_fusion
  7.4 3.5 %collective-permute-start.2 = (f32[6,8,16]{2,1,0:T(8,128)S(1)}, f32[6,8,16]{2,1,0:T(8,128)S(1)}, u32[]{:S(2)}, u32[]{:S(2)}) collective-permute-start(f32[6,8,16]{2,1,0:T(8,128)S(1)} %get-tuple-element.45), channel_id=1, source_target_pairs={{0,4},{4,8},{8,12},{12,16},{16,20},{20,24},{24,28},{28,32},{32,36}... | collective-permute-start | bytes 9224 | tf_op jit(solution)/shard_map/ppermute | solution.py:486
  10.9 6.9 %collective-permute-start.3 = (f32[6,8,16]{2,1,0:T(8,128)S(1)}, f32[6,8,16]{2,1,0:T(8,128)S(1)}, u32[]{:S(2)}, u32[]{:S(2)}) collective-permute-start(f32[6,8,16]{2,1,0:T(8,128)S(1)} %get-tuple-element.46), channel_id=1, source_target_pairs={{4,0},{8,4},{12,8},{16,12},{20,16},{24,20},{28,24},{32,28},{36,32}... | collective-permute-start | bytes 9224 | tf_op jit(solution)/shard_map/ppermute | solution.py:487
  17.8 0.1 sine_multiply_fusion
  17.9 0.0 collective-permute-done.top_ref
  17.9 0.0 collective-permute-done.1.bot_ref
  17.9 16.8 %propagate.1 = (f32[3456,128]{1,0:T(8,128)}, f32[3456,128]{1,0:T(8,128)}, bf16[32,216,128]{2,1,0:T(8,128)(2,1)}) custom-call(f32[2,36]{1,0:T(2,128)S(1)} %pad_maximum_fusion.4.speeds, f32[36,96,256]{2,1,0:T(8,128)} %spec_hbm.1, f32[37,4,256]{2,1,0:T(4,128)S(1)} %collective-permute-done.top_ref, f32[37,4,256]{2,1,0:T(4,128)S(1)} %collective-permute-done.1.bot_ref, ...), custom_call_target="tpu_custom_call" | custom-call | tf_op jit(solution)/shard_map/propagate/pallas_call | solution.py:186
  34.7 0.0 copy-start.3
  34.7 0.0 copy-start.1
  34.7 7.4 %all-to-all-start = ((bf16[32,216,128]{2,1,0:T(8,128)(2,1)}), bf16[32,216,128]{2,1,0:T(8,128)(2,1)S(1)}, u32[]{:S(2)}, u32[]{:S(2)}) async-start(bf16[32,216,128]{2,1,0:T(8,128)(2,1)} %get-tuple-element.7), calls=%async_computation | async-start | bytes 3538944 | tf_op jit(solution)/shard_map/all_to_all | solution.py:541
  42.1 0.2 multiply_add_fusion.1
  42.3 0.1 pad.121.clone
  42.4 0.2 multiply_add_fusion
  42.6 0.1 maximum_maximum_fusion.coef_ref
  42.7 0.0 collective-permute-done.2
  42.7 0.1 reshape.245
  42.8 0.0 collective-permute-done.3
  42.8 0.1 reshape.246
  42.9 0.0 copy-done.3
  42.9 0.6 reshape.244.points_ref
  43.5 22.4 %all-to-all-done = bf16[32,216,128]{2,1,0:T(8,128)(2,1)S(1)} async-done(((bf16[32,216,128]{2,1,0:T(8,128)(2,1)}), bf16[32,216,128]{2,1,0:T(8,128)(2,1)S(1)}, u32[]{:S(2)}, u32[]{:S(2)}) %all-to-all-start) | async-done | bytes 1769504 | tf_op jit(solution)/shard_map/all_to_all | solution.py:541
  65.9 0.0 copy-done.1
  65.9 15.1 %sources.1 = (bf16[32,120,128]{2,1,0:T(8,128)(2,1)}, bf16[32,144,128]{2,1,0:T(8,128)(2,1)}) custom-call(bf16[6912,128]{1,0:T(8,128)(2,1)S(1)} %bitcast.27, bf16[1152,1152]{1,0:T(8,128)(2,1)} %quad_hbm.1, f32[9,128]{1,0:T(8,128)S(1)} %bitcast.28, bf16[16,1152]{1,0:T(8,128)(2,1)S(1)} %maximum_maximum_fusion.coef_ref, s32[30,128]{1,0:T(8,128)} %reshape.244.points_ref), custom_call_target="tpu_custom_call" | custom-call | tf_op jit(solution)/shard_map/sources/pallas_call | solution.py:327
  81.1 0.0 copy-start
  81.1 8.5 %all-to-all-start.1 = ((bf16[32,120,128]{2,1,0:T(8,128)(2,1)}), bf16[32,120,128]{2,1,0:T(8,128)(2,1)S(1)}, u32[]{:S(2)}, u32[]{:S(2)}) async-start(bf16[32,120,128]{2,1,0:T(8,128)(2,1)} %get-tuple-element.8), calls=%async_computation.1 | async-start | bytes 1966080 | tf_op jit(solution)/shard_map/all_to_all | solution.py:562
  89.6 0.0 copy-start.2
  89.6 16.0 %all-to-all-done.1.first_ref = bf16[32,120,128]{2,1,0:T(8,128)(2,1)S(1)} async-done(((bf16[32,120,128]{2,1,0:T(8,128)(2,1)}), bf16[32,120,128]{2,1,0:T(8,128)(2,1)S(1)}, u32[]{:S(2)}, u32[]{:S(2)}) %all-to-all-start.1) | async-done | bytes 983072 | tf_op jit(solution)/shard_map/all_to_all | solution.py:562
  105.6 5.8 %all-to-all-start.2 = ((bf16[32,144,128]{2,1,0:T(8,128)(2,1)}), bf16[32,144,128]{2,1,0:T(8,128)(2,1)S(1)}, u32[]{:S(2)}, u32[]{:S(2)}) async-start(bf16[32,144,128]{2,1,0:T(8,128)(2,1)} %get-tuple-element.9), calls=%async_computation.2 | async-start | bytes 2359296 | tf_op jit(solution)/shard_map/all_to_all | solution.py:563
  111.4 0.0 copy-done
  111.4 2.4 %pick.1 = f32[3,10,128]{2,1,0:T(8,128)S(1)} custom-call(bf16[32,120,128]{2,1,0:T(8,128)(2,1)S(1)} %all-to-all-done.1.first_ref, s32[30,128]{1,0:T(8,128)S(1)} %copy-done), custom_call_target="tpu_custom_call" | custom-call | tf_op jit(solution)/shard_map/pick/pallas_call | solution.py:388
  113.8 0.1 reshape_squeeze.6
  113.8 0.1 reshape_squeeze.7
  113.9 0.0 copy-done.2
  113.9 0.1 fusion
  114.0 12.3 %all_gather.3 = f32[6,32,160]{2,1,0:T(8,128)S(1)} all-gather(f32[6,8,160]{2,1,0:T(8,128)S(1)} %fusion), channel_id=1, replica_groups=mesh['comp'=32,'band'=4] {'band'}, dimensions={1}, use_global_device_ids=true | all-gather | bytes 153600 | tf_op jit(solution)/shard_map/all_gather | solution.py:569
  126.3 0.1 fusion.5
  126.4 0.1 fusion.10
  126.5 0.1 fusion.63
  126.6 0.1 fusion.16
  126.7 0.1 fusion.73
  126.8 0.1 fusion.22
  126.9 0.1 fusion.83
  127.0 0.1 fusion.28
  127.1 0.1 fusion.93
  127.2 0.1 fusion.34
  127.3 0.1 fusion.103
  127.4 0.1 fusion.40
  127.5 0.1 fusion.113
  127.6 0.1 fusion.46
  127.7 0.1 fusion.123
  127.8 0.1 fusion.52
  127.9 0.1 fusion.135
  128.0 0.7 fusion.145
  128.7 0.6 all-to-all-done.2.rest_ref
  129.3 3.9 %finish.1 = f32[36,96,256]{2,1,0:T(8,128)} custom-call(bf16[32,120,128]{2,1,0:T(8,128)(2,1)S(1)} %all-to-all-done.1.first_ref, bf16[32,144,128]{2,1,0:T(8,128)(2,1)S(1)} %all-to-all-done.2.rest_ref, f32[3456,128]{1,0:T(8,128)} %get-tuple-element.10.prop0_hbm, f32[3456,128]{1,0:T(8,128)} %get-tuple-element.11.prop1_hbm), custom_call_target="tpu_custom_call" | custom-call | tf_op jit(solution)/shard_map/finish/pallas_call | solution.py:464
  (15 shorter events, 0.2 us)
Async XLA Ops:
  2.7 15.2 %collective-permute-start = (f32[37,4,256]{2,1,0:T(4,128)S(1)}, f32[37,4,256]{2,1,0:T(4,128)S(1)}, u32[]{:S(2)}, u32[]{:S(2)}) collective-permute-start(f32[37,4,256]{2,1,0:T(4,128)S(1)} %pad_maximum_fusion), channel_id=1, source_target_pairs={{0,1},{1,2},{2,3},{4,5},{5,6},{6,7},{8,9},{9,10},{10,11},{12,13},{... | collective-permute-start | bytes 454664 | tf_op jit(solution)/shard_map/ppermute | solution.py:486
  4.5 13.4 %collective-permute-start.1 = (f32[37,4,256]{2,1,0:T(4,128)S(1)}, f32[37,4,256]{2,1,0:T(4,128)S(1)}, u32[]{:S(2)}, u32[]{:S(2)}) collective-permute-start(f32[37,4,256]{2,1,0:T(4,128)S(1)} %pad_maximum_fusion.1), channel_id=1, source_target_pairs={{1,0},{2,1},{3,2},{5,4},{6,5},{7,6},{9,8},{10,9},{11,10},{13,12},{... | collective-permute-start | bytes 454664 | tf_op jit(solution)/shard_map/ppermute | solution.py:487
  7.4 35.3 %collective-permute-start.2 = (f32[6,8,16]{2,1,0:T(8,128)S(1)}, f32[6,8,16]{2,1,0:T(8,128)S(1)}, u32[]{:S(2)}, u32[]{:S(2)}) collective-permute-start(f32[6,8,16]{2,1,0:T(8,128)S(1)} %get-tuple-element.45), channel_id=1, source_target_pairs={{0,4},{4,8},{8,12},{12,16},{16,20},{20,24},{24,28},{28,32},{32,36}... | collective-permute-start | bytes 9224 | tf_op jit(solution)/shard_map/ppermute | solution.py:486
  10.9 31.9 %collective-permute-start.3 = (f32[6,8,16]{2,1,0:T(8,128)S(1)}, f32[6,8,16]{2,1,0:T(8,128)S(1)}, u32[]{:S(2)}, u32[]{:S(2)}) collective-permute-start(f32[6,8,16]{2,1,0:T(8,128)S(1)} %get-tuple-element.46), channel_id=1, source_target_pairs={{4,0},{8,4},{12,8},{16,12},{20,16},{24,20},{28,24},{32,28},{36,32}... | collective-permute-start | bytes 9224 | tf_op jit(solution)/shard_map/ppermute | solution.py:487
  34.7 8.2 %copy-start.3 = (s32[3,8,128]{2,1,0:T(8,128)S(1)}, s32[3,8,128]{2,1,0:T(8,128)}, u32[]{:S(2)}) copy-start(s32[3,8,128]{2,1,0:T(8,128)} %param.11) | copy-start | bytes 36868
  34.7 31.2 %copy-start.1 = (f32[1152]{0:T(1024)S(1)}, f32[1152]{0:T(1024)}, u32[]{:S(2)}) copy-start(f32[1152]{0:T(1024)} %param.9) | copy-start | bytes 13828
  34.7 31.2 %all-to-all-start = ((bf16[32,216,128]{2,1,0:T(8,128)(2,1)}), bf16[32,216,128]{2,1,0:T(8,128)(2,1)S(1)}, u32[]{:S(2)}, u32[]{:S(2)}) async-start(bf16[32,216,128]{2,1,0:T(8,128)(2,1)} %get-tuple-element.7), calls=%async_computation | async-start | bytes 3538944 | tf_op jit(solution)/shard_map/all_to_all | solution.py:541
  81.1 30.3 %copy-start = (s32[30,128]{1,0:T(8,128)S(1)}, s32[30,128]{1,0:T(8,128)}, u32[]{:S(2)}) copy-start(s32[30,128]{1,0:T(8,128)} %reshape.244.points_ref) | copy-start | bytes 46084
  81.1 24.5 %all-to-all-start.1 = ((bf16[32,120,128]{2,1,0:T(8,128)(2,1)}), bf16[32,120,128]{2,1,0:T(8,128)(2,1)S(1)}, u32[]{:S(2)}, u32[]{:S(2)}) async-start(bf16[32,120,128]{2,1,0:T(8,128)(2,1)} %get-tuple-element.8), calls=%async_computation.1 | async-start | bytes 1966080 | tf_op jit(solution)/shard_map/all_to_all | solution.py:562
  89.6 24.4 %copy-start.2 = (f32[3,8,128]{2,1,0:T(8,128)S(1)}, f32[3,8,128]{2,1,0:T(8,128)}, u32[]{:S(2)}) copy-start(f32[3,8,128]{2,1,0:T(8,128)} %param.10) | copy-start | bytes 36868
  105.6 23.7 %all-to-all-start.2 = ((bf16[32,144,128]{2,1,0:T(8,128)(2,1)}), bf16[32,144,128]{2,1,0:T(8,128)(2,1)S(1)}, u32[]{:S(2)}, u32[]{:S(2)}) async-start(bf16[32,144,128]{2,1,0:T(8,128)(2,1)} %get-tuple-element.9), calls=%async_computation.2 | async-start | bytes 2359296 | tf_op jit(solution)/shard_map/all_to_all | solution.py:563

commit v3 on v2

--- a/solution.py
+++ b/solution.py
@@ -27,6 +27,7 @@
 RUN = 6
 HALO = 4
 KB = 4
+PAIR = KB
 MARGIN = 2 * SW_STEPS
 TILES = 10
 
@@ -74,8 +75,15 @@
             for h, (prop, hbm) in enumerate(((prop0, prop0_hbm), (prop1, prop1_hbm)))
         ]
 
-    def give(o):
-        return pltpu.make_async_copy(sent_ref.at[o], sent_hbm.at[o], sent_sems.at[o])
+    def give(i):
+        rows = pl.ds(i * KB * RUN, KB * RUN)
+        return pltpu.make_async_copy(sent_ref.at[i], sent_hbm.at[:, rows, :], sent_sems.at[i])
+
+    def regroup(i):
+        for h, prop in enumerate((prop0, prop1)):
+            for g in range(GROUP):
+                picked = prop[pl.ds(i * KB * ROWS + g, KB * RUN, stride=GROUP), :]
+                sent_ref[i, h * GROUP + g] = picked.astype(jnp.bfloat16)
 
     def load(i):
         part = pl.ds(i * KB, KB)
@@ -90,92 +98,87 @@
     wet[ROWS:ROWS + HALO, :] = bot_ref[LOCAL]
     wet[ROWS + HALO:ext, :] = top_ref[LOCAL]
     lane = lax.broadcasted_iota(jnp.int32, (ext, 128), 1)
-
-    def advance(k, ahead, a, b, north):
-        c = 1.0 - a - b
+    fields = [[(left_a.at[q], right_a.at[q]), (left_b.at[q], right_b.at[q])] for q in range(PAIR)]
+
+    def advance(first, north):
         edge = 0 if north else 127
         turn = 1 if north else 127
-        side = jnp.where(lane == edge, 0.0, b)
-        fields = ((left_a, right_a), (left_b, right_b))
+        ahead, a, b, c, side = [], [], [], [], []
+        for q in range(PAIR):
+            ax = speeds[0, first + q]
+            ahead.append(jnp.where(ax >= 0.0, 7, 9))
+            a.append(jnp.abs(ax))
+            b.append(jnp.abs(speeds[1, first + q]))
+            c.append(1.0 - a[q] - b[q])
+            side.append(jnp.where(lane == edge, 0.0, b[q]))
         for s in range(SUBSTEPS):
-            left_ref, right_ref = fields[s % 2]
-            left, right = left_ref[8:8 + ext, :], right_ref[8:8 + ext, :]
-            ul = left_ref[pl.ds(8 + ahead, ext), :]
-            ur = right_ref[pl.ds(8 + ahead, ext), :]
-            rl = pltpu.roll(left, turn, 1)
-            rr = pltpu.roll(right, turn, 1)
-            if north:
-                across_l = side * rl
-                across_r = b * jnp.where(lane == 0, rl, rr)
-            else:
-                across_l = b * jnp.where(lane == 127, rr, rl)
-                across_r = side * rr
-            left = wet[:, :128] * (c * left + a * ul + across_l)
-            right = wet[:, 128:] * (c * right + a * ur + across_r)
-            if s + 1 < SUBSTEPS:
-                left_ref, right_ref = fields[(s + 1) % 2]
-                for ref, value in ((left_ref, left), (right_ref, right)):
-                    ref[8:8 + ext, :] = value
-                    ref[7:8, :] = value[ext - 1:]
-                    ref[8 + ext:9 + ext, :] = value[0:1]
-        prop0[pl.ds(k * ROWS, ROWS), :] = left[:ROWS]
-        prop1[pl.ds(k * ROWS, ROWS), :] = right[:ROWS]
-
-    def one(k, carry):
-        for h, ref in enumerate((left_a, right_a)):
-            cols = slice(h * 128, (h + 1) * 128)
-            top = top_ref[k, :, cols]
-            ref[8:8 + ROWS, :] = spec_ref[k, :, cols]
-            ref[8 + ROWS:8 + ROWS + HALO, :] = bot_ref[k, :, cols]
-            ref[8 + ROWS + HALO:8 + ext, :] = top
-            ref[7:8, :] = top[HALO - 1:]
-            ref[8 + ext:9 + ext, :] = spec_ref[k, 0:1, cols]
-        ax = speeds[0, k]
-        ay = speeds[1, k]
-        ahead = jnp.where(ax >= 0.0, -1, 1)
-        a = jnp.abs(ax)
-        b = jnp.abs(ay)
+            for q in range(PAIR):
+                left_ref, right_ref = fields[q][s % 2]
+                left, right = left_ref[8:8 + ext, :], right_ref[8:8 + ext, :]
+                ul = left_ref[pl.ds(ahead[q], ext), :]
+                ur = right_ref[pl.ds(ahead[q], ext), :]
+                rl = pltpu.roll(left, turn, 1)
+                rr = pltpu.roll(right, turn, 1)
+                if north:
+                    across_l = side[q] * rl
+                    across_r = b[q] * jnp.where(lane == 0, rl, rr)
+                else:
+                    across_l = b[q] * jnp.where(lane == 127, rr, rl)
+                    across_r = side[q] * rr
+                left = wet[:, :128] * (c[q] * left + a[q] * ul + across_l)
+                right = wet[:, 128:] * (c[q] * right + a[q] * ur + across_r)
+                if s + 1 < SUBSTEPS:
+                    for ref, value in zip(fields[q][(s + 1) % 2], (left, right)):
+                        ref[8:8 + ext, :] = value
+                        ref[7:8, :] = value[ext - 1:]
+                        ref[8 + ext:9 + ext, :] = value[0:1]
+                else:
+                    prop0[pl.ds((first + q) * ROWS, ROWS), :] = left[:ROWS]
+                    prop1[pl.ds((first + q) * ROWS, ROWS), :] = right[:ROWS]
+
+    def some(i, carry):
+        first = i * PAIR
+        for q in range(PAIR):
+            k = first + q
+            for h, ref in enumerate(fields[q][0]):
+                cols = slice(h * 128, (h + 1) * 128)
+                top = top_ref[k, :, cols]
+                ref[8:8 + ROWS, :] = spec_ref[k, :, cols]
+                ref[8 + ROWS:8 + ROWS + HALO, :] = bot_ref[k, :, cols]
+                ref[8 + ROWS + HALO:8 + ext, :] = top
+                ref[7:8, :] = top[HALO - 1:]
+                ref[8 + ext:9 + ext, :] = spec_ref[k, 0:1, cols]
+        ay = speeds[1, first]
 
         @pl.when(ay >= 0.0)
         def _():
-            advance(k, ahead, a, b, True)
+            advance(first, True)
 
         @pl.when(ay < 0.0)
         def _():
-            advance(k, ahead, a, b, False)
+            advance(first, False)
 
         return carry
 
     def block(i, carry):
         load(i).wait()
-        lax.fori_loop(i * KB, (i + 1) * KB, one, 0)
+        some(i, 0)
+        regroup(i)
+        give(i).start()
         for copy in keep(i):
             copy.start()
         return carry
 
-    lax.fori_loop(0, LOCAL // KB, block, 0)
-
-    def regroup(g, carry):
-        for h, prop in enumerate((prop0, prop1)):
-            o = h * GROUP + g
-            picked = prop[pl.ds(g, LOCAL * RUN, stride=GROUP), :]
-            sent_ref[o] = picked.astype(jnp.bfloat16)
-            give(o).start()
-        return carry
-
-    lax.fori_loop(0, GROUP, regroup, 0)
-
-    def settle_keep(i, carry):
+    count = LOCAL // KB
+    lax.fori_loop(0, count, block, 0)
+
+    def settle(i, carry):
         for copy in keep(i):
             copy.wait()
-        return carry
-
-    def settle_give(o, carry):
-        give(o).wait()
-        return carry
-
-    lax.fori_loop(0, LOCAL // KB, settle_keep, 0)
-    lax.fori_loop(0, OWNERS, settle_give, 0)
+        give(i).wait()
+        return carry
+
+    lax.fori_loop(0, count, settle, 0)
 
 
 def propagate(speeds, spectrum, top, bottom, wetness):
@@ -197,17 +200,18 @@
             pltpu.SemaphoreType.DMA((LOCAL // KB,)),
             pltpu.VMEM((LOCAL * ROWS, 128), jnp.float32),
             pltpu.VMEM((LOCAL * ROWS, 128), jnp.float32),
-            pltpu.VMEM((OWNERS, LOCAL * RUN, 128), jnp.bfloat16),
+            pltpu.VMEM((LOCAL // KB, OWNERS, KB * RUN, 128), jnp.bfloat16),
             pltpu.VMEM((ext, cols), jnp.float32),
         ]
-        + [pltpu.VMEM((ext + 16, 128), jnp.float32)] * 4
-        + [pltpu.SemaphoreType.DMA((2, LOCAL // KB)), pltpu.SemaphoreType.DMA((OWNERS,))],
+        + [pltpu.VMEM((PAIR, ext + 16, 128), jnp.float32)] * 4
+        + [pltpu.SemaphoreType.DMA((2, LOCAL // KB)), pltpu.SemaphoreType.DMA((LOCAL // KB,))],
         compiler_params=pltpu.CompilerParams(vmem_limit_bytes=16 << 20),
         name="propagate",
     )(speeds, in_hbm(spectrum), *map(in_vmem, (top, bottom, wetness)))
 
 
-MB = 384
+MB = 576
+EB = 64
 NB = 256
 FIRST = 2
 FIRST_ROWS = FIRST * LOCAL
@@ -218,7 +222,7 @@
 
 def source_kernel(
     recv_ref, quad_hbm, diss_ref, coef_ref, points_ref, first_hbm, rest_hbm,
-    quad_ref, first_ref, rest_ref, flat, cur, xa, xb, rate, level, flat_first, flat_rest,
+    quad_ref, first_ref, rest_ref, prod_a, prod_b, flat, cur, xa, xb, rate, level, flat_first, flat_rest,
     quad_sem, out_sems,
 ):
     chunk = K
@@ -253,30 +257,39 @@
 
     fetch.wait()
 
-    def step(old, new):
-        for n in range(BLOCKS):
-            cols = slice(n * NB, (n + 1) * NB)
-            mean = level[:, cols] * (1.0 / K)
-            sums = jnp.zeros((1, NB), jnp.float32)
-            for m in range(K // MB):
-                rows = slice(m * MB, (m + 1) * MB)
-                product = jnp.dot(
-                    quad_ref[rows, :], old[:, cols], preferred_element_type=jnp.float32
-                )
-                each = jnp.concatenate([rate[rows, :]] * (NB // 128), axis=1)
-                now = cur[rows, cols]
-                now = now + step_source * now * (product - each * mean)
-                cur[rows, cols] = now
+    def multiply(s, n):
+        held = (prod_a, prod_b)[(s * BLOCKS + n) % 2]
+        old = (xa, xb)[s % 2]
+        for m in range(K // MB):
+            rows = slice(m * MB, (m + 1) * MB)
+            held[rows, :] = jnp.dot(
+                quad_ref[rows, :], old[:, n * NB:(n + 1) * NB], preferred_element_type=jnp.float32
+            )
+
+    def update(s, n):
+        held = (prod_a, prod_b)[(s * BLOCKS + n) % 2]
+        new = (xb, xa)[s % 2]
+        cols = slice(n * NB, (n + 1) * NB)
+        mean = level[:, cols] * (1.0 / K)
+        sums = jnp.zeros((8, NB), jnp.float32)
+        for m in range(K // EB):
+            rows = slice(m * EB, (m + 1) * EB)
+            each = jnp.concatenate([rate[rows, :]] * (NB // 128), axis=1)
+            now = cur[rows, cols]
+            now = now + step_source * now * (held[rows, :] - each * mean)
+            cur[rows, cols] = now
+            if s + 1 < SRC_STEPS:
                 new[rows, cols] = now.astype(jnp.bfloat16)
-                sums = sums + jnp.sum(now, axis=0, keepdims=True)
-            level[:, cols] = sums
-
-    def two_steps(i, carry):
-        step(xa, xb)
-        step(xb, xa)
-        return carry
-
-    lax.fori_loop(0, SRC_STEPS // 2, two_steps, 0)
+                sums = sums + jnp.sum(now.reshape(EB // 8, 8, NB), axis=0)
+        if s + 1 < SRC_STEPS:
+            level[:, cols] = jnp.sum(sums, axis=0, keepdims=True)
+
+    turns = [(s, n) for s in range(SRC_STEPS) for n in range(BLOCKS)]
+    for i, turn in enumerate(turns):
+        multiply(*turn)
+        if i > 0:
+            update(*turns[i - 1])
+    update(*turns[-1])
     for j in range(RUN):
         base = flat[pl.ds(j, K, stride=RUN), :]
         cols = slice(j * 128, (j + 1) * 128)
@@ -336,6 +349,8 @@
             pltpu.VMEM((K, K), jnp.bfloat16),
             pltpu.VMEM((OWNERS, FIRST_ROWS + 8 * PIECES, 128), jnp.bfloat16),
             pltpu.VMEM((OWNERS, LOCAL * REST, 128), jnp.bfloat16),
+            pltpu.VMEM((K, NB), jnp.float32),
+            pltpu.VMEM((K, NB), jnp.float32),
             pltpu.VMEM((K * RUN, 128), jnp.float32),
             pltpu.VMEM((K, points), jnp.float32),
             pltpu.VMEM((K, points), jnp.bfloat16),

time: 135 us -> 126 us (0.933)
  Pallas kernels: 38.2 us -> 29.3 us
    pallas_call x1, Pallas kernels: 16.8 us -> 9.22 us  [propagate(): pl.pallas_call(propagate_kernel, in_specs=[pl.BlockSpec(memory_space=pltp...]
  transfers between devices with their start and end apart: 7 -> 7, of which waited for: 3 -> 3; matrix products, arithmetic and copies ran while one was open for 4% -> 4% of each run, Pallas kernels for 14% -> 9%
where the time goes in v3:
time: 126 us; the launch traced here: 124 us
  waiting for transfers between devices  39 us (31%)
  starting transfers between devices  35 us (28%)
  Pallas kernels  29.3 us (23%)
  blocking collectives  12.3 us (10%)
  other arithmetic  5.36 us (4%)
  local copies, waits for them, and re-layouts  2.26 us (2%)
    all_to_all x1, waiting for transfers between devices, window(): received = lax.all_to_all(sent, 'comp', 0, 0, tiled=True)  22.4 us
    all_to_all x1, waiting for transfers between devices, window(): first = lax.all_to_all(first, 'comp', 0, 0, tiled=True)  16 us
    pallas_call x1, Pallas kernels, sources(): pl.pallas_call(source_kernel, in_specs=[vmem, hbm, vmem, vmem, hbm], out_...  13.8 us
    all_gather x1, blocking collectives, window(): lax.all_gather(jnp.concatenate([wide[:3], wide_cells], axis=0), 'band', a...  12.3 us
    pallas_call x1, Pallas kernels, propagate(): pl.pallas_call(propagate_kernel, in_specs=[pl.BlockSpec(memory_space=pltp...  9.22 us
    all_to_all x1, starting transfers between devices, window(): first = lax.all_to_all(first, 'comp', 0, 0, tiled=True)  8.5 us
    ppermute x2, starting transfers between devices, from_neighbours(): after = lax.ppermute(low, axis, [((i + 1) % count, i) for i in range(ends)])  8.23 us
    all_to_all x1, starting transfers between devices, window(): received = lax.all_to_all(sent, 'comp', 0, 0, tiled=True)  7.3 us
  transfers between devices with their start and end apart: 7, of which 3 were waited for; matrix products, arithmetic and copies ran while one was open for 4% of the time, Pallas kernels for 9%

profile of v3, /device:TPU:6, one launch (start us, length us, event | category | flops | bytes accessed | tf_op | source)
XLA Modules:
  0.0 124.4 jit_solution(16787948582955048830)
XLA Ops:
  0.6 0.9 fusion.164
  1.6 1.1 fusion.163
  2.7 1.7 %collective-permute-start = (f32[37,4,256]{2,1,0:T(4,128)S(1)}, f32[37,4,256]{2,1,0:T(4,128)S(1)}, u32[]{:S(2)}, u32[]{:S(2)}) collective-permute-start(f32[37,4,256]{2,1,0:T(4,128)S(1)} %pad_maximum_fusion), channel_id=1, source_target_pairs={{0,1},{1,2},{2,3},{4,5},{5,6},{6,7},{8,9},{9,10},{10,11},{12,13},{... | collective-permute-start | bytes 454664 | tf_op jit(solution)/shard_map/ppermute | solution.py:501
  4.5 1.3 %collective-permute-start.1 = (f32[37,4,256]{2,1,0:T(4,128)S(1)}, f32[37,4,256]{2,1,0:T(4,128)S(1)}, u32[]{:S(2)}, u32[]{:S(2)}) collective-permute-start(f32[37,4,256]{2,1,0:T(4,128)S(1)} %pad_maximum_fusion.1), channel_id=1, source_target_pairs={{1,0},{2,1},{3,2},{5,4},{6,5},{7,6},{9,8},{10,9},{11,10},{13,12},{... | collective-permute-start | bytes 454664 | tf_op jit(solution)/shard_map/ppermute | solution.py:502
  5.8 0.7 convert_element_type.140
  6.5 0.9 slice_maximum_fusion
  7.4 3.5 %collective-permute-start.2 = (f32[6,8,16]{2,1,0:T(8,128)S(1)}, f32[6,8,16]{2,1,0:T(8,128)S(1)}, u32[]{:S(2)}, u32[]{:S(2)}) collective-permute-start(f32[6,8,16]{2,1,0:T(8,128)S(1)} %get-tuple-element.45), channel_id=1, source_target_pairs={{0,4},{4,8},{8,12},{12,16},{16,20},{20,24},{24,28},{28,32},{32,36}... | collective-permute-start | bytes 9224 | tf_op jit(solution)/shard_map/ppermute | solution.py:501
  10.9 6.9 %collective-permute-start.3 = (f32[6,8,16]{2,1,0:T(8,128)S(1)}, f32[6,8,16]{2,1,0:T(8,128)S(1)}, u32[]{:S(2)}, u32[]{:S(2)}) collective-permute-start(f32[6,8,16]{2,1,0:T(8,128)S(1)} %get-tuple-element.46), channel_id=1, source_target_pairs={{4,0},{8,4},{12,8},{16,12},{20,16},{24,20},{28,24},{32,28},{36,32}... | collective-permute-start | bytes 9224 | tf_op jit(solution)/shard_map/ppermute | solution.py:502
  17.8 0.1 sine_multiply_fusion
  17.9 0.0 collective-permute-done.top_ref
  17.9 0.0 collective-permute-done.1.bot_ref
  17.9 9.2 %propagate.1 = (f32[3456,128]{1,0:T(8,128)}, f32[3456,128]{1,0:T(8,128)}, bf16[32,216,128]{2,1,0:T(8,128)(2,1)}) custom-call(f32[2,36]{1,0:T(2,128)S(1)} %pad_maximum_fusion.4.speeds, f32[36,96,256]{2,1,0:T(8,128)} %spec_hbm.1, f32[37,4,256]{2,1,0:T(4,128)S(1)} %collective-permute-done.top_ref, f32[37,4,256]{2,1,0:T(4,128)S(1)} %collective-permute-done.1.bot_ref, ...), custom_call_target="tpu_custom_call" | custom-call | tf_op jit(solution)/shard_map/propagate/pallas_call | solution.py:189
  27.1 0.0 copy-start.3
  27.1 0.0 copy-start.1
  27.2 7.3 %all-to-all-start = ((bf16[32,216,128]{2,1,0:T(8,128)(2,1)}), bf16[32,216,128]{2,1,0:T(8,128)(2,1)S(1)}, u32[]{:S(2)}, u32[]{:S(2)}) async-start(bf16[32,216,128]{2,1,0:T(8,128)(2,1)} %get-tuple-element.7), calls=%async_computation | async-start | bytes 3538944 | tf_op jit(solution)/shard_map/all_to_all | solution.py:556
  34.5 0.2 multiply_add_fusion.1
  34.6 0.1 pad.121.clone
  34.7 0.2 multiply_add_fusion
  34.9 0.1 maximum_maximum_fusion.coef_ref
  35.0 0.0 collective-permute-done.2
  35.0 0.1 reshape.245
  35.1 0.0 collective-permute-done.3
  35.1 0.1 reshape.246
  35.2 0.0 copy-done.3
  35.2 0.6 reshape.244.points_ref
  35.8 22.4 %all-to-all-done = bf16[32,216,128]{2,1,0:T(8,128)(2,1)S(1)} async-done(((bf16[32,216,128]{2,1,0:T(8,128)(2,1)}), bf16[32,216,128]{2,1,0:T(8,128)(2,1)S(1)}, u32[]{:S(2)}, u32[]{:S(2)}) %all-to-all-start) | async-done | bytes 1769504 | tf_op jit(solution)/shard_map/all_to_all | solution.py:556
  58.2 0.0 copy-done.1
  58.2 13.8 %sources.1 = (bf16[32,120,128]{2,1,0:T(8,128)(2,1)}, bf16[32,144,128]{2,1,0:T(8,128)(2,1)}) custom-call(bf16[6912,128]{1,0:T(8,128)(2,1)S(1)} %bitcast.27, bf16[1152,1152]{1,0:T(8,128)(2,1)} %quad_hbm.1, f32[9,128]{1,0:T(8,128)S(1)} %bitcast.28, bf16[16,1152]{1,0:T(8,128)(2,1)S(1)} %maximum_maximum_fusion.coef_ref, s32[30,128]{1,0:T(8,128)} %reshape.244.points_ref), custom_call_target="tpu_custom_call" | custom-call | tf_op jit(solution)/shard_map/sources/pallas_call | solution.py:340
  72.1 0.0 copy-start
  72.1 8.5 %all-to-all-start.1 = ((bf16[32,120,128]{2,1,0:T(8,128)(2,1)}), bf16[32,120,128]{2,1,0:T(8,128)(2,1)S(1)}, u32[]{:S(2)}, u32[]{:S(2)}) async-start(bf16[32,120,128]{2,1,0:T(8,128)(2,1)} %get-tuple-element.8), calls=%async_computation.1 | async-start | bytes 1966080 | tf_op jit(solution)/shard_map/all_to_all | solution.py:577
  80.6 0.0 copy-start.2
  80.6 16.0 %all-to-all-done.1.first_ref = bf16[32,120,128]{2,1,0:T(8,128)(2,1)S(1)} async-done(((bf16[32,120,128]{2,1,0:T(8,128)(2,1)}), bf16[32,120,128]{2,1,0:T(8,128)(2,1)S(1)}, u32[]{:S(2)}, u32[]{:S(2)}) %all-to-all-start.1) | async-done | bytes 983072 | tf_op jit(solution)/shard_map/all_to_all | solution.py:577
  96.6 5.8 %all-to-all-start.2 = ((bf16[32,144,128]{2,1,0:T(8,128)(2,1)}), bf16[32,144,128]{2,1,0:T(8,128)(2,1)S(1)}, u32[]{:S(2)}, u32[]{:S(2)}) async-start(bf16[32,144,128]{2,1,0:T(8,128)(2,1)} %get-tuple-element.9), calls=%async_computation.2 | async-start | bytes 2359296 | tf_op jit(solution)/shard_map/all_to_all | solution.py:578
  102.4 0.0 copy-done
  102.4 2.3 %pick.1 = f32[3,10,128]{2,1,0:T(8,128)S(1)} custom-call(bf16[32,120,128]{2,1,0:T(8,128)(2,1)S(1)} %all-to-all-done.1.first_ref, s32[30,128]{1,0:T(8,128)S(1)} %copy-done), custom_call_target="tpu_custom_call" | custom-call | tf_op jit(solution)/shard_map/pick/pallas_call | solution.py:403
  104.8 0.1 reshape_squeeze.6
  104.8 0.1 reshape_squeeze.7
  104.9 0.0 copy-done.2
  104.9 0.1 fusion
  105.0 12.3 %all_gather.3 = f32[6,32,160]{2,1,0:T(8,128)S(1)} all-gather(f32[6,8,160]{2,1,0:T(8,128)S(1)} %fusion), channel_id=1, replica_groups=mesh['comp'=32,'band'=4] {'band'}, dimensions={1}, use_global_device_ids=true | all-gather | bytes 153600 | tf_op jit(solution)/shard_map/all_gather | solution.py:584
  117.3 0.1 fusion.5
  117.4 0.1 fusion.10
  117.5 0.1 fusion.63
  117.7 0.1 fusion.16
  117.8 0.1 fusion.73
  117.9 0.1 fusion.22
  118.0 0.1 fusion.83
  118.1 0.1 fusion.28
  118.2 0.1 fusion.93
  118.2 0.1 fusion.34
  118.3 0.1 fusion.103
  118.4 0.1 fusion.40
  118.5 0.1 fusion.113
  118.6 0.1 fusion.46
  118.7 0.1 fusion.123
  118.8 0.1 fusion.52
  118.9 0.1 fusion.135
  119.0 0.7 fusion.145
  119.7 0.6 all-to-all-done.2.rest_ref
  120.3 3.9 %finish.1 = f32[36,96,256]{2,1,0:T(8,128)} custom-call(bf16[32,120,128]{2,1,0:T(8,128)(2,1)S(1)} %all-to-all-done.1.first_ref, bf16[32,144,128]{2,1,0:T(8,128)(2,1)S(1)} %all-to-all-done.2.rest_ref, f32[3456,128]{1,0:T(8,128)} %get-tuple-element.10.prop0_hbm, f32[3456,128]{1,0:T(8,128)} %get-tuple-element.11.prop1_hbm), custom_call_target="tpu_custom_call" | custom-call | tf_op jit(solution)/shard_map/finish/pallas_call | solution.py:479
  (15 shorter events, 0.2 us)
Async XLA Ops:
  2.7 15.2 %collective-permute-start = (f32[37,4,256]{2,1,0:T(4,128)S(1)}, f32[37,4,256]{2,1,0:T(4,128)S(1)}, u32[]{:S(2)}, u32[]{:S(2)}) collective-permute-start(f32[37,4,256]{2,1,0:T(4,128)S(1)} %pad_maximum_fusion), channel_id=1, source_target_pairs={{0,1},{1,2},{2,3},{4,5},{5,6},{6,7},{8,9},{9,10},{10,11},{12,13},{... | collective-permute-start | bytes 454664 | tf_op jit(solution)/shard_map/ppermute | solution.py:501
  4.5 13.4 %collective-permute-start.1 = (f32[37,4,256]{2,1,0:T(4,128)S(1)}, f32[37,4,256]{2,1,0:T(4,128)S(1)}, u32[]{:S(2)}, u32[]{:S(2)}) collective-permute-start(f32[37,4,256]{2,1,0:T(4,128)S(1)} %pad_maximum_fusion.1), channel_id=1, source_target_pairs={{1,0},{2,1},{3,2},{5,4},{6,5},{7,6},{9,8},{10,9},{11,10},{13,12},{... | collective-permute-start | bytes 454664 | tf_op jit(solution)/shard_map/ppermute | solution.py:502
  7.4 27.6 %collective-permute-start.2 = (f32[6,8,16]{2,1,0:T(8,128)S(1)}, f32[6,8,16]{2,1,0:T(8,128)S(1)}, u32[]{:S(2)}, u32[]{:S(2)}) collective-permute-start(f32[6,8,16]{2,1,0:T(8,128)S(1)} %get-tuple-element.45), channel_id=1, source_target_pairs={{0,4},{4,8},{8,12},{12,16},{16,20},{20,24},{24,28},{28,32},{32,36}... | collective-permute-start | bytes 9224 | tf_op jit(solution)/shard_map/ppermute | solution.py:501
  10.9 24.3 %collective-permute-start.3 = (f32[6,8,16]{2,1,0:T(8,128)S(1)}, f32[6,8,16]{2,1,0:T(8,128)S(1)}, u32[]{:S(2)}, u32[]{:S(2)}) collective-permute-start(f32[6,8,16]{2,1,0:T(8,128)S(1)} %get-tuple-element.46), channel_id=1, source_target_pairs={{4,0},{8,4},{12,8},{16,12},{20,16},{24,20},{28,24},{32,28},{36,32}... | collective-permute-start | bytes 9224 | tf_op jit(solution)/shard_map/ppermute | solution.py:502
  27.1 8.1 %copy-start.3 = (s32[3,8,128]{2,1,0:T(8,128)S(1)}, s32[3,8,128]{2,1,0:T(8,128)}, u32[]{:S(2)}) copy-start(s32[3,8,128]{2,1,0:T(8,128)} %param.11) | copy-start | bytes 36868
  27.1 31.1 %copy-start.1 = (f32[1152]{0:T(1024)S(1)}, f32[1152]{0:T(1024)}, u32[]{:S(2)}) copy-start(f32[1152]{0:T(1024)} %param.9) | copy-start | bytes 13828
  27.2 31.1 %all-to-all-start = ((bf16[32,216,128]{2,1,0:T(8,128)(2,1)}), bf16[32,216,128]{2,1,0:T(8,128)(2,1)S(1)}, u32[]{:S(2)}, u32[]{:S(2)}) async-start(bf16[32,216,128]{2,1,0:T(8,128)(2,1)} %get-tuple-element.7), calls=%async_computation | async-start | bytes 3538944 | tf_op jit(solution)/shard_map/all_to_all | solution.py:556
  72.1 30.3 %copy-start = (s32[30,128]{1,0:T(8,128)S(1)}, s32[30,128]{1,0:T(8,128)}, u32[]{:S(2)}) copy-start(s32[30,128]{1,0:T(8,128)} %reshape.244.points_ref) | copy-start | bytes 46084
  72.1 24.5 %all-to-all-start.1 = ((bf16[32,120,128]{2,1,0:T(8,128)(2,1)}), bf16[32,120,128]{2,1,0:T(8,128)(2,1)S(1)}, u32[]{:S(2)}, u32[]{:S(2)}) async-start(bf16[32,120,128]{2,1,0:T(8,128)(2,1)} %get-tuple-element.8), calls=%async_computation.1 | async-start | bytes 1966080 | tf_op jit(solution)/shard_map/all_to_all | solution.py:577
  80.6 24.3 %copy-start.2 = (f32[3,8,128]{2,1,0:T(8,128)S(1)}, f32[3,8,128]{2,1,0:T(8,128)}, u32[]{:S(2)}) copy-start(f32[3,8,128]{2,1,0:T(8,128)} %param.10) | copy-start | bytes 36868
  96.6 23.7 %all-to-all-start.2 = ((bf16[32,144,128]{2,1,0:T(8,128)(2,1)}), bf16[32,144,128]{2,1,0:T(8,128)(2,1)S(1)}, u32[]{:S(2)}, u32[]{:S(2)}) async-start(bf16[32,144,128]{2,1,0:T(8,128)(2,1)} %get-tuple-element.9), calls=%async_computation.2 | async-start | bytes 2359296 | tf_op jit(solution)/shard_map/all_to_all | solution.py:578

commit v4 on v3

--- a/solution.py
+++ b/solution.py
@@ -213,54 +213,52 @@
 MB = 576
 EB = 64
 NB = 256
-FIRST = 2
-FIRST_ROWS = FIRST * LOCAL
-REST = RUN - FIRST
+OWN_ROWS = RUN * LOCAL
 PIECES = 6
 BLOCKS = RUN * 128 // NB
+BACK_ROWS = OWN_ROWS + 8 * PIECES
 
 
 def source_kernel(
-    recv_ref, quad_hbm, diss_ref, coef_ref, points_ref, first_hbm, rest_hbm,
-    quad_ref, first_ref, rest_ref, prod_a, prod_b, flat, cur, xa, xb, rate, level, flat_first, flat_rest,
-    quad_sem, out_sems,
+    recv_ref, quad_hbm, diss_ref, coef_ref, points_ref, back_hbm,
+    quad_ref, back_ref, prod_a, prod_b, flat, cur, xa, xb, rate, level, quad_sems, out_sem,
 ):
-    chunk = K
-    fetch = pltpu.make_async_copy(quad_hbm, quad_ref, quad_sem)
-    fetch.start()
-
-    def give(o):
-        return (
-            pltpu.make_async_copy(first_ref.at[o], first_hbm.at[o], out_sems.at[0, o]),
-            pltpu.make_async_copy(rest_ref.at[o], rest_hbm.at[o], out_sems.at[1, o]),
-        )
+    halves = K // MB
+
+    def fetch(m):
+        part = pl.ds(m * MB, MB)
+        return pltpu.make_async_copy(quad_hbm.at[part], quad_ref.at[part], quad_sems.at[m])
+
+    for m in range(halves):
+        fetch(m).start()
 
     def widen(i, carry):
-        flat[pl.ds(i * chunk, chunk), :] = recv_ref[pl.ds(i * chunk, chunk), :].astype(jnp.float32)
+        flat[pl.ds(i * K, K), :] = recv_ref[pl.ds(i * K, K), :].astype(jnp.float32)
         return carry
 
     lax.fori_loop(0, RUN, widen, 0)
     for i in range(K // 128):
         rate[i * 128:(i + 1) * 128, :] = jnp.broadcast_to(diss_ref[i:i + 1, :], (128, 128)).T
-    for j in range(RUN):
-        base = flat[pl.ds(j, K, stride=RUN), :]
-        cols = slice(j * 128, (j + 1) * 128)
-        cur[:, cols] = base
-        xa[:, cols] = base.astype(jnp.bfloat16)
-        level[:, cols] = jnp.sum(base, axis=0, keepdims=True)
-
     coef = coef_ref[...]
-    stress = [
-        jnp.dot(coef, xa[:, n * NB:(n + 1) * NB], preferred_element_type=jnp.float32)
-        for n in range(BLOCKS)
-    ]
-
-    fetch.wait()
+    each_block = NB // 128
+    stress = []
+    rows_of = [[], [], []]
+
+    def prepare(n):
+        for j in range(n * each_block, (n + 1) * each_block):
+            base = flat[pl.ds(j, K, stride=RUN), :]
+            cols = slice(j * 128, (j + 1) * 128)
+            cur[:, cols] = base
+            xa[:, cols] = base.astype(jnp.bfloat16)
+            level[:, cols] = jnp.sum(base, axis=0, keepdims=True)
+        stress.append(
+            jnp.dot(coef, xa[:, n * NB:(n + 1) * NB], preferred_element_type=jnp.float32)
+        )
 
     def multiply(s, n):
         held = (prod_a, prod_b)[(s * BLOCKS + n) % 2]
         old = (xa, xb)[s % 2]
-        for m in range(K // MB):
+        for m in range(halves):
             rows = slice(m * MB, (m + 1) * MB)
             held[rows, :] = jnp.dot(
                 quad_ref[rows, :], old[:, n * NB:(n + 1) * NB], preferred_element_type=jnp.float32
@@ -274,7 +272,7 @@
         sums = jnp.zeros((8, NB), jnp.float32)
         for m in range(K // EB):
             rows = slice(m * EB, (m + 1) * EB)
-            each = jnp.concatenate([rate[rows, :]] * (NB // 128), axis=1)
+            each = jnp.concatenate([rate[rows, :]] * each_block, axis=1)
             now = cur[rows, cols]
             now = now + step_source * now * (held[rows, :] - each * mean)
             cur[rows, cols] = now
@@ -284,53 +282,49 @@
         if s + 1 < SRC_STEPS:
             level[:, cols] = jnp.sum(sums, axis=0, keepdims=True)
 
+    def conclude(n):
+        for j in range(n * each_block, (n + 1) * each_block):
+            base = flat[pl.ds(j, K, stride=RUN), :]
+            cols = slice(j * 128, (j + 1) * 128)
+            gain = (cur[:, cols] - base).astype(jnp.bfloat16)
+            xa[:, cols] = gain
+            flat[pl.ds(j, K, stride=RUN), :] = gain.astype(jnp.float32)
+        both = stress[n] + jnp.dot(
+            coef, xa[:, n * NB:(n + 1) * NB], preferred_element_type=jnp.float32
+        )
+        for c in range(3):
+            row = (both[c:c + 1] + both[3 + c:4 + c] + both[6 + c:7 + c]) * (1.0 / K)
+            rows_of[c] += [row[:, i * 128:(i + 1) * 128] for i in range(each_block)]
+
+    for m in range(halves):
+        fetch(m).wait()
+    prepare(0)
     turns = [(s, n) for s in range(SRC_STEPS) for n in range(BLOCKS)]
-    for i, turn in enumerate(turns):
-        multiply(*turn)
+    for i, (s, n) in enumerate(turns):
+        multiply(s, n)
+        if s == 0 and n + 1 < BLOCKS:
+            prepare(n + 1)
         if i > 0:
             update(*turns[i - 1])
+        if s == SRC_STEPS - 1 and n > 0:
+            conclude(n - 1)
     update(*turns[-1])
-    for j in range(RUN):
-        base = flat[pl.ds(j, K, stride=RUN), :]
-        cols = slice(j * 128, (j + 1) * 128)
-        gain = (cur[:, cols] - base).astype(jnp.bfloat16)
-        xb[:, cols] = gain
-        if j < FIRST:
-            flat_first[pl.ds(j, K, stride=FIRST), :] = gain.astype(jnp.float32)
-        else:
-            flat_rest[pl.ds(j - FIRST, K, stride=REST), :] = gain.astype(jnp.float32)
-    parts = []
-    for n in range(BLOCKS):
-        both = stress[n] + jnp.dot(
-            coef, xb[:, n * NB:(n + 1) * NB], preferred_element_type=jnp.float32
-        )
-        rows = [both[c:c + 1] + both[3 + c:4 + c] + both[6 + c:7 + c] for c in range(3)]
-        parts.append(jnp.concatenate(rows, axis=0) * (1.0 / K))
+    conclude(BLOCKS - 1)
     pieces = []
     for c in range(3):
-        rows = [parts[j * 128 // NB][c:c + 1, j * 128 % NB:j * 128 % NB + 128] for j in range(RUN)]
-        whole = jnp.concatenate(rows + [jnp.zeros((8 - RUN, 128), jnp.float32)], axis=0)
+        whole = jnp.concatenate(rows_of[c] + [jnp.zeros((8 - RUN, 128), jnp.float32)], axis=0)
         high = whole.astype(jnp.bfloat16).astype(jnp.float32)
         pieces += [high, whole - high]
     shared = jnp.concatenate(pieces, axis=0).astype(jnp.bfloat16)
 
     def narrow(o, carry):
-        gain = flat_first[pl.ds(o * FIRST_ROWS, FIRST_ROWS), :].astype(jnp.bfloat16)
-        first_ref[o, 0:FIRST_ROWS, :] = gain
-        first_ref[o, FIRST_ROWS:FIRST_ROWS + 8 * PIECES, :] = shared
-        rows = LOCAL * REST
-        rest_ref[o] = flat_rest[pl.ds(o * rows, rows), :].astype(jnp.bfloat16)
-        for copy in give(o):
-            copy.start()
-        return carry
-
-    def settle(o, carry):
-        for copy in give(o):
-            copy.wait()
+        back_ref[o, 0:OWN_ROWS, :] = flat[pl.ds(o * OWN_ROWS, OWN_ROWS), :].astype(jnp.bfloat16)
+        back_ref[o, OWN_ROWS:BACK_ROWS, :] = shared
+        pltpu.make_async_copy(back_ref.at[o], back_hbm.at[o], out_sem).start()
         return carry
 
     lax.fori_loop(0, OWNERS, narrow, 0)
-    lax.fori_loop(0, OWNERS, settle, 0)
+    pltpu.make_async_copy(back_ref, back_hbm, out_sem).wait()
 
 
 def sources(received, quad_matrix, rates, coef, points_list):
@@ -340,15 +334,11 @@
     return pl.pallas_call(
         source_kernel,
         in_specs=[vmem, hbm, vmem, vmem, hbm],
-        out_specs=[hbm] * 2,
-        out_shape=[
-            pltpu.HBM((OWNERS, FIRST_ROWS + 8 * PIECES, 128), jnp.bfloat16),
-            pltpu.HBM((OWNERS, LOCAL * REST, 128), jnp.bfloat16),
-        ],
+        out_specs=hbm,
+        out_shape=pltpu.HBM((OWNERS, BACK_ROWS, 128), jnp.bfloat16),
         scratch_shapes=[
             pltpu.VMEM((K, K), jnp.bfloat16),
-            pltpu.VMEM((OWNERS, FIRST_ROWS + 8 * PIECES, 128), jnp.bfloat16),
-            pltpu.VMEM((OWNERS, LOCAL * REST, 128), jnp.bfloat16),
+            pltpu.VMEM((OWNERS, BACK_ROWS, 128), jnp.bfloat16),
             pltpu.VMEM((K, NB), jnp.float32),
             pltpu.VMEM((K, NB), jnp.float32),
             pltpu.VMEM((K * RUN, 128), jnp.float32),
@@ -357,21 +347,19 @@
             pltpu.VMEM((K, points), jnp.bfloat16),
             pltpu.VMEM((K, 128), jnp.float32),
             pltpu.VMEM((1, points), jnp.float32),
-            pltpu.VMEM((K * FIRST, 128), jnp.float32),
-            pltpu.VMEM((K * REST, 128), jnp.float32),
+            pltpu.SemaphoreType.DMA((K // MB,)),
             pltpu.SemaphoreType.DMA(()),
-            pltpu.SemaphoreType.DMA((2, OWNERS)),
         ],
         compiler_params=pltpu.CompilerParams(vmem_limit_bytes=30 << 20),
         name="sources",
     )(in_vmem(received), in_hbm(quad_matrix), in_vmem(rates), in_vmem(coef), in_hbm(points_list))
 
 
-def pick_kernel(first_ref, points_ref, out_ref):
+def pick_kernel(back_ref, points_ref, out_ref):
     pieces = []
     for i in range(PIECES):
-        at = FIRST_ROWS + 8 * i
-        rows = first_ref[:, at:at + 8, :].astype(jnp.float32).reshape(OWNERS * 8, 128)
+        at = OWN_ROWS + 8 * i
+        rows = back_ref[:, at:at + 8, :].astype(jnp.float32).reshape(OWNERS * 8, 128)
         pieces.append(rows.T.astype(jnp.bfloat16))
     table = jnp.concatenate(pieces, axis=0)
     slot = lax.broadcasted_iota(jnp.int32, (OWNERS * 8, 128), 0)
@@ -398,7 +386,7 @@
             out_ref[c, t:t + 1, :] = jnp.sum(acc, axis=0, keepdims=True)
 
 
-def pick(first, points):
+def pick(back, points):
     vmem = pl.BlockSpec(memory_space=pltpu.VMEM)
     return pl.pallas_call(
         pick_kernel,
@@ -407,12 +395,11 @@
         out_shape=pltpu.VMEM((3, TILES, 128), jnp.float32),
         compiler_params=pltpu.CompilerParams(vmem_limit_bytes=10 << 20),
         name="pick",
-    )(in_vmem(first), in_vmem(points))
+    )(in_vmem(back), in_vmem(points))
 
 
 def finish_kernel(
-    first_ref, rest_ref, prop0_hbm, prop1_hbm, out_hbm,
-    prop0, prop1, spread_first, spread_rest, out, sems, keep_sems,
+    back_ref, prop0_hbm, prop1_hbm, out_hbm, prop0, prop1, wide, out, sems, keep_sems,
 ):
     def keep(i):
         part = pl.ds(i * KB * ROWS, KB * ROWS)
@@ -430,17 +417,11 @@
 
     def spread(g, carry):
         for h in range(2):
-            o = h * GROUP + g
-            spread_first[h, pl.ds(g, FIRST_ROWS, stride=GROUP), :] = first_ref[
-                o, 0:FIRST_ROWS, :
-            ].astype(jnp.float32)
-            spread_rest[h, pl.ds(g, LOCAL * REST, stride=GROUP), :] = rest_ref[o].astype(
-                jnp.float32
-            )
+            gain = back_ref[h * GROUP + g, 0:OWN_ROWS, :].astype(jnp.float32)
+            wide[h, pl.ds(g, OWN_ROWS, stride=GROUP), :] = gain
         return carry
 
     lax.fori_loop(0, GROUP, spread, 0)
-    cut = FIRST * GROUP
 
     def copy(i):
         part = pl.ds(i * KB, KB)
@@ -452,14 +433,8 @@
         for kk in range(KB):
             k = i * KB + kk
             for h, prop in enumerate((prop0, prop1)):
-                cols = slice(h * 128, (h + 1) * 128)
-                out[k, 0:cut, cols] = (
-                    prop[pl.ds(k * ROWS, cut), :] + spread_first[h, pl.ds(k * cut, cut), :]
-                )
-                tail = ROWS - cut
-                out[k, cut:ROWS, cols] = (
-                    prop[pl.ds(k * ROWS + cut, tail), :] + spread_rest[h, pl.ds(k * tail, tail), :]
-                )
+                rows = pl.ds(k * ROWS, ROWS)
+                out[k, :, h * 128:(h + 1) * 128] = prop[rows, :] + wide[h, rows, :]
         copy(i).start()
         return carry
 
@@ -472,27 +447,26 @@
     lax.fori_loop(0, LOCAL // KB, settle, 0)
 
 
-def finish(first, rest, prop0, prop1):
+def finish(back, prop0, prop1):
     vmem = pl.BlockSpec(memory_space=pltpu.VMEM)
     hbm = pl.BlockSpec(memory_space=pltpu.HBM)
     shape = (LOCAL, ROWS, 256)
     return pl.pallas_call(
         finish_kernel,
-        in_specs=[vmem, vmem, hbm, hbm],
+        in_specs=[vmem, hbm, hbm],
         out_specs=hbm,
         out_shape=pltpu.HBM(shape, jnp.float32),
         scratch_shapes=[
             pltpu.VMEM((LOCAL * ROWS, 128), jnp.float32),
             pltpu.VMEM((LOCAL * ROWS, 128), jnp.float32),
-            pltpu.VMEM((2, LOCAL * FIRST * GROUP, 128), jnp.float32),
-            pltpu.VMEM((2, LOCAL * REST * GROUP, 128), jnp.float32),
+            pltpu.VMEM((2, LOCAL * ROWS, 128), jnp.float32),
             pltpu.VMEM(shape, jnp.float32),
             pltpu.SemaphoreType.DMA((LOCAL // KB,)),
             pltpu.SemaphoreType.DMA((2, LOCAL // KB)),
         ],
         compiler_params=pltpu.CompilerParams(vmem_limit_bytes=16 << 20),
         name="finish",
-    )(in_vmem(first), in_vmem(rest), in_hbm(prop0), in_hbm(prop1))
+    )(in_vmem(back), in_hbm(prop0), in_hbm(prop1))
 
 
 def from_neighbours(low, high, axis):
@@ -503,45 +477,68 @@
     return before, after
 
 
-def diff_rows(extended):
-    return 0.5 * (extended[2:, 1:-1] - extended[:-2, 1:-1])
-
-
-def diff_cols(extended):
-    return 0.5 * (extended[1:-1, 2:] - extended[1:-1, :-2])
-
-
-def shallow_water(wide_state, wide_stress, tile_cols, tile_rows):
-    groups = lax.axis_size("comp")
-    wide_cols = wide_state.shape[2]
-    global_col = (
-        lax.axis_index("comp") * tile_cols - MARGIN + jnp.arange(wide_cols, dtype=jnp.int32)
-    )
-    within = (global_col >= 0) & (global_col < tile_cols * groups)
-    inside = within.astype(jnp.float32)[None, :]
-    rimmed = jnp.pad(jnp.where(within, wide_stress, 0.0), ((0, 0), (1, 1), (1, 1)))
-    force_down = -(diff_rows(rimmed[0]) + diff_cols(rimmed[1]))
-    force_across = -(diff_rows(rimmed[1]) + diff_cols(rimmed[2]))
-    height, flow_down, flow_across = wide_state
+WIDE = 256
+
+
+def water_kernel(place, own_ref, one_ref, two_ref, three_ref, out_ref, whole, result):
+    bands = 4
+    tile = own_ref.shape[1]
+    width = own_ref.shape[2]
+    own_cols = width - 2 * MARGIN
+    band = place[0]
+    whole[...] = jnp.zeros_like(whole)
+    for d, ref in enumerate((own_ref, one_ref, two_ref, three_ref)):
+        row = pl.multiple_of((band ^ d) * tile, tile)
+        whole[:, pl.ds(row, tile), 0:width] = ref[...]
+    shape = (bands * tile, WIDE)
+    lane = lax.broadcasted_iota(jnp.int32, shape, 1)
+    line = lax.broadcasted_iota(jnp.int32, shape, 0)
+    col = place[1] * own_cols - MARGIN + lane
+    inside = (col >= 0) & (col < place[2]) & (lane < width)
+    first = line == 0
+    last = line == shape[0] - 1
+
+    def dx(f):
+        after = jnp.where(last, 0.0, pltpu.roll(f, shape[0] - 1, 0))
+        before = jnp.where(first, 0.0, pltpu.roll(f, 1, 0))
+        return 0.5 * (after - before)
+
+    def dy(f):
+        return 0.5 * (pltpu.roll(f, WIDE - 1, 1) - pltpu.roll(f, 1, 1))
+
+    sxx, sxy, syy = (jnp.where(inside, whole[3 + c], 0.0) for c in range(3))
+    force_down = -forcing_gain * (dx(sxx) + dy(sxy))
+    force_across = -forcing_gain * (dx(sxy) + dy(syy))
+    height, down, across = (whole[c] for c in range(3))
     for _ in range(SW_STEPS):
-        down_ext = jnp.pad(flow_down, 1)
-        across_ext = jnp.pad(flow_across, 1)
-        height = (height - wave_speed * (diff_rows(down_ext) + diff_cols(across_ext))) * inside
-        height_ext = jnp.pad(height, 1)
-        flow_down = (
-            (1.0 - friction) * flow_down
-            - wave_speed * diff_rows(height_ext)
-            + forcing_gain * force_down
-        ) * inside
-        flow_across = (
-            (1.0 - friction) * flow_across
-            - wave_speed * diff_cols(height_ext)
-            + forcing_gain * force_across
-        ) * inside
-    stacked = jnp.stack([height, flow_down, flow_across])
-    row_start = lax.axis_index("band") * tile_rows
-    own_rows = lax.dynamic_slice_in_dim(stacked, row_start, tile_rows, 1)
-    return own_rows[:, :, MARGIN:MARGIN + tile_cols]
+        height = jnp.where(inside, height - wave_speed * (dx(down) + dy(across)), 0.0)
+        down = jnp.where(
+            inside, (1.0 - friction) * down - wave_speed * dx(height) + force_down, 0.0
+        )
+        across = jnp.where(
+            inside, (1.0 - friction) * across - wave_speed * dy(height) + force_across, 0.0
+        )
+    for c, value in enumerate((height, down, across)):
+        result[c] = pltpu.roll(value, WIDE - MARGIN, 1)[:, :own_cols]
+        out_ref[c] = result[c, pl.ds(pl.multiple_of(band * tile, tile), tile), :]
+
+
+def shallow_water(place, tiles):
+    vmem = pl.BlockSpec(memory_space=pltpu.VMEM)
+    fields, rows, width = tiles[0].shape
+    own_cols = width - 2 * MARGIN
+    return pl.pallas_call(
+        water_kernel,
+        in_specs=[pl.BlockSpec(memory_space=pltpu.SMEM)] + [vmem] * 4,
+        out_specs=vmem,
+        out_shape=jax.ShapeDtypeStruct((3, rows, own_cols), jnp.float32),
+        scratch_shapes=[
+            pltpu.VMEM((fields, 4 * rows, WIDE), jnp.float32),
+            pltpu.VMEM((3, 4 * rows, own_cols), jnp.float32),
+        ],
+        compiler_params=pltpu.CompilerParams(vmem_limit_bytes=4 << 20),
+        name="water",
+    )(place, *map(in_vmem, tiles))
 
 
 def window(spectrum, wet_mask, quad_matrix, dissipation, circulation, source_points):
@@ -571,21 +568,25 @@
     coef_low = full_coef - coef_high - coef_mid
     spare = jnp.zeros((7, K), jnp.float32)
     coef = jnp.concatenate([coef_high, coef_mid, coef_low, spare]).astype(jnp.bfloat16)
-    first, rest = sources(
+    back = sources(
         received.reshape(K * RUN, 128), quad_matrix, dissipation.reshape(K // 128, 128), coef, points
     )
-    first = lax.all_to_all(first, "comp", 0, 0, tiled=True)
-    rest = lax.all_to_all(rest, "comp", 0, 0, tiled=True)
-    cells = pick(first, points)
+    back = lax.all_to_all(back, "comp", 0, 0, tiled=True)
+    cells = pick(back, points)
     own = cells[:, :tile_rows]
     left = cells[:, tile_rows].reshape(3, tile_rows, MARGIN)
     right = cells[:, tile_rows + 1].reshape(3, tile_rows, MARGIN)
     wide_cells = jnp.concatenate([left, own, right], axis=2)
-    everything = lax.all_gather(
-        jnp.concatenate([wide[:3], wide_cells], axis=0), "band", axis=1, tiled=True
+    tile = jnp.concatenate([wide[:3], wide_cells], axis=0)
+    bands = lax.axis_size("band")
+    tiles = [tile]
+    for d in range(1, bands):
+        tiles.append(lax.ppermute(tile, "band", [(i, i ^ d) for i in range(bands)]))
+    spectrum_out = finish(back, prop0, prop1)
+    place = jnp.stack(
+        [lax.axis_index("band"), lax.axis_index("comp"), tile_cols * lax.axis_size("comp")]
     )
-    circulation_out = shallow_water(everything[:3], everything[3:], tile_cols, tile_rows)
-    spectrum_out = finish(first, rest, prop0, prop1)
+    circulation_out = shallow_water(place.astype(jnp.int32), tiles)
     return spectrum_out, circulation_out
 
 

time: 126 us -> 125 us (level)
  the two profiles are of different devices: /device:TPU:6 before, /device:TPU:9 now
where the time goes in v4:
time: 125 us; the launch traced here: 124 us
  waiting for transfers between devices  54.9 us (44%)
  Pallas kernels  32.7 us (26%)
  starting transfers between devices  30.5 us (24%)
  other arithmetic  3.25 us (3%)
  local copies, waits for them, and re-layouts  2.15 us (2%)
    all_to_all x1, waiting for transfers between devices, window(): back = lax.all_to_all(back, 'comp', 0, 0, tiled=True)  30.3 us
    all_to_all x1, waiting for transfers between devices, window(): received = lax.all_to_all(sent, 'comp', 0, 0, tiled=True)  24.6 us
    pallas_call x1, Pallas kernels, sources(): pl.pallas_call(source_kernel, in_specs=[vmem, hbm, vmem, vmem, hbm], out_...  14.6 us
    all_to_all x1, starting transfers between devices, window(): received = lax.all_to_all(sent, 'comp', 0, 0, tiled=True)  11 us
    pallas_call x1, Pallas kernels, propagate(): pl.pallas_call(propagate_kernel, in_specs=[pl.BlockSpec(memory_space=pltp...  9.22 us
    ppermute x2, starting transfers between devices, from_neighbours(): lax.ppermute(high, axis, [(i, (i + 1) % count) for i in range(ends)])  7.3 us
    all_to_all x1, starting transfers between devices, window(): back = lax.all_to_all(back, 'comp', 0, 0, tiled=True)  4.21 us
    ppermute x3, starting transfers between devices, window(): tiles.append(lax.ppermute(tile, 'band', [(i, i ^ d) for i in range(bands)]))  4.02 us
  transfers between devices with their start and end apart: 9, of which 2 were waited for; matrix products, arithmetic and copies ran while one was open for 2% of the time, Pallas kernels for 11%

profile of v4, /device:TPU:9, one launch (start us, length us, event | category | flops | bytes accessed | tf_op | source)
XLA Modules:
  0.0 124.5 jit_solution(6032245613198783455)
XLA Ops:
  0.6 0.9 fusion.18
  1.6 1.1 fusion.17
  2.7 4.1 %collective-permute-start = (f32[37,4,256]{2,1,0:T(4,128)S(1)}, f32[37,4,256]{2,1,0:T(4,128)S(1)}, u32[]{:S(2)}, u32[]{:S(2)}) collective-permute-start(f32[37,4,256]{2,1,0:T(4,128)S(1)} %pad_maximum_fusion), channel_id=1, source_target_pairs={{0,1},{1,2},{2,3},{4,5},{5,6},{6,7},{8,9},{9,10},{10,11},{12,13},{... | collective-permute-start | bytes 454664 | tf_op jit(solution)/shard_map/ppermute | solution.py:475
  6.9 1.9 %collective-permute-start.1 = (f32[37,4,256]{2,1,0:T(4,128)S(1)}, f32[37,4,256]{2,1,0:T(4,128)S(1)}, u32[]{:S(2)}, u32[]{:S(2)}) collective-permute-start(f32[37,4,256]{2,1,0:T(4,128)S(1)} %pad_maximum_fusion.1), channel_id=1, source_target_pairs={{1,0},{2,1},{3,2},{5,4},{6,5},{7,6},{9,8},{10,9},{11,10},{13,12},{... | collective-permute-start | bytes 454664 | tf_op jit(solution)/shard_map/ppermute | solution.py:476
  8.8 0.7 convert_element_type.106
  9.5 0.9 slice_maximum_fusion
  10.4 3.2 %collective-permute-start.2 = (f32[6,8,16]{2,1,0:T(8,128)S(1)}, f32[6,8,16]{2,1,0:T(8,128)S(1)}, u32[]{:S(2)}, u32[]{:S(2)}) collective-permute-start(f32[6,8,16]{2,1,0:T(8,128)S(1)} %get-tuple-element.16), channel_id=1, source_target_pairs={{0,4},{4,8},{8,12},{12,16},{16,20},{20,24},{24,28},{28,32},{32,36}... | collective-permute-start | bytes 9224 | tf_op jit(solution)/shard_map/ppermute | solution.py:475
  13.6 2.1 %collective-permute-start.3 = (f32[6,8,16]{2,1,0:T(8,128)S(1)}, f32[6,8,16]{2,1,0:T(8,128)S(1)}, u32[]{:S(2)}, u32[]{:S(2)}) collective-permute-start(f32[6,8,16]{2,1,0:T(8,128)S(1)} %get-tuple-element.17), channel_id=1, source_target_pairs={{4,0},{8,4},{12,8},{16,12},{20,16},{24,20},{28,24},{32,28},{36,32}... | collective-permute-start | bytes 9224 | tf_op jit(solution)/shard_map/ppermute | solution.py:476
  15.7 0.1 sine_multiply_fusion
  15.7 0.0 collective-permute-done.top_ref
  15.7 0.0 collective-permute-done.1.bot_ref
  15.7 9.2 %propagate.1 = (f32[3456,128]{1,0:T(8,128)}, f32[3456,128]{1,0:T(8,128)}, bf16[32,216,128]{2,1,0:T(8,128)(2,1)}) custom-call(f32[2,36]{1,0:T(2,128)S(1)} %pad_maximum_fusion.4.speeds, f32[36,96,256]{2,1,0:T(8,128)} %spec_hbm.1, f32[37,4,256]{2,1,0:T(4,128)S(1)} %collective-permute-done.top_ref, f32[37,4,256]{2,1,0:T(4,128)S(1)} %collective-permute-done.1.bot_ref, ...), custom_call_target="tpu_custom_call" | custom-call | tf_op jit(solution)/shard_map/propagate/pallas_call | solution.py:189
  25.0 0.0 copy-start.3
  25.0 0.0 copy-start.1
  25.0 11.0 %all-to-all-start = ((bf16[32,216,128]{2,1,0:T(8,128)(2,1)}), bf16[32,216,128]{2,1,0:T(8,128)(2,1)S(1)}, u32[]{:S(2)}, u32[]{:S(2)}) async-start(bf16[32,216,128]{2,1,0:T(8,128)(2,1)} %get-tuple-element.5), calls=%async_computation | async-start | bytes 3538944 | tf_op jit(solution)/shard_map/all_to_all | solution.py:553
  36.0 0.2 multiply_add_fusion.1
  36.1 0.1 pad.19.clone
  36.2 0.2 multiply_add_fusion
  36.5 0.1 maximum_maximum_fusion.coef_ref
  36.5 0.0 collective-permute-done.2
  36.5 0.1 reshape.237
  36.6 0.0 collective-permute-done.3
  36.6 0.1 reshape.238
  36.7 0.0 copy-done.3
  36.7 0.6 reshape.236.points_ref
  37.3 24.6 %all-to-all-done = bf16[32,216,128]{2,1,0:T(8,128)(2,1)S(1)} async-done(((bf16[32,216,128]{2,1,0:T(8,128)(2,1)}), bf16[32,216,128]{2,1,0:T(8,128)(2,1)S(1)}, u32[]{:S(2)}, u32[]{:S(2)}) %all-to-all-start) | async-done | bytes 1769504 | tf_op jit(solution)/shard_map/all_to_all | solution.py:553
  61.9 0.0 copy-done.1
  61.9 14.6 %sources.1 = bf16[32,264,128]{2,1,0:T(8,128)(2,1)} custom-call(bf16[6912,128]{1,0:T(8,128)(2,1)S(1)} %bitcast.6, bf16[1152,1152]{1,0:T(8,128)(2,1)} %quad_hbm.1, f32[9,128]{1,0:T(8,128)S(1)} %bitcast.7, bf16[16,1152]{1,0:T(8,128)(2,1)S(1)} %maximum_maximum_fusion.coef_ref, s32[30,128]{1,0:T(8,128)} %reshape.236.points_ref), custom_call_target="tpu_custom_call" | custom-call | tf_op jit(solution)/shard_map/sources/pallas_call | solution.py:334
  76.5 0.0 copy-start
  76.5 4.2 %all-to-all-start.1 = ((bf16[32,264,128]{2,1,0:T(8,128)(2,1)}), bf16[32,264,128]{2,1,0:T(8,128)(2,1)S(1)}, u32[]{:S(2)}, u32[]{:S(2)}) async-start(bf16[32,264,128]{2,1,0:T(8,128)(2,1)} %sources.1), calls=%async_computation.1 | async-start | bytes 4325376 | tf_op jit(solution)/shard_map/all_to_all | solution.py:574
  80.7 0.0 copy-start.2
  80.7 30.3 %all-to-all-done.1.back_ref = bf16[32,264,128]{2,1,0:T(8,128)(2,1)S(1)} async-done(((bf16[32,264,128]{2,1,0:T(8,128)(2,1)}), bf16[32,264,128]{2,1,0:T(8,128)(2,1)S(1)}, u32[]{:S(2)}, u32[]{:S(2)}) %all-to-all-start.1) | async-done | bytes 2162720 | tf_op jit(solution)/shard_map/all_to_all | solution.py:574
  111.1 0.0 copy-done
  111.1 2.3 %pick.1 = f32[3,10,128]{2,1,0:T(8,128)S(1)} custom-call(bf16[32,264,128]{2,1,0:T(8,128)(2,1)S(1)} %all-to-all-done.1.back_ref, s32[30,128]{1,0:T(8,128)S(1)} %copy-done), custom_call_target="tpu_custom_call" | custom-call | tf_op jit(solution)/shard_map/pick/pallas_call | solution.py:391
  113.5 0.1 reshape_squeeze.6
  113.5 0.1 reshape_squeeze.7
  113.6 0.0 copy-done.2
  113.6 0.1 fusion.own_ref
  113.7 2.3 %collective-permute-start.4 = (f32[6,8,160]{2,1,0:T(8,128)S(1)}, f32[6,8,160]{2,1,0:T(8,128)S(1)}, u32[]{:S(2)}, u32[]{:S(2)}) collective-permute-start(f32[6,8,160]{2,1,0:T(8,128)S(1)} %fusion.own_ref), channel_id=1, source_target_pairs={{0,1},{1,0},{2,3},{3,2},{4,5},{5,4},{6,7},{7,6},{8,9},{9,8},{10,11... | collective-permute-start | bytes 92168 | tf_op jit(solution)/shard_map/ppermute | solution.py:584
  116.0 0.0 collective-permute-start.5
  116.0 1.7 %collective-permute-start.6 = (f32[6,8,160]{2,1,0:T(8,128)S(1)}, f32[6,8,160]{2,1,0:T(8,128)S(1)}, u32[]{:S(2)}, u32[]{:S(2)}) collective-permute-start(f32[6,8,160]{2,1,0:T(8,128)S(1)} %fusion.own_ref), channel_id=1, source_target_pairs={{0,3},{1,2},{2,1},{3,0},{4,7},{5,6},{6,5},{7,4},{8,11},{9,10},{10,... | collective-permute-start | bytes 92168 | tf_op jit(solution)/shard_map/ppermute | solution.py:584
  117.7 0.1 pad_add_fusion.1.place
  117.8 4.0 %finish.1 = f32[36,96,256]{2,1,0:T(8,128)} custom-call(bf16[32,264,128]{2,1,0:T(8,128)(2,1)S(1)} %all-to-all-done.1.back_ref, f32[3456,128]{1,0:T(8,128)} %get-tuple-element.6.prop0_hbm, f32[3456,128]{1,0:T(8,128)} %get-tuple-element.7.prop1_hbm), custom_call_target="tpu_custom_call" | custom-call | tf_op jit(solution)/shard_map/finish/pallas_call | solution.py:454
  121.8 0.0 collective-permute-done.4.one_ref
  121.8 0.0 collective-permute-done.5.two_ref
  121.8 0.0 collective-permute-done.6.three_ref
  121.8 2.6 %water.1 = f32[3,8,128]{2,1,0:T(8,128)} custom-call(s32[3]{0:T(128)S(1)} %pad_add_fusion.1.place, f32[6,8,160]{2,1,0:T(8,128)S(1)} %fusion.own_ref, f32[6,8,160]{2,1,0:T(8,128)S(1)} %collective-permute-done.4.one_ref, f32[6,8,160]{2,1,0:T(8,128)S(1)} %collective-permute-done.5.two_ref, f32[6,8,160]{2,1,0:T(8,128)S(1)} %collective-permute-done.6.three_ref), custom_call_target="tpu_custom_call" | custom-call | tf_op jit(solution)/shard_map/water/pallas_call | solution.py:530
  (12 shorter events, 0.2 us)
Async XLA Ops:
  2.7 13.0 %collective-permute-start = (f32[37,4,256]{2,1,0:T(4,128)S(1)}, f32[37,4,256]{2,1,0:T(4,128)S(1)}, u32[]{:S(2)}, u32[]{:S(2)}) collective-permute-start(f32[37,4,256]{2,1,0:T(4,128)S(1)} %pad_maximum_fusion), channel_id=1, source_target_pairs={{0,1},{1,2},{2,3},{4,5},{5,6},{6,7},{8,9},{9,10},{10,11},{12,13},{... | collective-permute-start | bytes 454664 | tf_op jit(solution)/shard_map/ppermute | solution.py:475
  6.9 8.9 %collective-permute-start.1 = (f32[37,4,256]{2,1,0:T(4,128)S(1)}, f32[37,4,256]{2,1,0:T(4,128)S(1)}, u32[]{:S(2)}, u32[]{:S(2)}) collective-permute-start(f32[37,4,256]{2,1,0:T(4,128)S(1)} %pad_maximum_fusion.1), channel_id=1, source_target_pairs={{1,0},{2,1},{3,2},{5,4},{6,5},{7,6},{9,8},{10,9},{11,10},{13,12},{... | collective-permute-start | bytes 454664 | tf_op jit(solution)/shard_map/ppermute | solution.py:476
  10.4 26.2 %collective-permute-start.2 = (f32[6,8,16]{2,1,0:T(8,128)S(1)}, f32[6,8,16]{2,1,0:T(8,128)S(1)}, u32[]{:S(2)}, u32[]{:S(2)}) collective-permute-start(f32[6,8,16]{2,1,0:T(8,128)S(1)} %get-tuple-element.16), channel_id=1, source_target_pairs={{0,4},{4,8},{8,12},{12,16},{16,20},{20,24},{24,28},{28,32},{32,36}... | collective-permute-start | bytes 9224 | tf_op jit(solution)/shard_map/ppermute | solution.py:475
  13.6 23.1 %collective-permute-start.3 = (f32[6,8,16]{2,1,0:T(8,128)S(1)}, f32[6,8,16]{2,1,0:T(8,128)S(1)}, u32[]{:S(2)}, u32[]{:S(2)}) collective-permute-start(f32[6,8,16]{2,1,0:T(8,128)S(1)} %get-tuple-element.17), channel_id=1, source_target_pairs={{4,0},{8,4},{12,8},{16,12},{20,16},{24,20},{28,24},{32,28},{36,32}... | collective-permute-start | bytes 9224 | tf_op jit(solution)/shard_map/ppermute | solution.py:476
  25.0 11.7 %copy-start.3 = (s32[3,8,128]{2,1,0:T(8,128)S(1)}, s32[3,8,128]{2,1,0:T(8,128)}, u32[]{:S(2)}) copy-start(s32[3,8,128]{2,1,0:T(8,128)} %param.11) | copy-start | bytes 36868
  25.0 36.9 %copy-start.1 = (f32[1152]{0:T(1024)S(1)}, f32[1152]{0:T(1024)}, u32[]{:S(2)}) copy-start(f32[1152]{0:T(1024)} %param.9) | copy-start | bytes 13828
  25.0 36.9 %all-to-all-start = ((bf16[32,216,128]{2,1,0:T(8,128)(2,1)}), bf16[32,216,128]{2,1,0:T(8,128)(2,1)S(1)}, u32[]{:S(2)}, u32[]{:S(2)}) async-start(bf16[32,216,128]{2,1,0:T(8,128)(2,1)} %get-tuple-element.5), calls=%async_computation | async-start | bytes 3538944 | tf_op jit(solution)/shard_map/all_to_all | solution.py:553
  76.5 34.6 %copy-start = (s32[30,128]{1,0:T(8,128)S(1)}, s32[30,128]{1,0:T(8,128)}, u32[]{:S(2)}) copy-start(s32[30,128]{1,0:T(8,128)} %reshape.236.points_ref) | copy-start | bytes 46084
  76.5 34.6 %all-to-all-start.1 = ((bf16[32,264,128]{2,1,0:T(8,128)(2,1)}), bf16[32,264,128]{2,1,0:T(8,128)(2,1)S(1)}, u32[]{:S(2)}, u32[]{:S(2)}) async-start(bf16[32,264,128]{2,1,0:T(8,128)(2,1)} %sources.1), calls=%async_computation.1 | async-start | bytes 4325376 | tf_op jit(solution)/shard_map/all_to_all | solution.py:574
  80.7 32.9 %copy-start.2 = (f32[3,8,128]{2,1,0:T(8,128)S(1)}, f32[3,8,128]{2,1,0:T(8,128)}, u32[]{:S(2)}) copy-start(f32[3,8,128]{2,1,0:T(8,128)} %param.10) | copy-start | bytes 36868
  113.7 8.1 %collective-permute-start.4 = (f32[6,8,160]{2,1,0:T(8,128)S(1)}, f32[6,8,160]{2,1,0:T(8,128)S(1)}, u32[]{:S(2)}, u32[]{:S(2)}) collective-permute-start(f32[6,8,160]{2,1,0:T(8,128)S(1)} %fusion.own_ref), channel_id=1, source_target_pairs={{0,1},{1,0},{2,3},{3,2},{4,5},{5,4},{6,7},{7,6},{8,9},{9,8},{10,11... | collective-permute-start | bytes 92168 | tf_op jit(solution)/shard_map/ppermute | solution.py:584
  116.0 5.8 %collective-permute-start.5 = (f32[6,8,160]{2,1,0:T(8,128)S(1)}, f32[6,8,160]{2,1,0:T(8,128)S(1)}, u32[]{:S(2)}, u32[]{:S(2)}) collective-permute-start(f32[6,8,160]{2,1,0:T(8,128)S(1)} %fusion.own_ref), channel_id=1, source_target_pairs={{0,2},{1,3},{2,0},{3,1},{4,6},{5,7},{6,4},{7,5},{8,10},{9,11},{10,... | collective-permute-start | bytes 92168 | tf_op jit(solution)/shard_map/ppermute | solution.py:584
  116.0 5.8 %collective-permute-start.6 = (f32[6,8,160]{2,1,0:T(8,128)S(1)}, f32[6,8,160]{2,1,0:T(8,128)S(1)}, u32[]{:S(2)}, u32[]{:S(2)}) collective-permute-start(f32[6,8,160]{2,1,0:T(8,128)S(1)} %fusion.own_ref), channel_id=1, source_target_pairs={{0,3},{1,2},{2,1},{3,0},{4,7},{5,6},{6,5},{7,4},{8,11},{9,10},{10,... | collective-permute-start | bytes 92168 | tf_op jit(solution)/shard_map/ppermute | solution.py:584

commit v5 on v4

--- a/solution.py
+++ b/solution.py
@@ -214,7 +214,7 @@
 EB = 64
 NB = 256
 OWN_ROWS = RUN * LOCAL
-PIECES = 6
+PIECES = 3
 BLOCKS = RUN * 128 // NB
 BACK_ROWS = OWN_ROWS + 8 * PIECES
 
@@ -224,6 +224,7 @@
     quad_ref, back_ref, prod_a, prod_b, flat, cur, xa, xb, rate, level, quad_sems, out_sem,
 ):
     halves = K // MB
+    points = RUN * 128
 
     def fetch(m):
         part = pl.ds(m * MB, MB)
@@ -251,9 +252,6 @@
             cur[:, cols] = base
             xa[:, cols] = base.astype(jnp.bfloat16)
             level[:, cols] = jnp.sum(base, axis=0, keepdims=True)
-        stress.append(
-            jnp.dot(coef, xa[:, n * NB:(n + 1) * NB], preferred_element_type=jnp.float32)
-        )
 
     def multiply(s, n):
         held = (prod_a, prod_b)[(s * BLOCKS + n) % 2]
@@ -287,34 +285,43 @@
             base = flat[pl.ds(j, K, stride=RUN), :]
             cols = slice(j * 128, (j + 1) * 128)
             gain = (cur[:, cols] - base).astype(jnp.bfloat16)
-            xa[:, cols] = gain
+            xb[:, cols] = gain
             flat[pl.ds(j, K, stride=RUN), :] = gain.astype(jnp.float32)
+
+    def weigh(n):
         both = stress[n] + jnp.dot(
-            coef, xa[:, n * NB:(n + 1) * NB], preferred_element_type=jnp.float32
+            coef, xb[:, n * NB:(n + 1) * NB], preferred_element_type=jnp.float32
         )
         for c in range(3):
             row = (both[c:c + 1] + both[3 + c:4 + c] + both[6 + c:7 + c]) * (1.0 / K)
             rows_of[c] += [row[:, i * 128:(i + 1) * 128] for i in range(each_block)]
 
+    for n in range(BLOCKS):
+        prepare(n)
+    for n in range(BLOCKS):
+        stress.append(
+            jnp.dot(coef, xa[:, n * NB:(n + 1) * NB], preferred_element_type=jnp.float32)
+        )
     for m in range(halves):
         fetch(m).wait()
-    prepare(0)
     turns = [(s, n) for s in range(SRC_STEPS) for n in range(BLOCKS)]
     for i, (s, n) in enumerate(turns):
         multiply(s, n)
-        if s == 0 and n + 1 < BLOCKS:
-            prepare(n + 1)
         if i > 0:
             update(*turns[i - 1])
-        if s == SRC_STEPS - 1 and n > 0:
-            conclude(n - 1)
     update(*turns[-1])
-    conclude(BLOCKS - 1)
+    for n in range(BLOCKS):
+        conclude(n)
+    for n in range(BLOCKS):
+        weigh(n)
     pieces = []
     for c in range(3):
-        whole = jnp.concatenate(rows_of[c] + [jnp.zeros((8 - RUN, 128), jnp.float32)], axis=0)
-        high = whole.astype(jnp.bfloat16).astype(jnp.float32)
-        pieces += [high, whole - high]
+        whole = jnp.concatenate(rows_of[c], axis=0)
+        mean = jnp.sum(jnp.sum(whole, axis=0, keepdims=True), axis=1, keepdims=True)
+        mean = jnp.broadcast_to(mean * (1.0 / points), (1, 128))
+        high = mean.astype(jnp.bfloat16).astype(jnp.float32)
+        low = (mean - high).astype(jnp.bfloat16).astype(jnp.float32)
+        pieces += [whole - (high + low), high, low]
     shared = jnp.concatenate(pieces, axis=0).astype(jnp.bfloat16)
 
     def narrow(o, carry):
@@ -372,12 +379,13 @@
             row = p >> 8
             col = p & 255
             hi = (((col >> 7) * GROUP + (row & (GROUP - 1))) << 3) + (row >> 4)
-            hots.append(jnp.where(slot == hi, 1.0, 0.0).astype(jnp.bfloat16))
+            taken = (slot == hi) | ((slot | 1) == (hi | 7))
+            hots.append(jnp.where(taken, 1.0, 0.0).astype(jnp.bfloat16))
             lows.append(col & 127)
         hot = jnp.concatenate(hots, axis=1)
         found = jnp.dot(table, hot, preferred_element_type=jnp.float32)
         for c in range(3):
-            both = found[2 * c * 128:(2 * c + 1) * 128] + found[(2 * c + 1) * 128:(2 * c + 2) * 128]
+            both = found[c * 128:(c + 1) * 128]
             acc = jnp.zeros((128, 128), jnp.float32)
             for m in range(3):
                 acc = acc + jnp.where(
@@ -415,13 +423,12 @@
 
     lax.fori_loop(0, LOCAL // KB, load, 0)
 
-    def spread(g, carry):
+    def spread(i):
+        rows = pl.ds(pl.multiple_of(i * KB * RUN, 8), KB * RUN)
         for h in range(2):
-            gain = back_ref[h * GROUP + g, 0:OWN_ROWS, :].astype(jnp.float32)
-            wide[h, pl.ds(g, OWN_ROWS, stride=GROUP), :] = gain
-        return carry
-
-    lax.fori_loop(0, GROUP, spread, 0)
+            for g in range(GROUP):
+                gain = back_ref[h * GROUP + g, rows, :].astype(jnp.float32)
+                wide[h, pl.ds(g, KB * RUN, stride=GROUP), :] = gain
 
     def copy(i):
         part = pl.ds(i * KB, KB)
@@ -430,11 +437,14 @@
     def add(i, carry):
         for copy_in in keep(i):
             copy_in.wait()
+        spread(i)
         for kk in range(KB):
             k = i * KB + kk
             for h, prop in enumerate((prop0, prop1)):
                 rows = pl.ds(k * ROWS, ROWS)
-                out[k, :, h * 128:(h + 1) * 128] = prop[rows, :] + wide[h, rows, :]
+                out[k, :, h * 128:(h + 1) * 128] = (
+                    prop[rows, :] + wide[h, kk * ROWS:(kk + 1) * ROWS, :]
+                )
         copy(i).start()
         return carry
 
@@ -459,7 +469,7 @@
         scratch_shapes=[
             pltpu.VMEM((LOCAL * ROWS, 128), jnp.float32),
             pltpu.VMEM((LOCAL * ROWS, 128), jnp.float32),
-            pltpu.VMEM((2, LOCAL * ROWS, 128), jnp.float32),
+            pltpu.VMEM((2, KB * ROWS, 128), jnp.float32),
             pltpu.VMEM(shape, jnp.float32),
             pltpu.SemaphoreType.DMA((LOCAL // KB,)),
             pltpu.SemaphoreType.DMA((2, LOCAL // KB)),

time: 125 us -> 121 us (0.968)
  waiting for transfers between devices: 54.9 us -> 52.7 us
  Pallas kernels: 32.7 us -> 30.9 us
    all_to_all x1, waiting for transfers between devices: 30.3 us -> 28 us  [window(): back = lax.all_to_all(back, 'comp', 0, 0, tiled=True)]
    pallas_call x1, Pallas kernels: 14.6 us -> 13.3 us  [sources(): pl.pallas_call(source_kernel, in_specs=[vmem, hbm, vmem, vmem, hbm], out_...]
  transfers between devices with their start and end apart: 9 -> 9, of which waited for: 2 -> 2; matrix products, arithmetic and copies ran while one was open for 2% -> 3% of each run, Pallas kernels for 11% -> 11%
where the time goes in v5:
time: 121 us; the launch traced here: 120 us
  waiting for transfers between devices  52.7 us (44%)
  Pallas kernels  30.9 us (26%)
  starting transfers between devices  30 us (25%)
  other arithmetic  3.25 us (3%)
  local copies, waits for them, and re-layouts  2.15 us (2%)
    all_to_all x1, waiting for transfers between devices, window(): back = lax.all_to_all(back, 'comp', 0, 0, tiled=True)  28 us
    all_to_all x1, waiting for transfers between devices, window(): received = lax.all_to_all(sent, 'comp', 0, 0, tiled=True)  24.6 us
    pallas_call x1, Pallas kernels, sources(): pl.pallas_call(source_kernel, in_specs=[vmem, hbm, vmem, vmem, hbm], out_...  13.3 us
    all_to_all x1, starting transfers between devices, window(): received = lax.all_to_all(sent, 'comp', 0, 0, tiled=True)  11 us
    pallas_call x1, Pallas kernels, propagate(): pl.pallas_call(propagate_kernel, in_specs=[pl.BlockSpec(memory_space=pltp...  9.22 us
    ppermute x2, starting transfers between devices, from_neighbours(): lax.ppermute(high, axis, [(i, (i + 1) % count) for i in range(ends)])  7.3 us
    all_to_all x1, starting transfers between devices, window(): back = lax.all_to_all(back, 'comp', 0, 0, tiled=True)  4.21 us
    ppermute x2, starting transfers between devices, from_neighbours(): after = lax.ppermute(low, axis, [((i + 1) % count, i) for i in range(ends)])  4 us
  transfers between devices with their start and end apart: 9, of which 2 were waited for; matrix products, arithmetic and copies ran while one was open for 3% of the time, Pallas kernels for 11%

profile of v5, /device:TPU:9, one launch (start us, length us, event | category | flops | bytes accessed | tf_op | source)
XLA Modules:
  0.0 119.9 jit_solution(9106665086568457400)
XLA Ops:
  0.6 0.9 fusion.18
  1.6 1.1 fusion.17
  2.7 4.1 %collective-permute-start = (f32[37,4,256]{2,1,0:T(4,128)S(1)}, f32[37,4,256]{2,1,0:T(4,128)S(1)}, u32[]{:S(2)}, u32[]{:S(2)}) collective-permute-start(f32[37,4,256]{2,1,0:T(4,128)S(1)} %pad_maximum_fusion), channel_id=1, source_target_pairs={{0,1},{1,2},{2,3},{4,5},{5,6},{6,7},{8,9},{9,10},{10,11},{12,13},{... | collective-permute-start | bytes 454664 | tf_op jit(solution)/shard_map/ppermute | solution.py:485
  6.9 1.9 %collective-permute-start.1 = (f32[37,4,256]{2,1,0:T(4,128)S(1)}, f32[37,4,256]{2,1,0:T(4,128)S(1)}, u32[]{:S(2)}, u32[]{:S(2)}) collective-permute-start(f32[37,4,256]{2,1,0:T(4,128)S(1)} %pad_maximum_fusion.1), channel_id=1, source_target_pairs={{1,0},{2,1},{3,2},{5,4},{6,5},{7,6},{9,8},{10,9},{11,10},{13,12},{... | collective-permute-start | bytes 454664 | tf_op jit(solution)/shard_map/ppermute | solution.py:486
  8.8 0.7 convert_element_type.106
  9.5 0.9 slice_maximum_fusion
  10.4 3.2 %collective-permute-start.2 = (f32[6,8,16]{2,1,0:T(8,128)S(1)}, f32[6,8,16]{2,1,0:T(8,128)S(1)}, u32[]{:S(2)}, u32[]{:S(2)}) collective-permute-start(f32[6,8,16]{2,1,0:T(8,128)S(1)} %get-tuple-element.16), channel_id=1, source_target_pairs={{0,4},{4,8},{8,12},{12,16},{16,20},{20,24},{24,28},{28,32},{32,36}... | collective-permute-start | bytes 9224 | tf_op jit(solution)/shard_map/ppermute | solution.py:485
  13.6 2.1 %collective-permute-start.3 = (f32[6,8,16]{2,1,0:T(8,128)S(1)}, f32[6,8,16]{2,1,0:T(8,128)S(1)}, u32[]{:S(2)}, u32[]{:S(2)}) collective-permute-start(f32[6,8,16]{2,1,0:T(8,128)S(1)} %get-tuple-element.17), channel_id=1, source_target_pairs={{4,0},{8,4},{12,8},{16,12},{20,16},{24,20},{28,24},{32,28},{36,32}... | collective-permute-start | bytes 9224 | tf_op jit(solution)/shard_map/ppermute | solution.py:486
  15.7 0.1 sine_multiply_fusion
  15.7 0.0 collective-permute-done.top_ref
  15.7 0.0 collective-permute-done.1.bot_ref
  15.7 9.2 %propagate.1 = (f32[3456,128]{1,0:T(8,128)}, f32[3456,128]{1,0:T(8,128)}, bf16[32,216,128]{2,1,0:T(8,128)(2,1)}) custom-call(f32[2,36]{1,0:T(2,128)S(1)} %pad_maximum_fusion.4.speeds, f32[36,96,256]{2,1,0:T(8,128)} %spec_hbm.1, f32[37,4,256]{2,1,0:T(4,128)S(1)} %collective-permute-done.top_ref, f32[37,4,256]{2,1,0:T(4,128)S(1)} %collective-permute-done.1.bot_ref, ...), custom_call_target="tpu_custom_call" | custom-call | tf_op jit(solution)/shard_map/propagate/pallas_call | solution.py:189
  25.0 0.0 copy-start.3
  25.0 0.0 copy-start.1
  25.0 11.0 %all-to-all-start = ((bf16[32,216,128]{2,1,0:T(8,128)(2,1)}), bf16[32,216,128]{2,1,0:T(8,128)(2,1)S(1)}, u32[]{:S(2)}, u32[]{:S(2)}) async-start(bf16[32,216,128]{2,1,0:T(8,128)(2,1)} %get-tuple-element.5), calls=%async_computation | async-start | bytes 3538944 | tf_op jit(solution)/shard_map/all_to_all | solution.py:563
  36.0 0.2 multiply_add_fusion.1
  36.1 0.1 pad.19.clone
  36.2 0.2 multiply_add_fusion
  36.4 0.1 maximum_maximum_fusion.coef_ref
  36.5 0.0 collective-permute-done.2
  36.5 0.1 reshape.237
  36.6 0.0 collective-permute-done.3
  36.6 0.1 reshape.238
  36.7 0.0 copy-done.3
  36.7 0.6 reshape.236.points_ref
  37.3 24.6 %all-to-all-done = bf16[32,216,128]{2,1,0:T(8,128)(2,1)S(1)} async-done(((bf16[32,216,128]{2,1,0:T(8,128)(2,1)}), bf16[32,216,128]{2,1,0:T(8,128)(2,1)S(1)}, u32[]{:S(2)}, u32[]{:S(2)}) %all-to-all-start) | async-done | bytes 1769504 | tf_op jit(solution)/shard_map/all_to_all | solution.py:563
  61.9 0.0 copy-done.1
  61.9 13.3 %sources.1 = bf16[32,240,128]{2,1,0:T(8,128)(2,1)} custom-call(bf16[6912,128]{1,0:T(8,128)(2,1)S(1)} %bitcast.6, bf16[1152,1152]{1,0:T(8,128)(2,1)} %quad_hbm.1, f32[9,128]{1,0:T(8,128)S(1)} %bitcast.7, bf16[16,1152]{1,0:T(8,128)(2,1)S(1)} %maximum_maximum_fusion.coef_ref, s32[30,128]{1,0:T(8,128)} %reshape.236.points_ref), custom_call_target="tpu_custom_call" | custom-call | tf_op jit(solution)/shard_map/sources/pallas_call | solution.py:341
  75.2 0.0 copy-start
  75.2 4.2 %all-to-all-start.1 = ((bf16[32,240,128]{2,1,0:T(8,128)(2,1)}), bf16[32,240,128]{2,1,0:T(8,128)(2,1)S(1)}, u32[]{:S(2)}, u32[]{:S(2)}) async-start(bf16[32,240,128]{2,1,0:T(8,128)(2,1)} %sources.1), calls=%async_computation.1 | async-start | bytes 3932160 | tf_op jit(solution)/shard_map/all_to_all | solution.py:584
  79.5 0.0 copy-start.2
  79.5 28.0 %all-to-all-done.1.back_ref = bf16[32,240,128]{2,1,0:T(8,128)(2,1)S(1)} async-done(((bf16[32,240,128]{2,1,0:T(8,128)(2,1)}), bf16[32,240,128]{2,1,0:T(8,128)(2,1)S(1)}, u32[]{:S(2)}, u32[]{:S(2)}) %all-to-all-start.1) | async-done | bytes 1966112 | tf_op jit(solution)/shard_map/all_to_all | solution.py:584
  107.5 0.0 copy-done
  107.5 2.0 %pick.1 = f32[3,10,128]{2,1,0:T(8,128)S(1)} custom-call(bf16[32,240,128]{2,1,0:T(8,128)(2,1)S(1)} %all-to-all-done.1.back_ref, s32[30,128]{1,0:T(8,128)S(1)} %copy-done), custom_call_target="tpu_custom_call" | custom-call | tf_op jit(solution)/shard_map/pick/pallas_call | solution.py:399
  109.5 0.1 reshape_squeeze.6
  109.6 0.1 reshape_squeeze.7
  109.7 0.0 copy-done.2
  109.7 0.1 fusion.own_ref
  109.8 1.8 %collective-permute-start.4 = (f32[6,8,160]{2,1,0:T(8,128)S(1)}, f32[6,8,160]{2,1,0:T(8,128)S(1)}, u32[]{:S(2)}, u32[]{:S(2)}) collective-permute-start(f32[6,8,160]{2,1,0:T(8,128)S(1)} %fusion.own_ref), channel_id=1, source_target_pairs={{0,1},{1,0},{2,3},{3,2},{4,5},{5,4},{6,7},{7,6},{8,9},{9,8},{10,11... | collective-permute-start | bytes 92168 | tf_op jit(solution)/shard_map/ppermute | solution.py:594
  111.7 0.0 collective-permute-start.5
  111.7 1.7 %collective-permute-start.6 = (f32[6,8,160]{2,1,0:T(8,128)S(1)}, f32[6,8,160]{2,1,0:T(8,128)S(1)}, u32[]{:S(2)}, u32[]{:S(2)}) collective-permute-start(f32[6,8,160]{2,1,0:T(8,128)S(1)} %fusion.own_ref), channel_id=1, source_target_pairs={{0,3},{1,2},{2,1},{3,0},{4,7},{5,6},{6,5},{7,4},{8,11},{9,10},{10,... | collective-permute-start | bytes 92168 | tf_op jit(solution)/shard_map/ppermute | solution.py:594
  113.4 0.1 pad_add_fusion.1.place
  113.5 3.7 %finish.1 = f32[36,96,256]{2,1,0:T(8,128)} custom-call(bf16[32,240,128]{2,1,0:T(8,128)(2,1)S(1)} %all-to-all-done.1.back_ref, f32[3456,128]{1,0:T(8,128)} %get-tuple-element.6.prop0_hbm, f32[3456,128]{1,0:T(8,128)} %get-tuple-element.7.prop1_hbm), custom_call_target="tpu_custom_call" | custom-call | tf_op jit(solution)/shard_map/finish/pallas_call | solution.py:464
  117.2 0.0 collective-permute-done.4.one_ref
  117.2 0.0 collective-permute-done.5.two_ref
  117.2 0.0 collective-permute-done.6.three_ref
  117.2 2.6 %water.1 = f32[3,8,128]{2,1,0:T(8,128)} custom-call(s32[3]{0:T(128)S(1)} %pad_add_fusion.1.place, f32[6,8,160]{2,1,0:T(8,128)S(1)} %fusion.own_ref, f32[6,8,160]{2,1,0:T(8,128)S(1)} %collective-permute-done.4.one_ref, f32[6,8,160]{2,1,0:T(8,128)S(1)} %collective-permute-done.5.two_ref, f32[6,8,160]{2,1,0:T(8,128)S(1)} %collective-permute-done.6.three_ref), custom_call_target="tpu_custom_call" | custom-call | tf_op jit(solution)/shard_map/water/pallas_call | solution.py:540
  (12 shorter events, 0.2 us)
Async XLA Ops:
  2.7 13.0 %collective-permute-start = (f32[37,4,256]{2,1,0:T(4,128)S(1)}, f32[37,4,256]{2,1,0:T(4,128)S(1)}, u32[]{:S(2)}, u32[]{:S(2)}) collective-permute-start(f32[37,4,256]{2,1,0:T(4,128)S(1)} %pad_maximum_fusion), channel_id=1, source_target_pairs={{0,1},{1,2},{2,3},{4,5},{5,6},{6,7},{8,9},{9,10},{10,11},{12,13},{... | collective-permute-start | bytes 454664 | tf_op jit(solution)/shard_map/ppermute | solution.py:485
  6.9 8.9 %collective-permute-start.1 = (f32[37,4,256]{2,1,0:T(4,128)S(1)}, f32[37,4,256]{2,1,0:T(4,128)S(1)}, u32[]{:S(2)}, u32[]{:S(2)}) collective-permute-start(f32[37,4,256]{2,1,0:T(4,128)S(1)} %pad_maximum_fusion.1), channel_id=1, source_target_pairs={{1,0},{2,1},{3,2},{5,4},{6,5},{7,6},{9,8},{10,9},{11,10},{13,12},{... | collective-permute-start | bytes 454664 | tf_op jit(solution)/shard_map/ppermute | solution.py:486
  10.4 26.2 %collective-permute-start.2 = (f32[6,8,16]{2,1,0:T(8,128)S(1)}, f32[6,8,16]{2,1,0:T(8,128)S(1)}, u32[]{:S(2)}, u32[]{:S(2)}) collective-permute-start(f32[6,8,16]{2,1,0:T(8,128)S(1)} %get-tuple-element.16), channel_id=1, source_target_pairs={{0,4},{4,8},{8,12},{12,16},{16,20},{20,24},{24,28},{28,32},{32,36}... | collective-permute-start | bytes 9224 | tf_op jit(solution)/shard_map/ppermute | solution.py:485
  13.6 23.1 %collective-permute-start.3 = (f32[6,8,16]{2,1,0:T(8,128)S(1)}, f32[6,8,16]{2,1,0:T(8,128)S(1)}, u32[]{:S(2)}, u32[]{:S(2)}) collective-permute-start(f32[6,8,16]{2,1,0:T(8,128)S(1)} %get-tuple-element.17), channel_id=1, source_target_pairs={{4,0},{8,4},{12,8},{16,12},{20,16},{24,20},{28,24},{32,28},{36,32}... | collective-permute-start | bytes 9224 | tf_op jit(solution)/shard_map/ppermute | solution.py:486
  25.0 11.7 %copy-start.3 = (s32[3,8,128]{2,1,0:T(8,128)S(1)}, s32[3,8,128]{2,1,0:T(8,128)}, u32[]{:S(2)}) copy-start(s32[3,8,128]{2,1,0:T(8,128)} %param.11) | copy-start | bytes 36868
  25.0 36.9 %copy-start.1 = (f32[1152]{0:T(1024)S(1)}, f32[1152]{0:T(1024)}, u32[]{:S(2)}) copy-start(f32[1152]{0:T(1024)} %param.9) | copy-start | bytes 13828
  25.0 36.9 %all-to-all-start = ((bf16[32,216,128]{2,1,0:T(8,128)(2,1)}), bf16[32,216,128]{2,1,0:T(8,128)(2,1)S(1)}, u32[]{:S(2)}, u32[]{:S(2)}) async-start(bf16[32,216,128]{2,1,0:T(8,128)(2,1)} %get-tuple-element.5), calls=%async_computation | async-start | bytes 3538944 | tf_op jit(solution)/shard_map/all_to_all | solution.py:563
  75.2 32.3 %copy-start = (s32[30,128]{1,0:T(8,128)S(1)}, s32[30,128]{1,0:T(8,128)}, u32[]{:S(2)}) copy-start(s32[30,128]{1,0:T(8,128)} %reshape.236.points_ref) | copy-start | bytes 46084
  75.2 32.3 %all-to-all-start.1 = ((bf16[32,240,128]{2,1,0:T(8,128)(2,1)}), bf16[32,240,128]{2,1,0:T(8,128)(2,1)S(1)}, u32[]{:S(2)}, u32[]{:S(2)}) async-start(bf16[32,240,128]{2,1,0:T(8,128)(2,1)} %sources.1), calls=%async_computation.1 | async-start | bytes 3932160 | tf_op jit(solution)/shard_map/all_to_all | solution.py:584
  79.5 30.2 %copy-start.2 = (f32[3,8,128]{2,1,0:T(8,128)S(1)}, f32[3,8,128]{2,1,0:T(8,128)}, u32[]{:S(2)}) copy-start(f32[3,8,128]{2,1,0:T(8,128)} %param.10) | copy-start | bytes 36868
  109.8 7.4 %collective-permute-start.4 = (f32[6,8,160]{2,1,0:T(8,128)S(1)}, f32[6,8,160]{2,1,0:T(8,128)S(1)}, u32[]{:S(2)}, u32[]{:S(2)}) collective-permute-start(f32[6,8,160]{2,1,0:T(8,128)S(1)} %fusion.own_ref), channel_id=1, source_target_pairs={{0,1},{1,0},{2,3},{3,2},{4,5},{5,4},{6,7},{7,6},{8,9},{9,8},{10,11... | collective-permute-start | bytes 92168 | tf_op jit(solution)/shard_map/ppermute | solution.py:594
  111.7 5.6 %collective-permute-start.5 = (f32[6,8,160]{2,1,0:T(8,128)S(1)}, f32[6,8,160]{2,1,0:T(8,128)S(1)}, u32[]{:S(2)}, u32[]{:S(2)}) collective-permute-start(f32[6,8,160]{2,1,0:T(8,128)S(1)} %fusion.own_ref), channel_id=1, source_target_pairs={{0,2},{1,3},{2,0},{3,1},{4,6},{5,7},{6,4},{7,5},{8,10},{9,11},{10,... | collective-permute-start | bytes 92168 | tf_op jit(solution)/shard_map/ppermute | solution.py:594
  111.7 5.6 %collective-permute-start.6 = (f32[6,8,160]{2,1,0:T(8,128)S(1)}, f32[6,8,160]{2,1,0:T(8,128)S(1)}, u32[]{:S(2)}, u32[]{:S(2)}) collective-permute-start(f32[6,8,160]{2,1,0:T(8,128)S(1)} %fusion.own_ref), channel_id=1, source_target_pairs={{0,3},{1,2},{2,1},{3,0},{4,7},{5,6},{6,5},{7,4},{8,11},{9,10},{10,... | collective-permute-start | bytes 92168 | tf_op jit(solution)/shard_map/ppermute | solution.py:594

commit v6 on v5

--- a/solution.py
+++ b/solution.py
@@ -62,6 +62,49 @@
     return pltpu.with_memory_space_constraint(array, pltpu.VMEM)
 
 
+def rim_kernel(spec_hbm, wet_hbm, low_ref, high_ref, wet_ref, head, tail, mask, sems):
+    copies = (
+        pltpu.make_async_copy(spec_hbm.at[:, 0:8, :], head, sems.at[0]),
+        pltpu.make_async_copy(spec_hbm.at[:, ROWS - 8:ROWS, :], tail, sems.at[1]),
+        pltpu.make_async_copy(wet_hbm, mask, sems.at[2]),
+    )
+    for copy in copies:
+        copy.start()
+    copies[2].wait()
+    wet = mask[...].astype(jnp.float32)
+    wet_ref[...] = wet
+    low_ref[LOCAL] = wet[0:HALO]
+    high_ref[LOCAL] = wet[ROWS - HALO:ROWS]
+    copies[0].wait()
+    low_ref[0:LOCAL] = head[:, 0:HALO, :]
+    copies[1].wait()
+    high_ref[0:LOCAL] = tail[:, 8 - HALO:8, :]
+
+
+def rims(spectrum, wet_mask):
+    cols = spectrum.shape[2]
+    vmem = pl.BlockSpec(memory_space=pltpu.VMEM)
+    hbm = pl.BlockSpec(memory_space=pltpu.HBM)
+    return pl.pallas_call(
+        rim_kernel,
+        in_specs=[hbm] * 2,
+        out_specs=[vmem] * 3,
+        out_shape=[
+            pltpu.VMEM((LOCAL + 1, HALO, cols), jnp.float32),
+            pltpu.VMEM((LOCAL + 1, HALO, cols), jnp.float32),
+            pltpu.VMEM((ROWS, cols), jnp.float32),
+        ],
+        scratch_shapes=[
+            pltpu.VMEM((LOCAL, 8, cols), jnp.float32),
+            pltpu.VMEM((LOCAL, 8, cols), jnp.float32),
+            pltpu.VMEM((ROWS, cols), jnp.int32),
+            pltpu.SemaphoreType.DMA((3,)),
+        ],
+        compiler_params=pltpu.CompilerParams(vmem_limit_bytes=4 << 20),
+        name="rims",
+    )(in_hbm(spectrum), in_hbm(wet_mask))
+
+
 def propagate_kernel(
     speeds, spec_hbm, top_ref, bot_ref, wet_ref, prop0_hbm, prop1_hbm, sent_hbm,
     spec_ref, load_sems, prop0, prop1, sent_ref, wet, left_a, right_a, left_b, right_b, keep_sems, sent_sems,
@@ -113,28 +156,29 @@
             side.append(jnp.where(lane == edge, 0.0, b[q]))
         for s in range(SUBSTEPS):
             for q in range(PAIR):
+                count = ext if s + 1 < SUBSTEPS else ROWS
                 left_ref, right_ref = fields[q][s % 2]
-                left, right = left_ref[8:8 + ext, :], right_ref[8:8 + ext, :]
-                ul = left_ref[pl.ds(ahead[q], ext), :]
-                ur = right_ref[pl.ds(ahead[q], ext), :]
+                left, right = left_ref[8:8 + count, :], right_ref[8:8 + count, :]
+                ul = left_ref[pl.ds(ahead[q], count), :]
+                ur = right_ref[pl.ds(ahead[q], count), :]
                 rl = pltpu.roll(left, turn, 1)
                 rr = pltpu.roll(right, turn, 1)
                 if north:
-                    across_l = side[q] * rl
-                    across_r = b[q] * jnp.where(lane == 0, rl, rr)
+                    across_l = side[q][:count] * rl
+                    across_r = b[q] * jnp.where(lane[:count] == 0, rl, rr)
                 else:
-                    across_l = b[q] * jnp.where(lane == 127, rr, rl)
-                    across_r = side[q] * rr
-                left = wet[:, :128] * (c[q] * left + a[q] * ul + across_l)
-                right = wet[:, 128:] * (c[q] * right + a[q] * ur + across_r)
+                    across_l = b[q] * jnp.where(lane[:count] == 127, rr, rl)
+                    across_r = side[q][:count] * rr
+                left = wet[:count, :128] * (c[q] * left + a[q] * ul + across_l)
+                right = wet[:count, 128:] * (c[q] * right + a[q] * ur + across_r)
                 if s + 1 < SUBSTEPS:
                     for ref, value in zip(fields[q][(s + 1) % 2], (left, right)):
                         ref[8:8 + ext, :] = value
                         ref[7:8, :] = value[ext - 1:]
                         ref[8 + ext:9 + ext, :] = value[0:1]
                 else:
-                    prop0[pl.ds((first + q) * ROWS, ROWS), :] = left[:ROWS]
-                    prop1[pl.ds((first + q) * ROWS, ROWS), :] = right[:ROWS]
+                    prop0[pl.ds((first + q) * ROWS, ROWS), :] = left
+                    prop1[pl.ds((first + q) * ROWS, ROWS), :] = right
 
     def some(i, carry):
         first = i * PAIR
@@ -207,7 +251,7 @@
         + [pltpu.SemaphoreType.DMA((2, LOCAL // KB)), pltpu.SemaphoreType.DMA((LOCAL // KB,))],
         compiler_params=pltpu.CompilerParams(vmem_limit_bytes=16 << 20),
         name="propagate",
-    )(speeds, in_hbm(spectrum), *map(in_vmem, (top, bottom, wetness)))
+    )(pltpu.with_memory_space_constraint(speeds, pltpu.SMEM), in_hbm(spectrum), *map(in_vmem, (top, bottom, wetness)))
 
 
 MB = 576
@@ -369,7 +413,8 @@
         rows = back_ref[:, at:at + 8, :].astype(jnp.float32).reshape(OWNERS * 8, 128)
         pieces.append(rows.T.astype(jnp.bfloat16))
     table = jnp.concatenate(pieces, axis=0)
-    slot = lax.broadcasted_iota(jnp.int32, (OWNERS * 8, 128), 0)
+    kind = lax.broadcasted_iota(jnp.int32, (8, 128), 0)
+    slot = lax.broadcasted_iota(jnp.int32, (OWNERS, 8, 128), 0) * 8 + kind
     within = lax.broadcasted_iota(jnp.int32, (128, 128), 0)
     weights = (0.5, 0.3, 0.2)
     for t in range(TILES):
@@ -379,18 +424,18 @@
             row = p >> 8
             col = p & 255
             hi = (((col >> 7) * GROUP + (row & (GROUP - 1))) << 3) + (row >> 4)
-            taken = (slot == hi) | ((slot | 1) == (hi | 7))
-            hots.append(jnp.where(taken, 1.0, 0.0).astype(jnp.bfloat16))
+            wanted = jnp.where(kind < RUN, hi, (hi & -8) + kind)
+            taken = jnp.where(slot == wanted, 1.0, 0.0).reshape(OWNERS * 8, 128)
+            hots.append(taken.astype(jnp.bfloat16))
             lows.append(col & 127)
         hot = jnp.concatenate(hots, axis=1)
         found = jnp.dot(table, hot, preferred_element_type=jnp.float32)
         for c in range(3):
             both = found[c * 128:(c + 1) * 128]
-            acc = jnp.zeros((128, 128), jnp.float32)
+            acc = jnp.zeros((8, 128), jnp.float32)
             for m in range(3):
-                acc = acc + jnp.where(
-                    within == lows[m], both[:, m * 128:(m + 1) * 128] * weights[m], 0.0
-                )
+                kept = jnp.where(within == lows[m], both[:, m * 128:(m + 1) * 128], 0.0)
+                acc = acc + weights[m] * jnp.sum(kept.reshape(16, 8, 128), axis=0)
             out_ref[c, t:t + 1, :] = jnp.sum(acc, axis=0, keepdims=True)
 
 
@@ -435,9 +480,9 @@
         return pltpu.make_async_copy(out.at[part], out_hbm.at[part], sems.at[i])
 
     def add(i, carry):
+        spread(i)
         for copy_in in keep(i):
             copy_in.wait()
-        spread(i)
         for kk in range(KB):
             k = i * KB + kk
             for h, prop in enumerate((prop0, prop1)):
@@ -490,12 +535,13 @@
 WIDE = 256
 
 
-def water_kernel(place, own_ref, one_ref, two_ref, three_ref, out_ref, whole, result):
+def water_kernel(own_ref, one_ref, two_ref, three_ref, out_ref, whole, result):
     bands = 4
     tile = own_ref.shape[1]
     width = own_ref.shape[2]
     own_cols = width - 2 * MARGIN
-    band = place[0]
+    band = lax.axis_index("band")
+    comp = lax.axis_index("comp")
     whole[...] = jnp.zeros_like(whole)
     for d, ref in enumerate((own_ref, one_ref, two_ref, three_ref)):
         row = pl.multiple_of((band ^ d) * tile, tile)
@@ -503,8 +549,8 @@
     shape = (bands * tile, WIDE)
     lane = lax.broadcasted_iota(jnp.int32, shape, 1)
     line = lax.broadcasted_iota(jnp.int32, shape, 0)
-    col = place[1] * own_cols - MARGIN + lane
-    inside = (col >= 0) & (col < place[2]) & (lane < width)
+    col = comp * own_cols - MARGIN + lane
+    inside = (col >= 0) & (col < lax.axis_size("comp") * own_cols) & (lane < width)
     first = line == 0
     last = line == shape[0] - 1
 
@@ -533,13 +579,13 @@
         out_ref[c] = result[c, pl.ds(pl.multiple_of(band * tile, tile), tile), :]
 
 
-def shallow_water(place, tiles):
+def shallow_water(tiles):
     vmem = pl.BlockSpec(memory_space=pltpu.VMEM)
     fields, rows, width = tiles[0].shape
     own_cols = width - 2 * MARGIN
     return pl.pallas_call(
         water_kernel,
-        in_specs=[pl.BlockSpec(memory_space=pltpu.SMEM)] + [vmem] * 4,
+        in_specs=[vmem] * 4,
         out_specs=vmem,
         out_shape=jax.ShapeDtypeStruct((3, rows, own_cols), jnp.float32),
         scratch_shapes=[
@@ -548,22 +594,19 @@
         ],
         compiler_params=pltpu.CompilerParams(vmem_limit_bytes=4 << 20),
         name="water",
-    )(place, *map(in_vmem, tiles))
+    )(*map(in_vmem, tiles))
 
 
 def window(spectrum, wet_mask, quad_matrix, dissipation, circulation, source_points):
     offset = lax.axis_index("comp") * LOCAL
     speed_east, speed_north, _ = component_tables(offset, LOCAL)
     speeds = jnp.stack([speed_east, speed_north])
-    wetness = wet_mask.astype(jnp.float32)[None]
-    low = jnp.concatenate([spectrum[:, :HALO], wetness[:, :HALO]], axis=0)
-    high = jnp.concatenate([spectrum[:, -HALO:], wetness[:, -HALO:]], axis=0)
+    low, high, wetness = rims(spectrum, wet_mask)
     top, bottom = from_neighbours(low, high, "band")
-    prop0, prop1, sent = propagate(speeds, spectrum, top, bottom, wetness[0])
+    prop0, prop1, sent = propagate(speeds, spectrum, top, bottom, wetness)
     received = lax.all_to_all(sent, "comp", 0, 0, tiled=True)
 
     tile_rows = circulation.shape[1]
-    tile_cols = circulation.shape[2]
     both = jnp.concatenate([circulation, source_points.astype(jnp.float32)], axis=0)
     before, after = from_neighbours(both[:, :, :MARGIN], both[:, :, -MARGIN:], "comp")
     wide = jnp.concatenate([before, both, after], axis=2)
@@ -593,10 +636,7 @@
     for d in range(1, bands):
         tiles.append(lax.ppermute(tile, "band", [(i, i ^ d) for i in range(bands)]))
     spectrum_out = finish(back, prop0, prop1)
-    place = jnp.stack(
-        [lax.axis_index("band"), lax.axis_index("comp"), tile_cols * lax.axis_size("comp")]
-    )
-    circulation_out = shallow_water(place.astype(jnp.int32), tiles)
+    circulation_out = shallow_water(tiles)
     return spectrum_out, circulation_out
 
 

time: 121 us -> 117 us (0.967)
  the two profiles are of different devices: /device:TPU:9 before, /device:TPU:1 now
where the time goes in v6:
time: 117 us; the launch traced here: 116 us
  blocking collectives  31.9 us (27%)
  Pallas kernels  30.9 us (26%)
  starting transfers between devices  27.4 us (23%)
  waiting for transfers between devices  23.2 us (20%)
    all_to_all x1, blocking collectives, window(): back = lax.all_to_all(back, 'comp', 0, 0, tiled=True)  31.9 us
    all_to_all x1, waiting for transfers between devices, window(): received = lax.all_to_all(sent, 'comp', 0, 0, tiled=True)  23.2 us
    pallas_call x1, Pallas kernels, sources(): pl.pallas_call(source_kernel, in_specs=[vmem, hbm, vmem, vmem, hbm], out_...  13.3 us
    all_to_all x1, starting transfers between devices, window(): received = lax.all_to_all(sent, 'comp', 0, 0, tiled=True)  11.8 us
    pallas_call x1, Pallas kernels, propagate(): pl.pallas_call(propagate_kernel, in_specs=[pl.BlockSpec(memory_space=pltp...  9.23 us
    ppermute x2, starting transfers between devices, from_neighbours(): lax.ppermute(high, axis, [(i, (i + 1) % count) for i in range(ends)])  8.12 us
    ppermute x3, starting transfers between devices, window(): tiles.append(lax.ppermute(tile, 'band', [(i, i ^ d) for i in range(bands)]))  4.31 us
    pallas_call x1, Pallas kernels, finish(): pl.pallas_call(finish_kernel, in_specs=[vmem, hbm, hbm], out_specs=hbm, o...  3.59 us
  transfers between devices with their start and end apart: 8, of which 1 were waited for; matrix products, arithmetic and copies ran while one was open for 1% of the time, Pallas kernels for 11%

profile of v6, /device:TPU:1, one launch (start us, length us, event | category | flops | bytes accessed | tf_op | source)
XLA Modules:
  0.0 116.1 jit_solution(17879730500448118252)
XLA Ops:
  0.6 0.0 copy-start.3
  0.6 0.0 copy-start.2
  0.7 1.1 rims.1
  1.8 4.9 %collective-permute-start = (f32[37,4,256]{2,1,0:T(4,128)S(1)}, f32[37,4,256]{2,1,0:T(4,128)S(1)}, u32[]{:S(2)}, u32[]{:S(2)}) collective-permute-start(f32[37,4,256]{2,1,0:T(4,128)S(1)} %get-tuple-element.8), channel_id=1, source_target_pairs={{0,1},{1,2},{2,3},{4,5},{5,6},{6,7},{8,9},{9,10},{10,11},{12,13},{... | collective-permute-start | bytes 454664 | tf_op jit(solution)/shard_map/ppermute | solution.py:530
  6.7 1.9 %collective-permute-start.1 = (f32[37,4,256]{2,1,0:T(4,128)S(1)}, f32[37,4,256]{2,1,0:T(4,128)S(1)}, u32[]{:S(2)}, u32[]{:S(2)}) collective-permute-start(f32[37,4,256]{2,1,0:T(4,128)S(1)} %get-tuple-element.9), channel_id=1, source_target_pairs={{1,0},{2,1},{3,2},{5,4},{6,5},{7,6},{9,8},{10,9},{11,10},{13,12},{... | collective-permute-start | bytes 454664 | tf_op jit(solution)/shard_map/ppermute | solution.py:531
  8.7 0.0 copy-done.3
  8.7 0.0 copy-done.2
  8.7 0.1 slice_maximum_fusion
  8.8 3.2 %collective-permute-start.2 = (f32[6,8,16]{2,1,0:T(8,128)S(1)}, f32[6,8,16]{2,1,0:T(8,128)S(1)}, u32[]{:S(2)}, u32[]{:S(2)}) collective-permute-start(f32[6,8,16]{2,1,0:T(8,128)S(1)} %get-tuple-element.16), channel_id=1, source_target_pairs={{0,4},{4,8},{8,12},{12,16},{16,20},{20,24},{24,28},{28,32},{32,36}... | collective-permute-start | bytes 9224 | tf_op jit(solution)/shard_map/ppermute | solution.py:530
  12.0 1.3 %collective-permute-start.3 = (f32[6,8,16]{2,1,0:T(8,128)S(1)}, f32[6,8,16]{2,1,0:T(8,128)S(1)}, u32[]{:S(2)}, u32[]{:S(2)}) collective-permute-start(f32[6,8,16]{2,1,0:T(8,128)S(1)} %get-tuple-element.17), channel_id=1, source_target_pairs={{4,0},{8,4},{12,8},{16,12},{20,16},{24,20},{28,24},{32,28},{36,32}... | collective-permute-start | bytes 9224 | tf_op jit(solution)/shard_map/ppermute | solution.py:531
  13.3 0.1 sine_multiply_fusion
  13.3 0.0 collective-permute-done.top_ref
  13.4 0.0 collective-permute-done.1.bot_ref
  13.4 9.2 %propagate.1 = (f32[3456,128]{1,0:T(8,128)}, f32[3456,128]{1,0:T(8,128)}, bf16[32,216,128]{2,1,0:T(8,128)(2,1)}) custom-call(f32[2,36]{1,0:T(2,128)S(1)} %pad_maximum_fusion.2.speeds, f32[36,96,256]{2,1,0:T(8,128)} %spec_hbm.3, f32[37,4,256]{2,1,0:T(4,128)S(1)} %collective-permute-done.top_ref, f32[37,4,256]{2,1,0:T(4,128)S(1)} %collective-permute-done.1.bot_ref, ...), custom_call_target="tpu_custom_call" | custom-call | tf_op jit(solution)/shard_map/propagate/pallas_call | solution.py:233
  22.6 0.0 copy-start.1
  22.6 11.8 %all-to-all-start = ((bf16[32,216,128]{2,1,0:T(8,128)(2,1)}), bf16[32,216,128]{2,1,0:T(8,128)(2,1)S(1)}, u32[]{:S(2)}, u32[]{:S(2)}) async-start(bf16[32,216,128]{2,1,0:T(8,128)(2,1)} %get-tuple-element.11), calls=%async_computation | async-start | bytes 3538944 | tf_op jit(solution)/shard_map/all_to_all | solution.py:607
  34.4 0.2 multiply_add_fusion.1
  34.6 0.1 pad.16.clone
  34.7 0.2 multiply_add_fusion
  34.9 0.1 maximum_maximum_fusion.coef_ref
  35.0 0.0 collective-permute-done.2
  35.0 0.1 reshape.237
  35.1 0.0 collective-permute-done.3
  35.1 0.1 reshape.238
  35.2 0.6 reshape.236.points_ref
  35.8 23.2 %all-to-all-done = bf16[32,216,128]{2,1,0:T(8,128)(2,1)S(1)} async-done(((bf16[32,216,128]{2,1,0:T(8,128)(2,1)}), bf16[32,216,128]{2,1,0:T(8,128)(2,1)S(1)}, u32[]{:S(2)}, u32[]{:S(2)}) %all-to-all-start) | async-done | bytes 1769504 | tf_op jit(solution)/shard_map/all_to_all | solution.py:607
  59.0 0.0 copy-done.1
  59.0 13.3 %sources.1 = bf16[32,240,128]{2,1,0:T(8,128)(2,1)} custom-call(bf16[6912,128]{1,0:T(8,128)(2,1)S(1)} %bitcast.2, bf16[1152,1152]{1,0:T(8,128)(2,1)} %quad_hbm.1, f32[9,128]{1,0:T(8,128)S(1)} %bitcast.3, bf16[16,1152]{1,0:T(8,128)(2,1)S(1)} %maximum_maximum_fusion.coef_ref, s32[30,128]{1,0:T(8,128)} %reshape.236.points_ref), custom_call_target="tpu_custom_call" | custom-call | tf_op jit(solution)/shard_map/sources/pallas_call | solution.py:385
  72.3 0.0 copy-start
  72.3 31.9 %all_to_all.10.back_ref = bf16[32,240,128]{2,1,0:T(8,128)(2,1)S(1)} all-to-all(bf16[32,240,128]{2,1,0:T(8,128)(2,1)} %sources.1), channel_id=1, replica_groups=mesh['comp'=32,'band'=4] {'comp'}, dimensions={0} | all-to-all | bytes 3932160 | tf_op jit(solution)/shard_map/all_to_all | solution.py:627
  104.2 0.0 copy-done
  104.2 1.6 %pick.1 = f32[3,10,128]{2,1,0:T(8,128)S(1)} custom-call(bf16[32,240,128]{2,1,0:T(8,128)(2,1)S(1)} %all_to_all.10.back_ref, s32[30,128]{1,0:T(8,128)S(1)} %copy-done), custom_call_target="tpu_custom_call" | custom-call | tf_op jit(solution)/shard_map/pick/pallas_call | solution.py:444
  105.8 0.1 reshape_squeeze.6
  105.9 0.1 reshape_squeeze.7
  106.0 0.1 fusion.own_ref
  106.1 2.6 %collective-permute-start.4 = (f32[6,8,160]{2,1,0:T(8,128)S(1)}, f32[6,8,160]{2,1,0:T(8,128)S(1)}, u32[]{:S(2)}, u32[]{:S(2)}) collective-permute-start(f32[6,8,160]{2,1,0:T(8,128)S(1)} %fusion.own_ref), channel_id=1, source_target_pairs={{0,1},{1,0},{2,3},{3,2},{4,5},{5,4},{6,7},{7,6},{8,9},{9,8},{10,11... | collective-permute-start | bytes 92168 | tf_op jit(solution)/shard_map/ppermute | solution.py:637
  108.7 0.0 collective-permute-start.5
  108.7 1.7 %collective-permute-start.6 = (f32[6,8,160]{2,1,0:T(8,128)S(1)}, f32[6,8,160]{2,1,0:T(8,128)S(1)}, u32[]{:S(2)}, u32[]{:S(2)}) collective-permute-start(f32[6,8,160]{2,1,0:T(8,128)S(1)} %fusion.own_ref), channel_id=1, source_target_pairs={{0,3},{1,2},{2,1},{3,0},{4,7},{5,6},{6,5},{7,4},{8,11},{9,10},{10,... | collective-permute-start | bytes 92168 | tf_op jit(solution)/shard_map/ppermute | solution.py:637
  110.4 3.6 %finish.1 = f32[36,96,256]{2,1,0:T(8,128)} custom-call(bf16[32,240,128]{2,1,0:T(8,128)(2,1)S(1)} %all_to_all.10.back_ref, f32[3456,128]{1,0:T(8,128)} %get-tuple-element.12.prop0_hbm, f32[3456,128]{1,0:T(8,128)} %get-tuple-element.13.prop1_hbm), custom_call_target="tpu_custom_call" | custom-call | tf_op jit(solution)/shard_map/finish/pallas_call | solution.py:509
  114.0 0.0 collective-permute-done.4.one_ref
  114.0 0.0 collective-permute-done.5.two_ref
  114.0 0.0 collective-permute-done.6.three_ref
  114.0 2.1 %water.1 = f32[3,8,128]{2,1,0:T(8,128)} custom-call(f32[6,8,160]{2,1,0:T(8,128)S(1)} %fusion.own_ref, f32[6,8,160]{2,1,0:T(8,128)S(1)} %collective-permute-done.4.one_ref, f32[6,8,160]{2,1,0:T(8,128)S(1)} %collective-permute-done.5.two_ref, f32[6,8,160]{2,1,0:T(8,128)S(1)} %collective-permute-done.6.three_ref), custom_call_target="tpu_custom_call" | custom-call | tf_op jit(solution)/shard_map/water/pallas_call | solution.py:586
  (10 shorter events, 0.1 us)
Async XLA Ops:
  0.6 8.0 %copy-start.3 = (s32[3,8,128]{2,1,0:T(8,128)S(1)}, s32[3,8,128]{2,1,0:T(8,128)}, u32[]{:S(2)}) copy-start(s32[3,8,128]{2,1,0:T(8,128)} %param.11) | copy-start | bytes 36868
  0.6 8.0 %copy-start.2 = (f32[3,8,128]{2,1,0:T(8,128)S(1)}, f32[3,8,128]{2,1,0:T(8,128)}, u32[]{:S(2)}) copy-start(f32[3,8,128]{2,1,0:T(8,128)} %param.10) | copy-start | bytes 36868
  1.8 11.5 %collective-permute-start = (f32[37,4,256]{2,1,0:T(4,128)S(1)}, f32[37,4,256]{2,1,0:T(4,128)S(1)}, u32[]{:S(2)}, u32[]{:S(2)}) collective-permute-start(f32[37,4,256]{2,1,0:T(4,128)S(1)} %get-tuple-element.8), channel_id=1, source_target_pairs={{0,1},{1,2},{2,3},{4,5},{5,6},{6,7},{8,9},{9,10},{10,11},{12,13},{... | collective-permute-start | bytes 454664 | tf_op jit(solution)/shard_map/ppermute | solution.py:530
  6.7 6.6 %collective-permute-start.1 = (f32[37,4,256]{2,1,0:T(4,128)S(1)}, f32[37,4,256]{2,1,0:T(4,128)S(1)}, u32[]{:S(2)}, u32[]{:S(2)}) collective-permute-start(f32[37,4,256]{2,1,0:T(4,128)S(1)} %get-tuple-element.9), channel_id=1, source_target_pairs={{1,0},{2,1},{3,2},{5,4},{6,5},{7,6},{9,8},{10,9},{11,10},{13,12},{... | collective-permute-start | bytes 454664 | tf_op jit(solution)/shard_map/ppermute | solution.py:531
  8.8 26.2 %collective-permute-start.2 = (f32[6,8,16]{2,1,0:T(8,128)S(1)}, f32[6,8,16]{2,1,0:T(8,128)S(1)}, u32[]{:S(2)}, u32[]{:S(2)}) collective-permute-start(f32[6,8,16]{2,1,0:T(8,128)S(1)} %get-tuple-element.16), channel_id=1, source_target_pairs={{0,4},{4,8},{8,12},{12,16},{16,20},{20,24},{24,28},{28,32},{32,36}... | collective-permute-start | bytes 9224 | tf_op jit(solution)/shard_map/ppermute | solution.py:530
  12.0 23.1 %collective-permute-start.3 = (f32[6,8,16]{2,1,0:T(8,128)S(1)}, f32[6,8,16]{2,1,0:T(8,128)S(1)}, u32[]{:S(2)}, u32[]{:S(2)}) collective-permute-start(f32[6,8,16]{2,1,0:T(8,128)S(1)} %get-tuple-element.17), channel_id=1, source_target_pairs={{4,0},{8,4},{12,8},{16,12},{20,16},{24,20},{28,24},{32,28},{36,32}... | collective-permute-start | bytes 9224 | tf_op jit(solution)/shard_map/ppermute | solution.py:531
  22.6 36.4 %copy-start.1 = (f32[1152]{0:T(1024)S(1)}, f32[1152]{0:T(1024)}, u32[]{:S(2)}) copy-start(f32[1152]{0:T(1024)} %param.9) | copy-start | bytes 13828
  22.6 36.4 %all-to-all-start = ((bf16[32,216,128]{2,1,0:T(8,128)(2,1)}), bf16[32,216,128]{2,1,0:T(8,128)(2,1)S(1)}, u32[]{:S(2)}, u32[]{:S(2)}) async-start(bf16[32,216,128]{2,1,0:T(8,128)(2,1)} %get-tuple-element.11), calls=%async_computation | async-start | bytes 3538944 | tf_op jit(solution)/shard_map/all_to_all | solution.py:607
  72.3 32.0 %copy-start = (s32[30,128]{1,0:T(8,128)S(1)}, s32[30,128]{1,0:T(8,128)}, u32[]{:S(2)}) copy-start(s32[30,128]{1,0:T(8,128)} %reshape.236.points_ref) | copy-start | bytes 46084
  106.1 7.9 %collective-permute-start.4 = (f32[6,8,160]{2,1,0:T(8,128)S(1)}, f32[6,8,160]{2,1,0:T(8,128)S(1)}, u32[]{:S(2)}, u32[]{:S(2)}) collective-permute-start(f32[6,8,160]{2,1,0:T(8,128)S(1)} %fusion.own_ref), channel_id=1, source_target_pairs={{0,1},{1,0},{2,3},{3,2},{4,5},{5,4},{6,7},{7,6},{8,9},{9,8},{10,11... | collective-permute-start | bytes 92168 | tf_op jit(solution)/shard_map/ppermute | solution.py:637
  108.7 5.3 %collective-permute-start.5 = (f32[6,8,160]{2,1,0:T(8,128)S(1)}, f32[6,8,160]{2,1,0:T(8,128)S(1)}, u32[]{:S(2)}, u32[]{:S(2)}) collective-permute-start(f32[6,8,160]{2,1,0:T(8,128)S(1)} %fusion.own_ref), channel_id=1, source_target_pairs={{0,2},{1,3},{2,0},{3,1},{4,6},{5,7},{6,4},{7,5},{8,10},{9,11},{10,... | collective-permute-start | bytes 92168 | tf_op jit(solution)/shard_map/ppermute | solution.py:637
  108.7 5.3 %collective-permute-start.6 = (f32[6,8,160]{2,1,0:T(8,128)S(1)}, f32[6,8,160]{2,1,0:T(8,128)S(1)}, u32[]{:S(2)}, u32[]{:S(2)}) collective-permute-start(f32[6,8,160]{2,1,0:T(8,128)S(1)} %fusion.own_ref), channel_id=1, source_target_pairs={{0,3},{1,2},{2,1},{3,0},{4,7},{5,6},{6,5},{7,4},{8,11},{9,10},{10,... | collective-permute-start | bytes 92168 | tf_op jit(solution)/shard_map/ppermute | solution.py:637

commit v7 on v6

--- a/solution.py
+++ b/solution.py
@@ -264,7 +264,7 @@
 
 
 def source_kernel(
-    recv_ref, quad_hbm, diss_ref, coef_ref, points_ref, back_hbm,
+    recv_ref, quad_hbm, diss_ref, coef_ref, back_hbm,
     quad_ref, back_ref, prod_a, prod_b, flat, cur, xa, xb, rate, level, quad_sems, out_sem,
 ):
     halves = K // MB
@@ -378,13 +378,13 @@
     pltpu.make_async_copy(back_ref, back_hbm, out_sem).wait()
 
 
-def sources(received, quad_matrix, rates, coef, points_list):
+def sources(received, quad_matrix, rates, coef):
     points = RUN * 128
     vmem = pl.BlockSpec(memory_space=pltpu.VMEM)
     hbm = pl.BlockSpec(memory_space=pltpu.HBM)
     return pl.pallas_call(
         source_kernel,
-        in_specs=[vmem, hbm, vmem, vmem, hbm],
+        in_specs=[vmem, hbm, vmem, vmem],
         out_specs=hbm,
         out_shape=pltpu.HBM((OWNERS, BACK_ROWS, 128), jnp.bfloat16),
         scratch_shapes=[
@@ -403,7 +403,7 @@
         ],
         compiler_params=pltpu.CompilerParams(vmem_limit_bytes=30 << 20),
         name="sources",
-    )(in_vmem(received), in_hbm(quad_matrix), in_vmem(rates), in_vmem(coef), in_hbm(points_list))
+    )(in_vmem(received), in_hbm(quad_matrix), in_vmem(rates), in_vmem(coef))
 
 
 def pick_kernel(back_ref, points_ref, out_ref):
@@ -622,7 +622,7 @@
     spare = jnp.zeros((7, K), jnp.float32)
     coef = jnp.concatenate([coef_high, coef_mid, coef_low, spare]).astype(jnp.bfloat16)
     back = sources(
-        received.reshape(K * RUN, 128), quad_matrix, dissipation.reshape(K // 128, 128), coef, points
+        received.reshape(K * RUN, 128), quad_matrix, dissipation.reshape(K // 128, 128), coef
     )
     back = lax.all_to_all(back, "comp", 0, 0, tiled=True)
     cells = pick(back, points)

time: 117 us -> 113 us (0.966)
  the two profiles are of different devices: /device:TPU:1 before, /device:TPU:6 now
where the time goes in v7:
time: 113 us; the launch traced here: 111 us
  waiting for transfers between devices  43.7 us (39%)
  starting transfers between devices  34.8 us (31%)
  Pallas kernels  30.9 us (27%)
    all_to_all x1, waiting for transfers between devices, window(): received = lax.all_to_all(sent, 'comp', 0, 0, tiled=True)  21.3 us
    ppermute x2, waiting for transfers between devices, from_neighbours(): after = lax.ppermute(low, axis, [((i + 1) % count, i) for i in range(ends)])  18.1 us
    pallas_call x1, Pallas kernels, sources(): pl.pallas_call(source_kernel, in_specs=[vmem, hbm, vmem, vmem], out_specs...  13.3 us
    all_to_all x1, starting transfers between devices, window(): received = lax.all_to_all(sent, 'comp', 0, 0, tiled=True)  10.6 us
    all_to_all x1, starting transfers between devices, window(): back = lax.all_to_all(back, 'comp', 0, 0, tiled=True)  9.8 us
    pallas_call x1, Pallas kernels, propagate(): pl.pallas_call(propagate_kernel, in_specs=[pl.BlockSpec(memory_space=pltp...  9.22 us
    ppermute x2, starting transfers between devices, from_neighbours(): after = lax.ppermute(low, axis, [((i + 1) % count, i) for i in range(ends)])  8.56 us
    ppermute x2, waiting for transfers between devices, from_neighbours(): lax.ppermute(high, axis, [(i, (i + 1) % count) for i in range(ends)])  4.23 us
  transfers between devices with their start and end apart: 9, of which 4 were waited for; matrix products, arithmetic and copies ran while one was open for 1% of the time, Pallas kernels for 3%

profile of v7, /device:TPU:6, one launch (start us, length us, event | category | flops | bytes accessed | tf_op | source)
XLA Modules:
  0.0 111.4 jit_solution(12390935351503793156)
XLA Ops:
  0.6 1.1 %rims.1 = (f32[37,4,256]{2,1,0:T(4,128)S(1)}, f32[37,4,256]{2,1,0:T(4,128)S(1)}, f32[96,256]{1,0:T(8,128)S(1)}) custom-call(f32[36,96,256]{2,1,0:T(8,128)} %spec_hbm.3, s32[96,256]{1,0:T(8,128)} %wet_hbm.1), custom_call_target="tpu_custom_call" | custom-call | tf_op jit(solution)/shard_map/rims/pallas_call | solution.py:88
  1.8 1.7 %collective-permute-start = (f32[37,4,256]{2,1,0:T(4,128)S(1)}, f32[37,4,256]{2,1,0:T(4,128)S(1)}, u32[]{:S(2)}, u32[]{:S(2)}) collective-permute-start(f32[37,4,256]{2,1,0:T(4,128)S(1)} %get-tuple-element.8), channel_id=1, source_target_pairs={{0,1},{1,2},{2,3},{4,5},{5,6},{6,7},{8,9},{9,10},{10,11},{12,13},{... | collective-permute-start | bytes 454664 | tf_op jit(solution)/shard_map/ppermute | solution.py:530
  3.5 1.3 %collective-permute-start.1 = (f32[37,4,256]{2,1,0:T(4,128)S(1)}, f32[37,4,256]{2,1,0:T(4,128)S(1)}, u32[]{:S(2)}, u32[]{:S(2)}) collective-permute-start(f32[37,4,256]{2,1,0:T(4,128)S(1)} %get-tuple-element.9), channel_id=1, source_target_pairs={{1,0},{2,1},{3,2},{5,4},{6,5},{7,6},{9,8},{10,9},{11,10},{13,12},{... | collective-permute-start | bytes 454664 | tf_op jit(solution)/shard_map/ppermute | solution.py:531
  4.8 0.1 sine_multiply_fusion
  4.9 0.0 collective-permute-done.top_ref
  4.9 3.6 %collective-permute-done.1.bot_ref = f32[37,4,256]{2,1,0:T(4,128)S(1)} collective-permute-done((f32[37,4,256]{2,1,0:T(4,128)S(1)}, f32[37,4,256]{2,1,0:T(4,128)S(1)}, u32[]{:S(2)}, u32[]{:S(2)}) %collective-permute-start.1) | collective-permute-done | bytes 151584 | tf_op jit(solution)/shard_map/ppermute | solution.py:531
  8.5 9.2 %propagate.1 = (f32[3456,128]{1,0:T(8,128)}, f32[3456,128]{1,0:T(8,128)}, bf16[32,216,128]{2,1,0:T(8,128)(2,1)}) custom-call(f32[2,36]{1,0:T(2,128)S(1)} %pad_maximum_fusion.2.speeds, f32[36,96,256]{2,1,0:T(8,128)} %spec_hbm.3, f32[37,4,256]{2,1,0:T(4,128)S(1)} %collective-permute-done.top_ref, f32[37,4,256]{2,1,0:T(4,128)S(1)} %collective-permute-done.1.bot_ref, ...), custom_call_target="tpu_custom_call" | custom-call | tf_op jit(solution)/shard_map/propagate/pallas_call | solution.py:233
  17.7 0.0 copy-start
  17.7 10.6 %all-to-all-start = ((bf16[32,216,128]{2,1,0:T(8,128)(2,1)}), bf16[32,216,128]{2,1,0:T(8,128)(2,1)S(1)}, u32[]{:S(2)}, u32[]{:S(2)}) async-start(bf16[32,216,128]{2,1,0:T(8,128)(2,1)} %get-tuple-element.11), calls=%async_computation | async-start | bytes 3538944 | tf_op jit(solution)/shard_map/all_to_all | solution.py:607
  28.4 0.1 pad.16.clone
  28.5 0.2 multiply_add_fusion.1
  28.6 0.2 multiply_add_fusion
  28.9 0.1 maximum_maximum_fusion.coef_ref
  28.9 21.3 %all-to-all-done = bf16[32,216,128]{2,1,0:T(8,128)(2,1)S(1)} async-done(((bf16[32,216,128]{2,1,0:T(8,128)(2,1)}), bf16[32,216,128]{2,1,0:T(8,128)(2,1)S(1)}, u32[]{:S(2)}, u32[]{:S(2)}) %all-to-all-start) | async-done | bytes 1769504 | tf_op jit(solution)/shard_map/all_to_all | solution.py:607
  50.3 0.0 copy-done
  50.3 13.3 %sources.1 = bf16[32,240,128]{2,1,0:T(8,128)(2,1)} custom-call(bf16[6912,128]{1,0:T(8,128)(2,1)S(1)} %bitcast.2, bf16[1152,1152]{1,0:T(8,128)(2,1)} %quad_hbm.1, f32[9,128]{1,0:T(8,128)S(1)} %bitcast.3, bf16[16,1152]{1,0:T(8,128)(2,1)S(1)} %maximum_maximum_fusion.coef_ref), custom_call_target="tpu_custom_call" | custom-call | tf_op jit(solution)/shard_map/sources/pallas_call | solution.py:385
  63.6 0.0 copy-start.2
  63.6 0.0 copy-start.1
  63.6 9.8 %all-to-all-start.1 = ((bf16[32,240,128]{2,1,0:T(8,128)(2,1)}), bf16[32,240,128]{2,1,0:T(8,128)(2,1)S(1)}, u32[]{:S(2)}, u32[]{:S(2)}) async-start(bf16[32,240,128]{2,1,0:T(8,128)(2,1)} %sources.1), calls=%async_computation.1 | async-start | bytes 3932160 | tf_op jit(solution)/shard_map/all_to_all | solution.py:627
  73.4 0.0 copy-done.2
  73.4 0.0 copy-done.1
  73.4 0.1 slice_maximum_fusion
  73.5 7.3 %collective-permute-start.3 = (f32[6,8,16]{2,1,0:T(8,128)S(1)}, f32[6,8,16]{2,1,0:T(8,128)S(1)}, u32[]{:S(2)}, u32[]{:S(2)}) collective-permute-start(f32[6,8,16]{2,1,0:T(8,128)S(1)} %get-tuple-element.17), channel_id=1, source_target_pairs={{4,0},{8,4},{12,8},{16,12},{20,16},{24,20},{28,24},{32,28},{36,32}... | collective-permute-start | bytes 9224 | tf_op jit(solution)/shard_map/ppermute | solution.py:531
  80.8 2.1 %collective-permute-start.2 = (f32[6,8,16]{2,1,0:T(8,128)S(1)}, f32[6,8,16]{2,1,0:T(8,128)S(1)}, u32[]{:S(2)}, u32[]{:S(2)}) collective-permute-start(f32[6,8,16]{2,1,0:T(8,128)S(1)} %get-tuple-element.16), channel_id=1, source_target_pairs={{0,4},{4,8},{8,12},{12,16},{16,20},{20,24},{24,28},{28,32},{32,36}... | collective-permute-start | bytes 9224 | tf_op jit(solution)/shard_map/ppermute | solution.py:530
  82.9 14.6 %collective-permute-done.3 = f32[6,8,16]{2,1,0:T(8,128)S(1)} collective-permute-done((f32[6,8,16]{2,1,0:T(8,128)S(1)}, f32[6,8,16]{2,1,0:T(8,128)S(1)}, u32[]{:S(2)}, u32[]{:S(2)}) %collective-permute-start.3) | collective-permute-done | bytes 3104 | tf_op jit(solution)/shard_map/ppermute | solution.py:531
  97.4 0.1 reshape.238
  97.5 4.2 %collective-permute-done.2 = f32[6,8,16]{2,1,0:T(8,128)S(1)} collective-permute-done((f32[6,8,16]{2,1,0:T(8,128)S(1)}, f32[6,8,16]{2,1,0:T(8,128)S(1)}, u32[]{:S(2)}, u32[]{:S(2)}) %collective-permute-start.2) | collective-permute-done | bytes 3104 | tf_op jit(solution)/shard_map/ppermute | solution.py:530
  101.8 0.1 reshape.237
  101.9 0.0 all-to-all-done.1.back_ref
  101.9 1.5 %pick.1 = f32[3,10,128]{2,1,0:T(8,128)S(1)} custom-call(bf16[32,240,128]{2,1,0:T(8,128)(2,1)S(1)} %all-to-all-done.1.back_ref, s32[30,128]{1,0:T(8,128)S(1)} %reshape.236.points_ref), custom_call_target="tpu_custom_call" | custom-call | tf_op jit(solution)/shard_map/pick/pallas_call | solution.py:444
  103.5 0.1 reshape_squeeze.7
  103.5 0.1 reshape_squeeze.6
  103.6 0.1 fusion.own_ref
  103.7 0.1 collective-permute-start.4
  103.8 0.1 collective-permute-start.5
  103.9 1.8 %collective-permute-start.6 = (f32[6,8,160]{2,1,0:T(8,128)S(1)}, f32[6,8,160]{2,1,0:T(8,128)S(1)}, u32[]{:S(2)}, u32[]{:S(2)}) collective-permute-start(f32[6,8,160]{2,1,0:T(8,128)S(1)} %fusion.own_ref), channel_id=1, source_target_pairs={{0,3},{1,2},{2,1},{3,0},{4,7},{5,6},{6,5},{7,4},{8,11},{9,10},{10,... | collective-permute-start | bytes 92168 | tf_op jit(solution)/shard_map/ppermute | solution.py:637
  105.7 3.6 %finish.1 = f32[36,96,256]{2,1,0:T(8,128)} custom-call(bf16[32,240,128]{2,1,0:T(8,128)(2,1)S(1)} %all-to-all-done.1.back_ref, f32[3456,128]{1,0:T(8,128)} %get-tuple-element.12.prop0_hbm, f32[3456,128]{1,0:T(8,128)} %get-tuple-element.13.prop1_hbm), custom_call_target="tpu_custom_call" | custom-call | tf_op jit(solution)/shard_map/finish/pallas_call | solution.py:509
  109.3 0.0 collective-permute-done.4.one_ref
  109.3 0.0 collective-permute-done.5.two_ref
  109.3 0.0 collective-permute-done.6.three_ref
  109.3 2.1 %water.1 = f32[3,8,128]{2,1,0:T(8,128)} custom-call(f32[6,8,160]{2,1,0:T(8,128)S(1)} %fusion.own_ref, f32[6,8,160]{2,1,0:T(8,128)S(1)} %collective-permute-done.4.one_ref, f32[6,8,160]{2,1,0:T(8,128)S(1)} %collective-permute-done.5.two_ref, f32[6,8,160]{2,1,0:T(8,128)S(1)} %collective-permute-done.6.three_ref), custom_call_target="tpu_custom_call" | custom-call | tf_op jit(solution)/shard_map/water/pallas_call | solution.py:586
  (11 shorter events, 0.1 us)
Async XLA Ops:
  1.8 3.1 %collective-permute-start = (f32[37,4,256]{2,1,0:T(4,128)S(1)}, f32[37,4,256]{2,1,0:T(4,128)S(1)}, u32[]{:S(2)}, u32[]{:S(2)}) collective-permute-start(f32[37,4,256]{2,1,0:T(4,128)S(1)} %get-tuple-element.8), channel_id=1, source_target_pairs={{0,1},{1,2},{2,3},{4,5},{5,6},{6,7},{8,9},{9,10},{10,11},{12,13},{... | collective-permute-start | bytes 454664 | tf_op jit(solution)/shard_map/ppermute | solution.py:530
  3.5 5.0 %collective-permute-start.1 = (f32[37,4,256]{2,1,0:T(4,128)S(1)}, f32[37,4,256]{2,1,0:T(4,128)S(1)}, u32[]{:S(2)}, u32[]{:S(2)}) collective-permute-start(f32[37,4,256]{2,1,0:T(4,128)S(1)} %get-tuple-element.9), channel_id=1, source_target_pairs={{1,0},{2,1},{3,2},{5,4},{6,5},{7,6},{9,8},{10,9},{11,10},{13,12},{... | collective-permute-start | bytes 454664 | tf_op jit(solution)/shard_map/ppermute | solution.py:531
  17.7 32.5 %copy-start = (f32[1152]{0:T(1024)S(1)}, f32[1152]{0:T(1024)}, u32[]{:S(2)}) copy-start(f32[1152]{0:T(1024)} %param.9) | copy-start | bytes 13828
  17.7 32.5 %all-to-all-start = ((bf16[32,216,128]{2,1,0:T(8,128)(2,1)}), bf16[32,216,128]{2,1,0:T(8,128)(2,1)S(1)}, u32[]{:S(2)}, u32[]{:S(2)}) async-start(bf16[32,216,128]{2,1,0:T(8,128)(2,1)} %get-tuple-element.11), calls=%async_computation | async-start | bytes 3538944 | tf_op jit(solution)/shard_map/all_to_all | solution.py:607
  63.6 9.8 %copy-start.2 = (s32[3,8,128]{2,1,0:T(8,128)S(1)}, s32[3,8,128]{2,1,0:T(8,128)}, u32[]{:S(2)}) copy-start(s32[3,8,128]{2,1,0:T(8,128)} %param.11) | copy-start | bytes 36868
  63.6 9.8 %copy-start.1 = (f32[3,8,128]{2,1,0:T(8,128)S(1)}, f32[3,8,128]{2,1,0:T(8,128)}, u32[]{:S(2)}) copy-start(f32[3,8,128]{2,1,0:T(8,128)} %param.10) | copy-start | bytes 36868
  63.6 38.3 %all-to-all-start.1 = ((bf16[32,240,128]{2,1,0:T(8,128)(2,1)}), bf16[32,240,128]{2,1,0:T(8,128)(2,1)S(1)}, u32[]{:S(2)}, u32[]{:S(2)}) async-start(bf16[32,240,128]{2,1,0:T(8,128)(2,1)} %sources.1), calls=%async_computation.1 | async-start | bytes 3932160 | tf_op jit(solution)/shard_map/all_to_all | solution.py:627
  73.5 23.9 %collective-permute-start.3 = (f32[6,8,16]{2,1,0:T(8,128)S(1)}, f32[6,8,16]{2,1,0:T(8,128)S(1)}, u32[]{:S(2)}, u32[]{:S(2)}) collective-permute-start(f32[6,8,16]{2,1,0:T(8,128)S(1)} %get-tuple-element.17), channel_id=1, source_target_pairs={{4,0},{8,4},{12,8},{16,12},{20,16},{24,20},{28,24},{32,28},{36,32}... | collective-permute-start | bytes 9224 | tf_op jit(solution)/shard_map/ppermute | solution.py:531
  80.8 21.0 %collective-permute-start.2 = (f32[6,8,16]{2,1,0:T(8,128)S(1)}, f32[6,8,16]{2,1,0:T(8,128)S(1)}, u32[]{:S(2)}, u32[]{:S(2)}) collective-permute-start(f32[6,8,16]{2,1,0:T(8,128)S(1)} %get-tuple-element.16), channel_id=1, source_target_pairs={{0,4},{4,8},{8,12},{12,16},{16,20},{20,24},{24,28},{28,32},{32,36}... | collective-permute-start | bytes 9224 | tf_op jit(solution)/shard_map/ppermute | solution.py:530
  103.7 5.5 %collective-permute-start.4 = (f32[6,8,160]{2,1,0:T(8,128)S(1)}, f32[6,8,160]{2,1,0:T(8,128)S(1)}, u32[]{:S(2)}, u32[]{:S(2)}) collective-permute-start(f32[6,8,160]{2,1,0:T(8,128)S(1)} %fusion.own_ref), channel_id=1, source_target_pairs={{0,1},{1,0},{2,3},{3,2},{4,5},{5,4},{6,7},{7,6},{8,9},{9,8},{10,11... | collective-permute-start | bytes 92168 | tf_op jit(solution)/shard_map/ppermute | solution.py:637
  103.8 5.5 %collective-permute-start.5 = (f32[6,8,160]{2,1,0:T(8,128)S(1)}, f32[6,8,160]{2,1,0:T(8,128)S(1)}, u32[]{:S(2)}, u32[]{:S(2)}) collective-permute-start(f32[6,8,160]{2,1,0:T(8,128)S(1)} %fusion.own_ref), channel_id=1, source_target_pairs={{0,2},{1,3},{2,0},{3,1},{4,6},{5,7},{6,4},{7,5},{8,10},{9,11},{10,... | collective-permute-start | bytes 92168 | tf_op jit(solution)/shard_map/ppermute | solution.py:637
  103.9 5.4 %collective-permute-start.6 = (f32[6,8,160]{2,1,0:T(8,128)S(1)}, f32[6,8,160]{2,1,0:T(8,128)S(1)}, u32[]{:S(2)}, u32[]{:S(2)}) collective-permute-start(f32[6,8,160]{2,1,0:T(8,128)S(1)} %fusion.own_ref), channel_id=1, source_target_pairs={{0,3},{1,2},{2,1},{3,0},{4,7},{5,6},{6,5},{7,4},{8,11},{9,10},{10,... | collective-permute-start | bytes 92168 | tf_op jit(solution)/shard_map/ppermute | solution.py:637

commit v8 on v7

--- a/solution.py
+++ b/solution.py
@@ -62,11 +62,12 @@
     return pltpu.with_memory_space_constraint(array, pltpu.VMEM)
 
 
-def rim_kernel(spec_hbm, wet_hbm, low_ref, high_ref, wet_ref, head, tail, mask, sems):
+def rim_kernel(spec_hbm, wet_hbm, low_ref, high_ref, wet_ref, begin_ref, head, tail, mask, sems):
     copies = (
         pltpu.make_async_copy(spec_hbm.at[:, 0:8, :], head, sems.at[0]),
         pltpu.make_async_copy(spec_hbm.at[:, ROWS - 8:ROWS, :], tail, sems.at[1]),
         pltpu.make_async_copy(wet_hbm, mask, sems.at[2]),
+        pltpu.make_async_copy(spec_hbm.at[0:KB], begin_ref, sems.at[3]),
     )
     for copy in copies:
         copy.start()
@@ -79,6 +80,7 @@
     low_ref[0:LOCAL] = head[:, 0:HALO, :]
     copies[1].wait()
     high_ref[0:LOCAL] = tail[:, 8 - HALO:8, :]
+    copies[3].wait()
 
 
 def rims(spectrum, wet_mask):
@@ -88,17 +90,18 @@
     return pl.pallas_call(
         rim_kernel,
         in_specs=[hbm] * 2,
-        out_specs=[vmem] * 3,
+        out_specs=[vmem] * 4,
         out_shape=[
             pltpu.VMEM((LOCAL + 1, HALO, cols), jnp.float32),
             pltpu.VMEM((LOCAL + 1, HALO, cols), jnp.float32),
             pltpu.VMEM((ROWS, cols), jnp.float32),
+            pltpu.VMEM((KB, ROWS, cols), jnp.float32),
         ],
         scratch_shapes=[
             pltpu.VMEM((LOCAL, 8, cols), jnp.float32),
             pltpu.VMEM((LOCAL, 8, cols), jnp.float32),
             pltpu.VMEM((ROWS, cols), jnp.int32),
-            pltpu.SemaphoreType.DMA((3,)),
+            pltpu.SemaphoreType.DMA((4,)),
         ],
         compiler_params=pltpu.CompilerParams(vmem_limit_bytes=4 << 20),
         name="rims",
@@ -106,7 +109,7 @@
 
 
 def propagate_kernel(
-    speeds, spec_hbm, top_ref, bot_ref, wet_ref, prop0_hbm, prop1_hbm, sent_hbm,
+    speeds, spec_hbm, top_ref, bot_ref, wet_ref, begin_ref, prop0_hbm, prop1_hbm, sent_hbm,
     spec_ref, load_sems, prop0, prop1, sent_ref, wet, left_a, right_a, left_b, right_b, keep_sems, sent_sems,
 ):
     ext = ROWS + 2 * HALO
@@ -136,7 +139,8 @@
         load(i).start()
         return carry
 
-    lax.fori_loop(0, LOCAL // KB, start_load, 0)
+    lax.fori_loop(1, LOCAL // KB, start_load, 0)
+    spec_ref[0:KB] = begin_ref[...]
     wet[0:ROWS, :] = wet_ref[...]
     wet[ROWS:ROWS + HALO, :] = bot_ref[LOCAL]
     wet[ROWS + HALO:ext, :] = top_ref[LOCAL]
@@ -205,7 +209,10 @@
         return carry
 
     def block(i, carry):
-        load(i).wait()
+        @pl.when(i > 0)
+        def _():
+            load(i).wait()
+
         some(i, 0)
         regroup(i)
         give(i).start()
@@ -225,14 +232,14 @@
     lax.fori_loop(0, count, settle, 0)
 
 
-def propagate(speeds, spectrum, top, bottom, wetness):
+def propagate(speeds, spectrum, top, bottom, wetness, begin):
     cols = spectrum.shape[2]
     ext = ROWS + 2 * HALO
     vmem = pl.BlockSpec(memory_space=pltpu.VMEM)
     hbm = pl.BlockSpec(memory_space=pltpu.HBM)
     return pl.pallas_call(
         propagate_kernel,
-        in_specs=[pl.BlockSpec(memory_space=pltpu.SMEM), hbm] + [vmem] * 3,
+        in_specs=[pl.BlockSpec(memory_space=pltpu.SMEM), hbm] + [vmem] * 4,
         out_specs=[hbm] * 3,
         out_shape=[
             pltpu.HBM((LOCAL * ROWS, 128), jnp.float32),
@@ -251,7 +258,7 @@
         + [pltpu.SemaphoreType.DMA((2, LOCAL // KB)), pltpu.SemaphoreType.DMA((LOCAL // KB,))],
         compiler_params=pltpu.CompilerParams(vmem_limit_bytes=16 << 20),
         name="propagate",
-    )(pltpu.with_memory_space_constraint(speeds, pltpu.SMEM), in_hbm(spectrum), *map(in_vmem, (top, bottom, wetness)))
+    )(pltpu.with_memory_space_constraint(speeds, pltpu.SMEM), in_hbm(spectrum), *map(in_vmem, (top, bottom, wetness, begin)))
 
 
 MB = 576
@@ -601,9 +608,9 @@
     offset = lax.axis_index("comp") * LOCAL
     speed_east, speed_north, _ = component_tables(offset, LOCAL)
     speeds = jnp.stack([speed_east, speed_north])
-    low, high, wetness = rims(spectrum, wet_mask)
+    low, high, wetness, begin = rims(spectrum, wet_mask)
     top, bottom = from_neighbours(low, high, "band")
-    prop0, prop1, sent = propagate(speeds, spectrum, top, bottom, wetness)
+    prop0, prop1, sent = propagate(speeds, spectrum, top, bottom, wetness, begin)
     received = lax.all_to_all(sent, "comp", 0, 0, tiled=True)
 
     tile_rows = circulation.shape[1]

time: 113 us -> 113 us (level)
  no operation moved by 1% of the time
where the time goes in v8:
time: 113 us; the launch traced here: 111 us
  waiting for transfers between devices  43.7 us (39%)
  starting transfers between devices  34.8 us (31%)
  Pallas kernels  30.3 us (27%)
    all_to_all x1, waiting for transfers between devices, window(): received = lax.all_to_all(sent, 'comp', 0, 0, tiled=True)  21.3 us
    ppermute x2, waiting for transfers between devices, from_neighbours(): after = lax.ppermute(low, axis, [((i + 1) % count, i) for i in range(ends)])  18.1 us
    pallas_call x1, Pallas kernels, sources(): pl.pallas_call(source_kernel, in_specs=[vmem, hbm, vmem, vmem], out_specs...  13.3 us
    all_to_all x1, starting transfers between devices, window(): received = lax.all_to_all(sent, 'comp', 0, 0, tiled=True)  10.6 us
    all_to_all x1, starting transfers between devices, window(): back = lax.all_to_all(back, 'comp', 0, 0, tiled=True)  9.8 us
    ppermute x2, starting transfers between devices, from_neighbours(): after = lax.ppermute(low, axis, [((i + 1) % count, i) for i in range(ends)])  8.56 us
    pallas_call x1, Pallas kernels, propagate(): pl.pallas_call(propagate_kernel, in_specs=[pl.BlockSpec(memory_space=pltp...  8.46 us
    ppermute x2, waiting for transfers between devices, from_neighbours(): lax.ppermute(high, axis, [(i, (i + 1) % count) for i in range(ends)])  4.23 us
  transfers between devices with their start and end apart: 9, of which 4 were waited for; matrix products, arithmetic and copies ran while one was open for 1% of the time, Pallas kernels for 3%

profile of v8, /device:TPU:6, one launch (start us, length us, event | category | flops | bytes accessed | tf_op | source)
XLA Modules:
  0.0 110.8 jit_solution(6679620554262966812)
XLA Ops:
  0.6 1.2 %rims.1 = (f32[37,4,256]{2,1,0:T(4,128)S(1)}, f32[37,4,256]{2,1,0:T(4,128)S(1)}, f32[96,256]{1,0:T(8,128)S(1)}, f32[4,96,256]{2,1,0:T(8,128)S(1)}) custom-call(f32[36,96,256]{2,1,0:T(8,128)} %spec_hbm.3, s32[96,256]{1,0:T(8,128)} %wet_hbm.1), custom_call_target="tpu_custom_call" | custom-call | tf_op jit(solution)/shard_map/rims/pallas_call | solution.py:90
  1.9 1.7 %collective-permute-start = (f32[37,4,256]{2,1,0:T(4,128)S(1)}, f32[37,4,256]{2,1,0:T(4,128)S(1)}, u32[]{:S(2)}, u32[]{:S(2)}) collective-permute-start(f32[37,4,256]{2,1,0:T(4,128)S(1)} %get-tuple-element.9), channel_id=1, source_target_pairs={{0,1},{1,2},{2,3},{4,5},{5,6},{6,7},{8,9},{9,10},{10,11},{12,13},{... | collective-permute-start | bytes 454664 | tf_op jit(solution)/shard_map/ppermute | solution.py:537
  3.6 1.3 %collective-permute-start.1 = (f32[37,4,256]{2,1,0:T(4,128)S(1)}, f32[37,4,256]{2,1,0:T(4,128)S(1)}, u32[]{:S(2)}, u32[]{:S(2)}) collective-permute-start(f32[37,4,256]{2,1,0:T(4,128)S(1)} %get-tuple-element.10), channel_id=1, source_target_pairs={{1,0},{2,1},{3,2},{5,4},{6,5},{7,6},{9,8},{10,9},{11,10},{13,12},{... | collective-permute-start | bytes 454664 | tf_op jit(solution)/shard_map/ppermute | solution.py:538
  4.9 0.1 sine_multiply_fusion
  5.0 0.0 collective-permute-done.top_ref
  5.0 3.6 %collective-permute-done.1.bot_ref = f32[37,4,256]{2,1,0:T(4,128)S(1)} collective-permute-done((f32[37,4,256]{2,1,0:T(4,128)S(1)}, f32[37,4,256]{2,1,0:T(4,128)S(1)}, u32[]{:S(2)}, u32[]{:S(2)}) %collective-permute-start.1) | collective-permute-done | bytes 151584 | tf_op jit(solution)/shard_map/ppermute | solution.py:538
  8.6 8.5 %propagate.1 = (f32[3456,128]{1,0:T(8,128)}, f32[3456,128]{1,0:T(8,128)}, bf16[32,216,128]{2,1,0:T(8,128)(2,1)}) custom-call(f32[2,36]{1,0:T(2,128)S(1)} %pad_maximum_fusion.2.speeds, f32[36,96,256]{2,1,0:T(8,128)} %spec_hbm.3, f32[37,4,256]{2,1,0:T(4,128)S(1)} %collective-permute-done.top_ref, f32[37,4,256]{2,1,0:T(4,128)S(1)} %collective-permute-done.1.bot_ref, ...), custom_call_target="tpu_custom_call" | custom-call | tf_op jit(solution)/shard_map/propagate/pallas_call | solution.py:240
  17.1 0.0 copy-start
  17.1 10.6 %all-to-all-start = ((bf16[32,216,128]{2,1,0:T(8,128)(2,1)}), bf16[32,216,128]{2,1,0:T(8,128)(2,1)S(1)}, u32[]{:S(2)}, u32[]{:S(2)}) async-start(bf16[32,216,128]{2,1,0:T(8,128)(2,1)} %get-tuple-element.13), calls=%async_computation | async-start | bytes 3538944 | tf_op jit(solution)/shard_map/all_to_all | solution.py:614
  27.7 0.1 pad.16.clone
  27.8 0.2 multiply_add_fusion.1
  28.0 0.2 multiply_add_fusion
  28.2 0.1 maximum_maximum_fusion.coef_ref
  28.3 21.3 %all-to-all-done = bf16[32,216,128]{2,1,0:T(8,128)(2,1)S(1)} async-done(((bf16[32,216,128]{2,1,0:T(8,128)(2,1)}), bf16[32,216,128]{2,1,0:T(8,128)(2,1)S(1)}, u32[]{:S(2)}, u32[]{:S(2)}) %all-to-all-start) | async-done | bytes 1769504 | tf_op jit(solution)/shard_map/all_to_all | solution.py:614
  49.6 0.0 copy-done
  49.6 13.3 %sources.1 = bf16[32,240,128]{2,1,0:T(8,128)(2,1)} custom-call(bf16[6912,128]{1,0:T(8,128)(2,1)S(1)} %bitcast.2, bf16[1152,1152]{1,0:T(8,128)(2,1)} %quad_hbm.1, f32[9,128]{1,0:T(8,128)S(1)} %bitcast.3, bf16[16,1152]{1,0:T(8,128)(2,1)S(1)} %maximum_maximum_fusion.coef_ref), custom_call_target="tpu_custom_call" | custom-call | tf_op jit(solution)/shard_map/sources/pallas_call | solution.py:392
  62.9 0.0 copy-start.2
  62.9 0.0 copy-start.1
  62.9 9.8 %all-to-all-start.1 = ((bf16[32,240,128]{2,1,0:T(8,128)(2,1)}), bf16[32,240,128]{2,1,0:T(8,128)(2,1)S(1)}, u32[]{:S(2)}, u32[]{:S(2)}) async-start(bf16[32,240,128]{2,1,0:T(8,128)(2,1)} %sources.1), calls=%async_computation.1 | async-start | bytes 3932160 | tf_op jit(solution)/shard_map/all_to_all | solution.py:634
  72.7 0.0 copy-done.2
  72.8 0.0 copy-done.1
  72.8 0.1 slice_maximum_fusion
  72.8 7.3 %collective-permute-start.3 = (f32[6,8,16]{2,1,0:T(8,128)S(1)}, f32[6,8,16]{2,1,0:T(8,128)S(1)}, u32[]{:S(2)}, u32[]{:S(2)}) collective-permute-start(f32[6,8,16]{2,1,0:T(8,128)S(1)} %get-tuple-element.19), channel_id=1, source_target_pairs={{4,0},{8,4},{12,8},{16,12},{20,16},{24,20},{28,24},{32,28},{36,32}... | collective-permute-start | bytes 9224 | tf_op jit(solution)/shard_map/ppermute | solution.py:538
  80.1 2.1 %collective-permute-start.2 = (f32[6,8,16]{2,1,0:T(8,128)S(1)}, f32[6,8,16]{2,1,0:T(8,128)S(1)}, u32[]{:S(2)}, u32[]{:S(2)}) collective-permute-start(f32[6,8,16]{2,1,0:T(8,128)S(1)} %get-tuple-element.18), channel_id=1, source_target_pairs={{0,4},{4,8},{8,12},{12,16},{16,20},{20,24},{24,28},{28,32},{32,36}... | collective-permute-start | bytes 9224 | tf_op jit(solution)/shard_map/ppermute | solution.py:537
  82.2 14.6 %collective-permute-done.3 = f32[6,8,16]{2,1,0:T(8,128)S(1)} collective-permute-done((f32[6,8,16]{2,1,0:T(8,128)S(1)}, f32[6,8,16]{2,1,0:T(8,128)S(1)}, u32[]{:S(2)}, u32[]{:S(2)}) %collective-permute-start.3) | collective-permute-done | bytes 3104 | tf_op jit(solution)/shard_map/ppermute | solution.py:538
  96.8 0.1 reshape.238
  96.9 4.2 %collective-permute-done.2 = f32[6,8,16]{2,1,0:T(8,128)S(1)} collective-permute-done((f32[6,8,16]{2,1,0:T(8,128)S(1)}, f32[6,8,16]{2,1,0:T(8,128)S(1)}, u32[]{:S(2)}, u32[]{:S(2)}) %collective-permute-start.2) | collective-permute-done | bytes 3104 | tf_op jit(solution)/shard_map/ppermute | solution.py:537
  101.1 0.1 reshape.237
  101.2 0.0 all-to-all-done.1.back_ref
  101.2 1.6 %pick.1 = f32[3,10,128]{2,1,0:T(8,128)S(1)} custom-call(bf16[32,240,128]{2,1,0:T(8,128)(2,1)S(1)} %all-to-all-done.1.back_ref, s32[30,128]{1,0:T(8,128)S(1)} %reshape.236.points_ref), custom_call_target="tpu_custom_call" | custom-call | tf_op jit(solution)/shard_map/pick/pallas_call | solution.py:451
  102.8 0.1 reshape_squeeze.7
  102.9 0.1 reshape_squeeze.6
  103.0 0.1 fusion.own_ref
  103.1 0.1 collective-permute-start.4
  103.2 0.1 collective-permute-start.5
  103.3 1.8 %collective-permute-start.6 = (f32[6,8,160]{2,1,0:T(8,128)S(1)}, f32[6,8,160]{2,1,0:T(8,128)S(1)}, u32[]{:S(2)}, u32[]{:S(2)}) collective-permute-start(f32[6,8,160]{2,1,0:T(8,128)S(1)} %fusion.own_ref), channel_id=1, source_target_pairs={{0,3},{1,2},{2,1},{3,0},{4,7},{5,6},{6,5},{7,4},{8,11},{9,10},{10,... | collective-permute-start | bytes 92168 | tf_op jit(solution)/shard_map/ppermute | solution.py:644
  105.0 3.6 %finish.1 = f32[36,96,256]{2,1,0:T(8,128)} custom-call(bf16[32,240,128]{2,1,0:T(8,128)(2,1)S(1)} %all-to-all-done.1.back_ref, f32[3456,128]{1,0:T(8,128)} %get-tuple-element.14.prop0_hbm, f32[3456,128]{1,0:T(8,128)} %get-tuple-element.15.prop1_hbm), custom_call_target="tpu_custom_call" | custom-call | tf_op jit(solution)/shard_map/finish/pallas_call | solution.py:516
  108.6 0.0 collective-permute-done.4.one_ref
  108.6 0.0 collective-permute-done.5.two_ref
  108.6 0.0 collective-permute-done.6.three_ref
  108.7 2.1 %water.1 = f32[3,8,128]{2,1,0:T(8,128)} custom-call(f32[6,8,160]{2,1,0:T(8,128)S(1)} %fusion.own_ref, f32[6,8,160]{2,1,0:T(8,128)S(1)} %collective-permute-done.4.one_ref, f32[6,8,160]{2,1,0:T(8,128)S(1)} %collective-permute-done.5.two_ref, f32[6,8,160]{2,1,0:T(8,128)S(1)} %collective-permute-done.6.three_ref), custom_call_target="tpu_custom_call" | custom-call | tf_op jit(solution)/shard_map/water/pallas_call | solution.py:593
  (11 shorter events, 0.1 us)
Async XLA Ops:
  1.9 3.1 %collective-permute-start = (f32[37,4,256]{2,1,0:T(4,128)S(1)}, f32[37,4,256]{2,1,0:T(4,128)S(1)}, u32[]{:S(2)}, u32[]{:S(2)}) collective-permute-start(f32[37,4,256]{2,1,0:T(4,128)S(1)} %get-tuple-element.9), channel_id=1, source_target_pairs={{0,1},{1,2},{2,3},{4,5},{5,6},{6,7},{8,9},{9,10},{10,11},{12,13},{... | collective-permute-start | bytes 454664 | tf_op jit(solution)/shard_map/ppermute | solution.py:537
  3.6 5.0 %collective-permute-start.1 = (f32[37,4,256]{2,1,0:T(4,128)S(1)}, f32[37,4,256]{2,1,0:T(4,128)S(1)}, u32[]{:S(2)}, u32[]{:S(2)}) collective-permute-start(f32[37,4,256]{2,1,0:T(4,128)S(1)} %get-tuple-element.10), channel_id=1, source_target_pairs={{1,0},{2,1},{3,2},{5,4},{6,5},{7,6},{9,8},{10,9},{11,10},{13,12},{... | collective-permute-start | bytes 454664 | tf_op jit(solution)/shard_map/ppermute | solution.py:538
  17.1 32.5 %copy-start = (f32[1152]{0:T(1024)S(1)}, f32[1152]{0:T(1024)}, u32[]{:S(2)}) copy-start(f32[1152]{0:T(1024)} %param.9) | copy-start | bytes 13828
  17.1 32.5 %all-to-all-start = ((bf16[32,216,128]{2,1,0:T(8,128)(2,1)}), bf16[32,216,128]{2,1,0:T(8,128)(2,1)S(1)}, u32[]{:S(2)}, u32[]{:S(2)}) async-start(bf16[32,216,128]{2,1,0:T(8,128)(2,1)} %get-tuple-element.13), calls=%async_computation | async-start | bytes 3538944 | tf_op jit(solution)/shard_map/all_to_all | solution.py:614
  62.9 9.8 %copy-start.2 = (s32[3,8,128]{2,1,0:T(8,128)S(1)}, s32[3,8,128]{2,1,0:T(8,128)}, u32[]{:S(2)}) copy-start(s32[3,8,128]{2,1,0:T(8,128)} %param.11) | copy-start | bytes 36868
  62.9 9.8 %copy-start.1 = (f32[3,8,128]{2,1,0:T(8,128)S(1)}, f32[3,8,128]{2,1,0:T(8,128)}, u32[]{:S(2)}) copy-start(f32[3,8,128]{2,1,0:T(8,128)} %param.10) | copy-start | bytes 36868
  62.9 38.3 %all-to-all-start.1 = ((bf16[32,240,128]{2,1,0:T(8,128)(2,1)}), bf16[32,240,128]{2,1,0:T(8,128)(2,1)S(1)}, u32[]{:S(2)}, u32[]{:S(2)}) async-start(bf16[32,240,128]{2,1,0:T(8,128)(2,1)} %sources.1), calls=%async_computation.1 | async-start | bytes 3932160 | tf_op jit(solution)/shard_map/all_to_all | solution.py:634
  72.8 23.9 %collective-permute-start.3 = (f32[6,8,16]{2,1,0:T(8,128)S(1)}, f32[6,8,16]{2,1,0:T(8,128)S(1)}, u32[]{:S(2)}, u32[]{:S(2)}) collective-permute-start(f32[6,8,16]{2,1,0:T(8,128)S(1)} %get-tuple-element.19), channel_id=1, source_target_pairs={{4,0},{8,4},{12,8},{16,12},{20,16},{24,20},{28,24},{32,28},{36,32}... | collective-permute-start | bytes 9224 | tf_op jit(solution)/shard_map/ppermute | solution.py:538
  80.1 21.0 %collective-permute-start.2 = (f32[6,8,16]{2,1,0:T(8,128)S(1)}, f32[6,8,16]{2,1,0:T(8,128)S(1)}, u32[]{:S(2)}, u32[]{:S(2)}) collective-permute-start(f32[6,8,16]{2,1,0:T(8,128)S(1)} %get-tuple-element.18), channel_id=1, source_target_pairs={{0,4},{4,8},{8,12},{12,16},{16,20},{20,24},{24,28},{28,32},{32,36}... | collective-permute-start | bytes 9224 | tf_op jit(solution)/shard_map/ppermute | solution.py:537
  103.1 5.5 %collective-permute-start.4 = (f32[6,8,160]{2,1,0:T(8,128)S(1)}, f32[6,8,160]{2,1,0:T(8,128)S(1)}, u32[]{:S(2)}, u32[]{:S(2)}) collective-permute-start(f32[6,8,160]{2,1,0:T(8,128)S(1)} %fusion.own_ref), channel_id=1, source_target_pairs={{0,1},{1,0},{2,3},{3,2},{4,5},{5,4},{6,7},{7,6},{8,9},{9,8},{10,11... | collective-permute-start | bytes 92168 | tf_op jit(solution)/shard_map/ppermute | solution.py:644
  103.2 5.5 %collective-permute-start.5 = (f32[6,8,160]{2,1,0:T(8,128)S(1)}, f32[6,8,160]{2,1,0:T(8,128)S(1)}, u32[]{:S(2)}, u32[]{:S(2)}) collective-permute-start(f32[6,8,160]{2,1,0:T(8,128)S(1)} %fusion.own_ref), channel_id=1, source_target_pairs={{0,2},{1,3},{2,0},{3,1},{4,6},{5,7},{6,4},{7,5},{8,10},{9,11},{10,... | collective-permute-start | bytes 92168 | tf_op jit(solution)/shard_map/ppermute | solution.py:644
  103.3 5.4 %collective-permute-start.6 = (f32[6,8,160]{2,1,0:T(8,128)S(1)}, f32[6,8,160]{2,1,0:T(8,128)S(1)}, u32[]{:S(2)}, u32[]{:S(2)}) collective-permute-start(f32[6,8,160]{2,1,0:T(8,128)S(1)} %fusion.own_ref), channel_id=1, source_target_pairs={{0,3},{1,2},{2,1},{3,0},{4,7},{5,6},{6,5},{7,4},{8,11},{9,10},{10,... | collective-permute-start | bytes 92168 | tf_op jit(solution)/shard_map/ppermute | solution.py:644

commit v9 on v8

--- a/solution.py
+++ b/solution.py
@@ -28,6 +28,7 @@
 HALO = 4
 KB = 4
 PAIR = KB
+EARLY = 3
 MARGIN = 2 * SW_STEPS
 TILES = 10
 
@@ -413,7 +414,16 @@
     )(in_vmem(received), in_hbm(quad_matrix), in_vmem(rates), in_vmem(coef))
 
 
-def pick_kernel(back_ref, points_ref, out_ref):
+def pick_kernel(
+    back_ref, points_ref, prop0_hbm, prop1_hbm, out_ref, early0, early1, sems
+):
+    rows = pl.ds(0, EARLY * KB * ROWS)
+    copies = (
+        pltpu.make_async_copy(prop0_hbm.at[rows], early0, sems.at[0]),
+        pltpu.make_async_copy(prop1_hbm.at[rows], early1, sems.at[1]),
+    )
+    for copy in copies:
+        copy.start()
     pieces = []
     for i in range(PIECES):
         at = OWN_ROWS + 8 * i
@@ -444,22 +454,28 @@
                 kept = jnp.where(within == lows[m], both[:, m * 128:(m + 1) * 128], 0.0)
                 acc = acc + weights[m] * jnp.sum(kept.reshape(16, 8, 128), axis=0)
             out_ref[c, t:t + 1, :] = jnp.sum(acc, axis=0, keepdims=True)
-
-
-def pick(back, points):
+    for copy in copies:
+        copy.wait()
+
+
+def pick(back, points, prop0, prop1):
     vmem = pl.BlockSpec(memory_space=pltpu.VMEM)
+    hbm = pl.BlockSpec(memory_space=pltpu.HBM)
+    early = pltpu.VMEM((EARLY * KB * ROWS, 128), jnp.float32)
     return pl.pallas_call(
         pick_kernel,
-        in_specs=[vmem] * 2,
-        out_specs=vmem,
-        out_shape=pltpu.VMEM((3, TILES, 128), jnp.float32),
+        in_specs=[vmem, vmem, hbm, hbm],
+        out_specs=[vmem] * 3,
+        out_shape=[pltpu.VMEM((3, TILES, 128), jnp.float32), early, early],
+        scratch_shapes=[pltpu.SemaphoreType.DMA((2,))],
         compiler_params=pltpu.CompilerParams(vmem_limit_bytes=10 << 20),
         name="pick",
-    )(in_vmem(back), in_vmem(points))
+    )(in_vmem(back), in_vmem(points), in_hbm(prop0), in_hbm(prop1))
 
 
 def finish_kernel(
-    back_ref, prop0_hbm, prop1_hbm, out_hbm, prop0, prop1, wide, out, sems, keep_sems,
+    back_ref, early0, early1, prop0_hbm, prop1_hbm, out_hbm,
+    prop0, prop1, wide, out, sems, keep_sems,
 ):
     def keep(i):
         part = pl.ds(i * KB * ROWS, KB * ROWS)
@@ -473,7 +489,7 @@
             copy.start()
         return carry
 
-    lax.fori_loop(0, LOCAL // KB, load, 0)
+    lax.fori_loop(EARLY, LOCAL // KB, load, 0)
 
     def spread(i):
         rows = pl.ds(pl.multiple_of(i * KB * RUN, 8), KB * RUN)
@@ -486,21 +502,30 @@
         part = pl.ds(i * KB, KB)
         return pltpu.make_async_copy(out.at[part], out_hbm.at[part], sems.at[i])
 
-    def add(i, carry):
-        spread(i)
-        for copy_in in keep(i):
-            copy_in.wait()
+    def add(i, halves):
         for kk in range(KB):
             k = i * KB + kk
-            for h, prop in enumerate((prop0, prop1)):
+            for h, prop in enumerate(halves):
                 rows = pl.ds(k * ROWS, ROWS)
                 out[k, :, h * 128:(h + 1) * 128] = (
                     prop[rows, :] + wide[h, kk * ROWS:(kk + 1) * ROWS, :]
                 )
         copy(i).start()
-        return carry
-
-    lax.fori_loop(0, LOCAL // KB, add, 0)
+
+    def add_early(i, carry):
+        spread(i)
+        add(i, (early0, early1))
+        return carry
+
+    def add_late(i, carry):
+        spread(i)
+        for copy_in in keep(i):
+            copy_in.wait()
+        add(i, (prop0, prop1))
+        return carry
+
+    lax.fori_loop(0, EARLY, add_early, 0)
+    lax.fori_loop(EARLY, LOCAL // KB, add_late, 0)
 
     def settle(i, carry):
         copy(i).wait()
@@ -509,13 +534,13 @@
     lax.fori_loop(0, LOCAL // KB, settle, 0)
 
 
-def finish(back, prop0, prop1):
+def finish(back, early0, early1, prop0, prop1):
     vmem = pl.BlockSpec(memory_space=pltpu.VMEM)
     hbm = pl.BlockSpec(memory_space=pltpu.HBM)
     shape = (LOCAL, ROWS, 256)
     return pl.pallas_call(
         finish_kernel,
-        in_specs=[vmem, hbm, hbm],
+        in_specs=[vmem, vmem, vmem, hbm, hbm],
         out_specs=hbm,
         out_shape=pltpu.HBM(shape, jnp.float32),
         scratch_shapes=[
@@ -528,7 +553,7 @@
         ],
         compiler_params=pltpu.CompilerParams(vmem_limit_bytes=16 << 20),
         name="finish",
-    )(in_vmem(back), in_hbm(prop0), in_hbm(prop1))
+    )(*map(in_vmem, (back, early0, early1)), in_hbm(prop0), in_hbm(prop1))
 
 
 def from_neighbours(low, high, axis):
@@ -632,7 +657,7 @@
         received.reshape(K * RUN, 128), quad_matrix, dissipation.reshape(K // 128, 128), coef
     )
     back = lax.all_to_all(back, "comp", 0, 0, tiled=True)
-    cells = pick(back, points)
+    cells, early0, early1 = pick(back, points, prop0, prop1)
     own = cells[:, :tile_rows]
     left = cells[:, tile_rows].reshape(3, tile_rows, MARGIN)
     right = cells[:, tile_rows + 1].reshape(3, tile_rows, MARGIN)
@@ -642,7 +667,7 @@
     tiles = [tile]
     for d in range(1, bands):
         tiles.append(lax.ppermute(tile, "band", [(i, i ^ d) for i in range(bands)]))
-    spectrum_out = finish(back, prop0, prop1)
+    spectrum_out = finish(back, early0, early1, prop0, prop1)
     circulation_out = shallow_water(tiles)
     return spectrum_out, circulation_out
 

time: 113 us -> 113 us (level)
    ppermute x2, waiting for transfers between devices: 18.1 us -> 3.58 us  [from_neighbours(): after = lax.ppermute(low, axis, [((i + 1) % count, i) for i in range(ends)])]
    ppermute x2, waiting for transfers between devices: 4.23 us -> 17.7 us  [from_neighbours(): lax.ppermute(high, axis, [(i, (i + 1) % count) for i in range(ends)])]
    ppermute x2, starting transfers between devices: 3.85 us -> 5.12 us  [from_neighbours(): lax.ppermute(high, axis, [(i, (i + 1) % count) for i in range(ends)])]
  transfers between devices with their start and end apart: 9 -> 9, of which waited for: 4 -> 3; matrix products, arithmetic and copies ran while one was open for 1% -> 1% of each run, Pallas kernels for 3% -> 3%
where the time goes in v9:
time: 113 us; the launch traced here: 111 us
  waiting for transfers between devices  42.6 us (38%)
  starting transfers between devices  35.9 us (32%)
  Pallas kernels  30 us (27%)
    all_to_all x1, waiting for transfers between devices, window(): received = lax.all_to_all(sent, 'comp', 0, 0, tiled=True)  21.3 us
    ppermute x2, waiting for transfers between devices, from_neighbours(): lax.ppermute(high, axis, [(i, (i + 1) % count) for i in range(ends)])  17.7 us
    pallas_call x1, Pallas kernels, sources(): pl.pallas_call(source_kernel, in_specs=[vmem, hbm, vmem, vmem], out_specs...  13.3 us
    all_to_all x1, starting transfers between devices, window(): received = lax.all_to_all(sent, 'comp', 0, 0, tiled=True)  10.6 us
    all_to_all x1, starting transfers between devices, window(): back = lax.all_to_all(back, 'comp', 0, 0, tiled=True)  9.8 us
    pallas_call x1, Pallas kernels, propagate(): pl.pallas_call(propagate_kernel, in_specs=[pl.BlockSpec(memory_space=pltp...  8.46 us
    ppermute x2, starting transfers between devices, from_neighbours(): after = lax.ppermute(low, axis, [((i + 1) % count, i) for i in range(ends)])  8.45 us
    ppermute x2, starting transfers between devices, from_neighbours(): lax.ppermute(high, axis, [(i, (i + 1) % count) for i in range(ends)])  5.12 us
  transfers between devices with their start and end apart: 9, of which 3 were waited for; matrix products, arithmetic and copies ran while one was open for 1% of the time, Pallas kernels for 3%

profile of v9, /device:TPU:6, one launch (start us, length us, event | category | flops | bytes accessed | tf_op | source)
XLA Modules:
  0.0 110.7 jit_solution(16602225103382643990)
XLA Ops:
  0.6 1.2 %rims.1 = (f32[37,4,256]{2,1,0:T(4,128)S(1)}, f32[37,4,256]{2,1,0:T(4,128)S(1)}, f32[96,256]{1,0:T(8,128)S(1)}, f32[4,96,256]{2,1,0:T(8,128)S(1)}) custom-call(f32[36,96,256]{2,1,0:T(8,128)} %spec_hbm.3, s32[96,256]{1,0:T(8,128)} %wet_hbm.1), custom_call_target="tpu_custom_call" | custom-call | tf_op jit(solution)/shard_map/rims/pallas_call | solution.py:91
  1.9 1.7 %collective-permute-start = (f32[37,4,256]{2,1,0:T(4,128)S(1)}, f32[37,4,256]{2,1,0:T(4,128)S(1)}, u32[]{:S(2)}, u32[]{:S(2)}) collective-permute-start(f32[37,4,256]{2,1,0:T(4,128)S(1)} %get-tuple-element.12), channel_id=1, source_target_pairs={{0,1},{1,2},{2,3},{4,5},{5,6},{6,7},{8,9},{9,10},{10,11},{12,13},{... | collective-permute-start | bytes 454664 | tf_op jit(solution)/shard_map/ppermute | solution.py:562
  3.6 1.3 %collective-permute-start.1 = (f32[37,4,256]{2,1,0:T(4,128)S(1)}, f32[37,4,256]{2,1,0:T(4,128)S(1)}, u32[]{:S(2)}, u32[]{:S(2)}) collective-permute-start(f32[37,4,256]{2,1,0:T(4,128)S(1)} %get-tuple-element.13), channel_id=1, source_target_pairs={{1,0},{2,1},{3,2},{5,4},{6,5},{7,6},{9,8},{10,9},{11,10},{13,12},{... | collective-permute-start | bytes 454664 | tf_op jit(solution)/shard_map/ppermute | solution.py:563
  4.9 0.1 sine_multiply_fusion
  5.0 0.0 collective-permute-done.top_ref
  5.0 3.6 %collective-permute-done.1.bot_ref = f32[37,4,256]{2,1,0:T(4,128)S(1)} collective-permute-done((f32[37,4,256]{2,1,0:T(4,128)S(1)}, f32[37,4,256]{2,1,0:T(4,128)S(1)}, u32[]{:S(2)}, u32[]{:S(2)}) %collective-permute-start.1) | collective-permute-done | bytes 151584 | tf_op jit(solution)/shard_map/ppermute | solution.py:563
  8.6 8.5 %propagate.1 = (f32[3456,128]{1,0:T(8,128)}, f32[3456,128]{1,0:T(8,128)}, bf16[32,216,128]{2,1,0:T(8,128)(2,1)}) custom-call(f32[2,36]{1,0:T(2,128)S(1)} %pad_maximum_fusion.2.speeds, f32[36,96,256]{2,1,0:T(8,128)} %spec_hbm.3, f32[37,4,256]{2,1,0:T(4,128)S(1)} %collective-permute-done.top_ref, f32[37,4,256]{2,1,0:T(4,128)S(1)} %collective-permute-done.1.bot_ref, ...), custom_call_target="tpu_custom_call" | custom-call | tf_op jit(solution)/shard_map/propagate/pallas_call | solution.py:241
  17.1 0.0 copy-start
  17.1 10.6 %all-to-all-start = ((bf16[32,216,128]{2,1,0:T(8,128)(2,1)}), bf16[32,216,128]{2,1,0:T(8,128)(2,1)S(1)}, u32[]{:S(2)}, u32[]{:S(2)}) async-start(bf16[32,216,128]{2,1,0:T(8,128)(2,1)} %get-tuple-element.16), calls=%async_computation | async-start | bytes 3538944 | tf_op jit(solution)/shard_map/all_to_all | solution.py:639
  27.7 0.1 pad.16.clone
  27.8 0.2 multiply_add_fusion.1
  28.0 0.2 multiply_add_fusion
  28.2 0.1 maximum_maximum_fusion.coef_ref
  28.3 21.3 %all-to-all-done = bf16[32,216,128]{2,1,0:T(8,128)(2,1)S(1)} async-done(((bf16[32,216,128]{2,1,0:T(8,128)(2,1)}), bf16[32,216,128]{2,1,0:T(8,128)(2,1)S(1)}, u32[]{:S(2)}, u32[]{:S(2)}) %all-to-all-start) | async-done | bytes 1769504 | tf_op jit(solution)/shard_map/all_to_all | solution.py:639
  49.6 0.0 copy-done
  49.6 13.3 %sources.1 = bf16[32,240,128]{2,1,0:T(8,128)(2,1)} custom-call(bf16[6912,128]{1,0:T(8,128)(2,1)S(1)} %bitcast.2, bf16[1152,1152]{1,0:T(8,128)(2,1)} %quad_hbm.1, f32[9,128]{1,0:T(8,128)S(1)} %bitcast.3, bf16[16,1152]{1,0:T(8,128)(2,1)S(1)} %maximum_maximum_fusion.coef_ref), custom_call_target="tpu_custom_call" | custom-call | tf_op jit(solution)/shard_map/sources/pallas_call | solution.py:393
  62.9 0.0 copy-start.2
  62.9 0.0 copy-start.1
  62.9 9.8 %all-to-all-start.1 = ((bf16[32,240,128]{2,1,0:T(8,128)(2,1)}), bf16[32,240,128]{2,1,0:T(8,128)(2,1)S(1)}, u32[]{:S(2)}, u32[]{:S(2)}) async-start(bf16[32,240,128]{2,1,0:T(8,128)(2,1)} %sources.1), calls=%async_computation.1 | async-start | bytes 3932160 | tf_op jit(solution)/shard_map/all_to_all | solution.py:659
  72.7 0.0 copy-done.2
  72.8 0.0 copy-done.1
  72.8 0.1 slice_maximum_fusion
  72.8 3.4 %collective-permute-start.2 = (f32[6,8,16]{2,1,0:T(8,128)S(1)}, f32[6,8,16]{2,1,0:T(8,128)S(1)}, u32[]{:S(2)}, u32[]{:S(2)}) collective-permute-start(f32[6,8,16]{2,1,0:T(8,128)S(1)} %get-tuple-element.24), channel_id=1, source_target_pairs={{0,4},{4,8},{8,12},{12,16},{16,20},{20,24},{24,28},{28,32},{32,36}... | collective-permute-start | bytes 9224 | tf_op jit(solution)/shard_map/ppermute | solution.py:562
  76.2 7.2 %collective-permute-start.3 = (f32[6,8,16]{2,1,0:T(8,128)S(1)}, f32[6,8,16]{2,1,0:T(8,128)S(1)}, u32[]{:S(2)}, u32[]{:S(2)}) collective-permute-start(f32[6,8,16]{2,1,0:T(8,128)S(1)} %get-tuple-element.25), channel_id=1, source_target_pairs={{4,0},{8,4},{12,8},{16,12},{20,16},{24,20},{28,24},{32,28},{36,32}... | collective-permute-start | bytes 9224 | tf_op jit(solution)/shard_map/ppermute | solution.py:563
  83.4 17.7 %collective-permute-done.2 = f32[6,8,16]{2,1,0:T(8,128)S(1)} collective-permute-done((f32[6,8,16]{2,1,0:T(8,128)S(1)}, f32[6,8,16]{2,1,0:T(8,128)S(1)}, u32[]{:S(2)}, u32[]{:S(2)}) %collective-permute-start.2) | collective-permute-done | bytes 3104 | tf_op jit(solution)/shard_map/ppermute | solution.py:562
  101.1 0.1 reshape.237
  101.2 0.0 collective-permute-done.3
  101.2 0.1 reshape.238
  101.3 0.0 all-to-all-done.1.back_ref
  101.3 1.6 %pick.1 = (f32[3,10,128]{2,1,0:T(8,128)S(1)}, f32[1152,128]{1,0:T(8,128)S(1)}, f32[1152,128]{1,0:T(8,128)S(1)}) custom-call(bf16[32,240,128]{2,1,0:T(8,128)(2,1)S(1)} %all-to-all-done.1.back_ref, s32[30,128]{1,0:T(8,128)S(1)} %reshape.236.points_ref, f32[3456,128]{1,0:T(8,128)} %get-tuple-element.17.prop0_hbm, f32[3456,128]{1,0:T(8,128)} %get-tuple-element.18.prop1_hbm), custom_call_target="tpu_custom_call" | custom-call | tf_op jit(solution)/shard_map/pick/pallas_call | solution.py:465
  102.9 0.1 reshape_squeeze.6
  103.0 0.1 reshape_squeeze.7
  103.1 0.1 fusion.own_ref
  103.2 0.1 collective-permute-start.4
  103.3 0.1 collective-permute-start.5
  103.4 1.8 %collective-permute-start.6 = (f32[6,8,160]{2,1,0:T(8,128)S(1)}, f32[6,8,160]{2,1,0:T(8,128)S(1)}, u32[]{:S(2)}, u32[]{:S(2)}) collective-permute-start(f32[6,8,160]{2,1,0:T(8,128)S(1)} %fusion.own_ref), channel_id=1, source_target_pairs={{0,3},{1,2},{2,1},{3,0},{4,7},{5,6},{6,5},{7,4},{8,11},{9,10},{10,... | collective-permute-start | bytes 92168 | tf_op jit(solution)/shard_map/ppermute | solution.py:669
  105.1 3.4 %finish.1 = f32[36,96,256]{2,1,0:T(8,128)} custom-call(bf16[32,240,128]{2,1,0:T(8,128)(2,1)S(1)} %all-to-all-done.1.back_ref, f32[1152,128]{1,0:T(8,128)S(1)} %get-tuple-element.19.early0, f32[1152,128]{1,0:T(8,128)S(1)} %get-tuple-element.20.early1, f32[3456,128]{1,0:T(8,128)} %get-tuple-element.17.prop0_hbm, f32[3456,128]{1,0:T(8,128)} %get-tuple-element.18.prop1_hbm), custom_call_target="tpu_custom_call" | custom-call | tf_op jit(solution)/shard_map/finish/pallas_call | solution.py:541
  108.5 0.0 collective-permute-done.4.one_ref
  108.5 0.0 collective-permute-done.5.two_ref
  108.5 0.0 collective-permute-done.6.three_ref
  108.5 2.1 %water.1 = f32[3,8,128]{2,1,0:T(8,128)} custom-call(f32[6,8,160]{2,1,0:T(8,128)S(1)} %fusion.own_ref, f32[6,8,160]{2,1,0:T(8,128)S(1)} %collective-permute-done.4.one_ref, f32[6,8,160]{2,1,0:T(8,128)S(1)} %collective-permute-done.5.two_ref, f32[6,8,160]{2,1,0:T(8,128)S(1)} %collective-permute-done.6.three_ref), custom_call_target="tpu_custom_call" | custom-call | tf_op jit(solution)/shard_map/water/pallas_call | solution.py:618
  (11 shorter events, 0.1 us)
Async XLA Ops:
  1.9 3.1 %collective-permute-start = (f32[37,4,256]{2,1,0:T(4,128)S(1)}, f32[37,4,256]{2,1,0:T(4,128)S(1)}, u32[]{:S(2)}, u32[]{:S(2)}) collective-permute-start(f32[37,4,256]{2,1,0:T(4,128)S(1)} %get-tuple-element.12), channel_id=1, source_target_pairs={{0,1},{1,2},{2,3},{4,5},{5,6},{6,7},{8,9},{9,10},{10,11},{12,13},{... | collective-permute-start | bytes 454664 | tf_op jit(solution)/shard_map/ppermute | solution.py:562
  3.6 5.0 %collective-permute-start.1 = (f32[37,4,256]{2,1,0:T(4,128)S(1)}, f32[37,4,256]{2,1,0:T(4,128)S(1)}, u32[]{:S(2)}, u32[]{:S(2)}) collective-permute-start(f32[37,4,256]{2,1,0:T(4,128)S(1)} %get-tuple-element.13), channel_id=1, source_target_pairs={{1,0},{2,1},{3,2},{5,4},{6,5},{7,6},{9,8},{10,9},{11,10},{13,12},{... | collective-permute-start | bytes 454664 | tf_op jit(solution)/shard_map/ppermute | solution.py:563
  17.1 32.5 %copy-start = (f32[1152]{0:T(1024)S(1)}, f32[1152]{0:T(1024)}, u32[]{:S(2)}) copy-start(f32[1152]{0:T(1024)} %param.9) | copy-start | bytes 13828
  17.1 32.5 %all-to-all-start = ((bf16[32,216,128]{2,1,0:T(8,128)(2,1)}), bf16[32,216,128]{2,1,0:T(8,128)(2,1)S(1)}, u32[]{:S(2)}, u32[]{:S(2)}) async-start(bf16[32,216,128]{2,1,0:T(8,128)(2,1)} %get-tuple-element.16), calls=%async_computation | async-start | bytes 3538944 | tf_op jit(solution)/shard_map/all_to_all | solution.py:639
  62.9 9.8 %copy-start.2 = (s32[3,8,128]{2,1,0:T(8,128)S(1)}, s32[3,8,128]{2,1,0:T(8,128)}, u32[]{:S(2)}) copy-start(s32[3,8,128]{2,1,0:T(8,128)} %param.11) | copy-start | bytes 36868
  62.9 9.8 %copy-start.1 = (f32[3,8,128]{2,1,0:T(8,128)S(1)}, f32[3,8,128]{2,1,0:T(8,128)}, u32[]{:S(2)}) copy-start(f32[3,8,128]{2,1,0:T(8,128)} %param.10) | copy-start | bytes 36868
  62.9 38.4 %all-to-all-start.1 = ((bf16[32,240,128]{2,1,0:T(8,128)(2,1)}), bf16[32,240,128]{2,1,0:T(8,128)(2,1)S(1)}, u32[]{:S(2)}, u32[]{:S(2)}) async-start(bf16[32,240,128]{2,1,0:T(8,128)(2,1)} %sources.1), calls=%async_computation.1 | async-start | bytes 3932160 | tf_op jit(solution)/shard_map/all_to_all | solution.py:659
  72.8 28.3 %collective-permute-start.2 = (f32[6,8,16]{2,1,0:T(8,128)S(1)}, f32[6,8,16]{2,1,0:T(8,128)S(1)}, u32[]{:S(2)}, u32[]{:S(2)}) collective-permute-start(f32[6,8,16]{2,1,0:T(8,128)S(1)} %get-tuple-element.24), channel_id=1, source_target_pairs={{0,4},{4,8},{8,12},{12,16},{16,20},{20,24},{24,28},{28,32},{32,36}... | collective-permute-start | bytes 9224 | tf_op jit(solution)/shard_map/ppermute | solution.py:562
  76.2 25.0 %collective-permute-start.3 = (f32[6,8,16]{2,1,0:T(8,128)S(1)}, f32[6,8,16]{2,1,0:T(8,128)S(1)}, u32[]{:S(2)}, u32[]{:S(2)}) collective-permute-start(f32[6,8,16]{2,1,0:T(8,128)S(1)} %get-tuple-element.25), channel_id=1, source_target_pairs={{4,0},{8,4},{12,8},{16,12},{20,16},{24,20},{28,24},{32,28},{36,32}... | collective-permute-start | bytes 9224 | tf_op jit(solution)/shard_map/ppermute | solution.py:563
  103.2 5.3 %collective-permute-start.4 = (f32[6,8,160]{2,1,0:T(8,128)S(1)}, f32[6,8,160]{2,1,0:T(8,128)S(1)}, u32[]{:S(2)}, u32[]{:S(2)}) collective-permute-start(f32[6,8,160]{2,1,0:T(8,128)S(1)} %fusion.own_ref), channel_id=1, source_target_pairs={{0,1},{1,0},{2,3},{3,2},{4,5},{5,4},{6,7},{7,6},{8,9},{9,8},{10,11... | collective-permute-start | bytes 92168 | tf_op jit(solution)/shard_map/ppermute | solution.py:669
  103.3 5.2 %collective-permute-start.5 = (f32[6,8,160]{2,1,0:T(8,128)S(1)}, f32[6,8,160]{2,1,0:T(8,128)S(1)}, u32[]{:S(2)}, u32[]{:S(2)}) collective-permute-start(f32[6,8,160]{2,1,0:T(8,128)S(1)} %fusion.own_ref), channel_id=1, source_target_pairs={{0,2},{1,3},{2,0},{3,1},{4,6},{5,7},{6,4},{7,5},{8,10},{9,11},{10,... | collective-permute-start | bytes 92168 | tf_op jit(solution)/shard_map/ppermute | solution.py:669
  103.4 5.2 %collective-permute-start.6 = (f32[6,8,160]{2,1,0:T(8,128)S(1)}, f32[6,8,160]{2,1,0:T(8,128)S(1)}, u32[]{:S(2)}, u32[]{:S(2)}) collective-permute-start(f32[6,8,160]{2,1,0:T(8,128)S(1)} %fusion.own_ref), channel_id=1, source_target_pairs={{0,3},{1,2},{2,1},{3,0},{4,7},{5,6},{6,5},{7,4},{8,11},{9,10},{10,... | collective-permute-start | bytes 92168 | tf_op jit(solution)/shard_map/ppermute | solution.py:669

commit v10 on v9

--- a/solution.py
+++ b/solution.py
@@ -473,101 +473,10 @@
     )(in_vmem(back), in_vmem(points), in_hbm(prop0), in_hbm(prop1))
 
 
-def finish_kernel(
-    back_ref, early0, early1, prop0_hbm, prop1_hbm, out_hbm,
-    prop0, prop1, wide, out, sems, keep_sems,
-):
-    def keep(i):
-        part = pl.ds(i * KB * ROWS, KB * ROWS)
-        return [
-            pltpu.make_async_copy(hbm.at[part], prop.at[part], keep_sems.at[h, i])
-            for h, (prop, hbm) in enumerate(((prop0, prop0_hbm), (prop1, prop1_hbm)))
-        ]
-
-    def load(i, carry):
-        for copy in keep(i):
-            copy.start()
-        return carry
-
-    lax.fori_loop(EARLY, LOCAL // KB, load, 0)
-
-    def spread(i):
-        rows = pl.ds(pl.multiple_of(i * KB * RUN, 8), KB * RUN)
-        for h in range(2):
-            for g in range(GROUP):
-                gain = back_ref[h * GROUP + g, rows, :].astype(jnp.float32)
-                wide[h, pl.ds(g, KB * RUN, stride=GROUP), :] = gain
-
-    def copy(i):
-        part = pl.ds(i * KB, KB)
-        return pltpu.make_async_copy(out.at[part], out_hbm.at[part], sems.at[i])
-
-    def add(i, halves):
-        for kk in range(KB):
-            k = i * KB + kk
-            for h, prop in enumerate(halves):
-                rows = pl.ds(k * ROWS, ROWS)
-                out[k, :, h * 128:(h + 1) * 128] = (
-                    prop[rows, :] + wide[h, kk * ROWS:(kk + 1) * ROWS, :]
-                )
-        copy(i).start()
-
-    def add_early(i, carry):
-        spread(i)
-        add(i, (early0, early1))
-        return carry
-
-    def add_late(i, carry):
-        spread(i)
-        for copy_in in keep(i):
-            copy_in.wait()
-        add(i, (prop0, prop1))
-        return carry
-
-    lax.fori_loop(0, EARLY, add_early, 0)
-    lax.fori_loop(EARLY, LOCAL // KB, add_late, 0)
-
-    def settle(i, carry):
-        copy(i).wait()
-        return carry
-
-    lax.fori_loop(0, LOCAL // KB, settle, 0)
-
-
-def finish(back, early0, early1, prop0, prop1):
-    vmem = pl.BlockSpec(memory_space=pltpu.VMEM)
-    hbm = pl.BlockSpec(memory_space=pltpu.HBM)
-    shape = (LOCAL, ROWS, 256)
-    return pl.pallas_call(
-        finish_kernel,
-        in_specs=[vmem, vmem, vmem, hbm, hbm],
-        out_specs=hbm,
-        out_shape=pltpu.HBM(shape, jnp.float32),
-        scratch_shapes=[
-            pltpu.VMEM((LOCAL * ROWS, 128), jnp.float32),
-            pltpu.VMEM((LOCAL * ROWS, 128), jnp.float32),
-            pltpu.VMEM((2, KB * ROWS, 128), jnp.float32),
-            pltpu.VMEM(shape, jnp.float32),
-            pltpu.SemaphoreType.DMA((LOCAL // KB,)),
-            pltpu.SemaphoreType.DMA((2, LOCAL // KB)),
-        ],
-        compiler_params=pltpu.CompilerParams(vmem_limit_bytes=16 << 20),
-        name="finish",
-    )(*map(in_vmem, (back, early0, early1)), in_hbm(prop0), in_hbm(prop1))
-
-
-def from_neighbours(low, high, axis):
-    count = lax.axis_size(axis)
-    ends = count - 1
-    before = lax.ppermute(high, axis, [(i, (i + 1) % count) for i in range(ends)])
-    after = lax.ppermute(low, axis, [((i + 1) % count, i) for i in range(ends)])
-    return before, after
-
-
 WIDE = 256
 
 
-def water_kernel(own_ref, one_ref, two_ref, three_ref, out_ref, whole, result):
+def water(own_ref, one_ref, two_ref, three_ref, out_ref, whole, result):
     bands = 4
     tile = own_ref.shape[1]
     width = own_ref.shape[2]
@@ -611,22 +520,134 @@
         out_ref[c] = result[c, pl.ds(pl.multiple_of(band * tile, tile), tile), :]
 
 
-def shallow_water(tiles):
+def spread(back_ref, wide, i):
+    rows = pl.ds(pl.multiple_of(i * KB * RUN, 8), KB * RUN)
+    for h in range(2):
+        for g in range(GROUP):
+            gain = back_ref[h * GROUP + g, rows, :].astype(jnp.float32)
+            wide[h, pl.ds(g, KB * RUN, stride=GROUP), :] = gain
+
+
+def add(halves, wide, out, i):
+    for kk in range(KB):
+        k = i * KB + kk
+        for h, prop in enumerate(halves):
+            rows = pl.ds(k * ROWS, ROWS)
+            out[k, :, h * 128:(h + 1) * 128] = (
+                prop[rows, :] + wide[h, kk * ROWS:(kk + 1) * ROWS, :]
+            )
+
+
+def group_copy(out, out_hbm, sems, i):
+    part = pl.ds(i * KB, KB)
+    return pltpu.make_async_copy(out.at[part], out_hbm.at[part], sems.at[i])
+
+
+def begin_kernel(back_ref, early0, early1, out_hbm, wide, out, sems):
+    def one(i, carry):
+        spread(back_ref, wide, i)
+        add((early0, early1), wide, out, i)
+        group_copy(out, out_hbm, sems, i).start()
+        return carry
+
+    def settle(i, carry):
+        group_copy(out, out_hbm, sems, i).wait()
+        return carry
+
+    lax.fori_loop(0, EARLY, one, 0)
+    lax.fori_loop(0, EARLY, settle, 0)
+
+
+def begin_sum(back, early0, early1):
     vmem = pl.BlockSpec(memory_space=pltpu.VMEM)
+    hbm = pl.BlockSpec(memory_space=pltpu.HBM)
+    return pl.pallas_call(
+        begin_kernel,
+        in_specs=[vmem] * 3,
+        out_specs=hbm,
+        out_shape=pltpu.HBM((LOCAL, ROWS, 256), jnp.float32),
+        scratch_shapes=[
+            pltpu.VMEM((2, KB * ROWS, 128), jnp.float32),
+            pltpu.VMEM((EARLY * KB, ROWS, 256), jnp.float32),
+            pltpu.SemaphoreType.DMA((EARLY,)),
+        ],
+        compiler_params=pltpu.CompilerParams(vmem_limit_bytes=8 << 20),
+        name="begin",
+    )(*map(in_vmem, (back, early0, early1)))
+
+
+def close_kernel(
+    back_ref, prop0_hbm, prop1_hbm, begun_hbm, own_ref, one_ref, two_ref, three_ref,
+    out_hbm, water_ref, prop0, prop1, wide, out, sems, keep_sems, whole, result,
+):
+    count = LOCAL // KB
+
+    def keep(i):
+        part = pl.ds(i * KB * ROWS, KB * ROWS)
+        return [
+            pltpu.make_async_copy(hbm.at[part], prop.at[part], keep_sems.at[h, i])
+            for h, (prop, hbm) in enumerate(((prop0, prop0_hbm), (prop1, prop1_hbm)))
+        ]
+
+    def load(i, carry):
+        for copy in keep(i):
+            copy.start()
+        return carry
+
+    def one(i, carry):
+        spread(back_ref, wide, i)
+        for copy in keep(i):
+            copy.wait()
+        add((prop0, prop1), wide, out, i)
+        group_copy(out, out_hbm, sems, i).start()
+        return carry
+
+    def settle(i, carry):
+        group_copy(out, out_hbm, sems, i).wait()
+        return carry
+
+    lax.fori_loop(EARLY, count, load, 0)
+    lax.fori_loop(EARLY, count, one, 0)
+    water(own_ref, one_ref, two_ref, three_ref, water_ref, whole, result)
+    lax.fori_loop(EARLY, count, settle, 0)
+
+
+def close_sum(back, prop0, prop1, begun, tiles):
+    vmem = pl.BlockSpec(memory_space=pltpu.VMEM)
+    hbm = pl.BlockSpec(memory_space=pltpu.HBM)
     fields, rows, width = tiles[0].shape
     own_cols = width - 2 * MARGIN
+    shape = (LOCAL, ROWS, 256)
     return pl.pallas_call(
-        water_kernel,
-        in_specs=[vmem] * 4,
-        out_specs=vmem,
-        out_shape=jax.ShapeDtypeStruct((3, rows, own_cols), jnp.float32),
+        close_kernel,
+        in_specs=[vmem, hbm, hbm, hbm] + [vmem] * 4,
+        out_specs=[hbm, vmem],
+        out_shape=[
+            pltpu.HBM(shape, jnp.float32),
+            jax.ShapeDtypeStruct((3, rows, own_cols), jnp.float32),
+        ],
+        input_output_aliases={3: 0},
         scratch_shapes=[
+            pltpu.VMEM((LOCAL * ROWS, 128), jnp.float32),
+            pltpu.VMEM((LOCAL * ROWS, 128), jnp.float32),
+            pltpu.VMEM((2, KB * ROWS, 128), jnp.float32),
+            pltpu.VMEM(shape, jnp.float32),
+            pltpu.SemaphoreType.DMA((LOCAL // KB,)),
+            pltpu.SemaphoreType.DMA((2, LOCAL // KB)),
             pltpu.VMEM((fields, 4 * rows, WIDE), jnp.float32),
             pltpu.VMEM((3, 4 * rows, own_cols), jnp.float32),
         ],
-        compiler_params=pltpu.CompilerParams(vmem_limit_bytes=4 << 20),
-        name="water",
-    )(*map(in_vmem, tiles))
+        compiler_params=pltpu.CompilerParams(vmem_limit_bytes=18 << 20),
+        name="close",
+    )(in_vmem(back), *map(in_hbm, (prop0, prop1, begun)), *map(in_vmem, tiles))
+
+
+def from_neighbours(low, high, axis):
+    count = lax.axis_size(axis)
+    ends = count - 1
+    before = lax.ppermute(high, axis, [(i, (i + 1) % count) for i in range(ends)])
+    after = lax.ppermute(low, axis, [((i + 1) % count, i) for i in range(ends)])
+    return before, after
 
 
 def window(spectrum, wet_mask, quad_matrix, dissipation, circulation, source_points):
@@ -667,8 +688,8 @@
     tiles = [tile]
     for d in range(1, bands):
         tiles.append(lax.ppermute(tile, "band", [(i, i ^ d) for i in range(bands)]))
-    spectrum_out = finish(back, early0, early1, prop0, prop1)
-    circulation_out = shallow_water(tiles)
+    begun = begin_sum(back, early0, early1)
+    spectrum_out, circulation_out = close_sum(back, prop0, prop1, begun, tiles)
     return spectrum_out, circulation_out
 
 

time: 113 us -> 114 us (level)
  waiting for transfers between devices: 42.6 us -> 44 us
    ppermute x3, waiting for transfers between devices: 0.01 us -> 1.36 us  [window(): tiles.append(lax.ppermute(tile, 'band', [(i, i ^ d) for i in range(bands)]))]
  transfers between devices with their start and end apart: 9 -> 9, of which waited for: 3 -> 5; matrix products, arithmetic and copies ran while one was open for 1% -> 1% of each run, Pallas kernels for 3% -> 1%
where the time goes in v10:
time: 114 us; the launch traced here: 112 us
  waiting for transfers between devices  44 us (39%)
  starting transfers between devices  35.9 us (31%)
  Pallas kernels  30.3 us (27%)
    all_to_all x1, waiting for transfers between devices, window(): received = lax.all_to_all(sent, 'comp', 0, 0, tiled=True)  21.3 us
    ppermute x2, waiting for transfers between devices, from_neighbours(): lax.ppermute(high, axis, [(i, (i + 1) % count) for i in range(ends)])  17.7 us
    pallas_call x1, Pallas kernels, sources(): pl.pallas_call(source_kernel, in_specs=[vmem, hbm, vmem, vmem], out_specs...  13.3 us
    all_to_all x1, starting transfers between devices, window(): received = lax.all_to_all(sent, 'comp', 0, 0, tiled=True)  10.6 us
    all_to_all x1, starting transfers between devices, window(): back = lax.all_to_all(back, 'comp', 0, 0, tiled=True)  9.8 us
    pallas_call x1, Pallas kernels, propagate(): pl.pallas_call(propagate_kernel, in_specs=[pl.BlockSpec(memory_space=pltp...  8.46 us
    ppermute x2, starting transfers between devices, from_neighbours(): after = lax.ppermute(low, axis, [((i + 1) % count, i) for i in range(ends)])  8.45 us
    ppermute x2, starting transfers between devices, from_neighbours(): lax.ppermute(high, axis, [(i, (i + 1) % count) for i in range(ends)])  5.12 us
  transfers between devices with their start and end apart: 9, of which 5 were waited for; matrix products, arithmetic and copies ran while one was open for 1% of the time, Pallas kernels for 1%

profile of v10, /device:TPU:6, one launch (start us, length us, event | category | flops | bytes accessed | tf_op | source)
XLA Modules:
  0.0 112.4 jit_solution(3700304834843949119)
XLA Ops:
  0.6 1.2 %rims.1 = (f32[37,4,256]{2,1,0:T(4,128)S(1)}, f32[37,4,256]{2,1,0:T(4,128)S(1)}, f32[96,256]{1,0:T(8,128)S(1)}, f32[4,96,256]{2,1,0:T(8,128)S(1)}) custom-call(f32[36,96,256]{2,1,0:T(8,128)} %spec_hbm.3, s32[96,256]{1,0:T(8,128)} %wet_hbm.1), custom_call_target="tpu_custom_call" | custom-call | tf_op jit(solution)/shard_map/rims/pallas_call | solution.py:91
  1.9 1.7 %collective-permute-start = (f32[37,4,256]{2,1,0:T(4,128)S(1)}, f32[37,4,256]{2,1,0:T(4,128)S(1)}, u32[]{:S(2)}, u32[]{:S(2)}) collective-permute-start(f32[37,4,256]{2,1,0:T(4,128)S(1)} %get-tuple-element.12), channel_id=1, source_target_pairs={{0,1},{1,2},{2,3},{4,5},{5,6},{6,7},{8,9},{9,10},{10,11},{12,13},{... | collective-permute-start | bytes 454664 | tf_op jit(solution)/shard_map/ppermute | solution.py:648
  3.6 1.3 %collective-permute-start.1 = (f32[37,4,256]{2,1,0:T(4,128)S(1)}, f32[37,4,256]{2,1,0:T(4,128)S(1)}, u32[]{:S(2)}, u32[]{:S(2)}) collective-permute-start(f32[37,4,256]{2,1,0:T(4,128)S(1)} %get-tuple-element.13), channel_id=1, source_target_pairs={{1,0},{2,1},{3,2},{5,4},{6,5},{7,6},{9,8},{10,9},{11,10},{13,12},{... | collective-permute-start | bytes 454664 | tf_op jit(solution)/shard_map/ppermute | solution.py:649
  4.9 0.1 sine_multiply_fusion
  5.0 0.0 collective-permute-done.top_ref
  5.0 3.6 %collective-permute-done.1.bot_ref = f32[37,4,256]{2,1,0:T(4,128)S(1)} collective-permute-done((f32[37,4,256]{2,1,0:T(4,128)S(1)}, f32[37,4,256]{2,1,0:T(4,128)S(1)}, u32[]{:S(2)}, u32[]{:S(2)}) %collective-permute-start.1) | collective-permute-done | bytes 151584 | tf_op jit(solution)/shard_map/ppermute | solution.py:649
  8.6 8.5 %propagate.1 = (f32[3456,128]{1,0:T(8,128)}, f32[3456,128]{1,0:T(8,128)}, bf16[32,216,128]{2,1,0:T(8,128)(2,1)}) custom-call(f32[2,36]{1,0:T(2,128)S(1)} %pad_maximum_fusion.2.speeds, f32[36,96,256]{2,1,0:T(8,128)} %spec_hbm.3, f32[37,4,256]{2,1,0:T(4,128)S(1)} %collective-permute-done.top_ref, f32[37,4,256]{2,1,0:T(4,128)S(1)} %collective-permute-done.1.bot_ref, ...), custom_call_target="tpu_custom_call" | custom-call | tf_op jit(solution)/shard_map/propagate/pallas_call | solution.py:241
  17.1 0.0 copy-start
  17.1 10.6 %all-to-all-start = ((bf16[32,216,128]{2,1,0:T(8,128)(2,1)}), bf16[32,216,128]{2,1,0:T(8,128)(2,1)S(1)}, u32[]{:S(2)}, u32[]{:S(2)}) async-start(bf16[32,216,128]{2,1,0:T(8,128)(2,1)} %get-tuple-element.16), calls=%async_computation | async-start | bytes 3538944 | tf_op jit(solution)/shard_map/all_to_all | solution.py:660
  27.7 0.1 pad.16.clone
  27.8 0.2 multiply_add_fusion.1
  28.0 0.2 multiply_add_fusion
  28.2 0.1 maximum_maximum_fusion.coef_ref
  28.3 21.3 %all-to-all-done = bf16[32,216,128]{2,1,0:T(8,128)(2,1)S(1)} async-done(((bf16[32,216,128]{2,1,0:T(8,128)(2,1)}), bf16[32,216,128]{2,1,0:T(8,128)(2,1)S(1)}, u32[]{:S(2)}, u32[]{:S(2)}) %all-to-all-start) | async-done | bytes 1769504 | tf_op jit(solution)/shard_map/all_to_all | solution.py:660
  49.6 0.0 copy-done
  49.6 13.3 %sources.1 = bf16[32,240,128]{2,1,0:T(8,128)(2,1)} custom-call(bf16[6912,128]{1,0:T(8,128)(2,1)S(1)} %bitcast.2, bf16[1152,1152]{1,0:T(8,128)(2,1)} %quad_hbm.1, f32[9,128]{1,0:T(8,128)S(1)} %bitcast.3, bf16[16,1152]{1,0:T(8,128)(2,1)S(1)} %maximum_maximum_fusion.coef_ref), custom_call_target="tpu_custom_call" | custom-call | tf_op jit(solution)/shard_map/sources/pallas_call | solution.py:393
  62.9 0.0 copy-start.2
  62.9 0.0 copy-start.1
  62.9 9.8 %all-to-all-start.1 = ((bf16[32,240,128]{2,1,0:T(8,128)(2,1)}), bf16[32,240,128]{2,1,0:T(8,128)(2,1)S(1)}, u32[]{:S(2)}, u32[]{:S(2)}) async-start(bf16[32,240,128]{2,1,0:T(8,128)(2,1)} %sources.1), calls=%async_computation.1 | async-start | bytes 3932160 | tf_op jit(solution)/shard_map/all_to_all | solution.py:680
  72.7 0.0 copy-done.2
  72.8 0.0 copy-done.1
  72.8 0.1 slice_maximum_fusion
  72.8 3.4 %collective-permute-start.2 = (f32[6,8,16]{2,1,0:T(8,128)S(1)}, f32[6,8,16]{2,1,0:T(8,128)S(1)}, u32[]{:S(2)}, u32[]{:S(2)}) collective-permute-start(f32[6,8,16]{2,1,0:T(8,128)S(1)} %get-tuple-element.24), channel_id=1, source_target_pairs={{0,4},{4,8},{8,12},{12,16},{16,20},{20,24},{24,28},{28,32},{32,36}... | collective-permute-start | bytes 9224 | tf_op jit(solution)/shard_map/ppermute | solution.py:648
  76.2 7.2 %collective-permute-start.3 = (f32[6,8,16]{2,1,0:T(8,128)S(1)}, f32[6,8,16]{2,1,0:T(8,128)S(1)}, u32[]{:S(2)}, u32[]{:S(2)}) collective-permute-start(f32[6,8,16]{2,1,0:T(8,128)S(1)} %get-tuple-element.25), channel_id=1, source_target_pairs={{4,0},{8,4},{12,8},{16,12},{20,16},{24,20},{28,24},{32,28},{36,32}... | collective-permute-start | bytes 9224 | tf_op jit(solution)/shard_map/ppermute | solution.py:649
  83.4 17.7 %collective-permute-done.2 = f32[6,8,16]{2,1,0:T(8,128)S(1)} collective-permute-done((f32[6,8,16]{2,1,0:T(8,128)S(1)}, f32[6,8,16]{2,1,0:T(8,128)S(1)}, u32[]{:S(2)}, u32[]{:S(2)}) %collective-permute-start.2) | collective-permute-done | bytes 3104 | tf_op jit(solution)/shard_map/ppermute | solution.py:648
  101.1 0.1 reshape.237
  101.2 0.0 collective-permute-done.3
  101.2 0.1 reshape.238
  101.3 0.0 all-to-all-done.1.back_ref
  101.3 1.6 %pick.1 = (f32[3,10,128]{2,1,0:T(8,128)S(1)}, f32[1152,128]{1,0:T(8,128)S(1)}, f32[1152,128]{1,0:T(8,128)S(1)}) custom-call(bf16[32,240,128]{2,1,0:T(8,128)(2,1)S(1)} %all-to-all-done.1.back_ref, s32[30,128]{1,0:T(8,128)S(1)} %reshape.236.points_ref, f32[3456,128]{1,0:T(8,128)} %get-tuple-element.17.prop0_hbm, f32[3456,128]{1,0:T(8,128)} %get-tuple-element.18.prop1_hbm), custom_call_target="tpu_custom_call" | custom-call | tf_op jit(solution)/shard_map/pick/pallas_call | solution.py:465
  102.9 0.1 reshape_squeeze.6
  103.0 0.1 reshape_squeeze.7
  103.1 0.1 fusion.own_ref
  103.2 0.1 collective-permute-start.6
  103.3 0.8 collective-permute-start.5
  104.1 1.0 collective-permute-start.4
  105.1 1.3 %begin.1.begun_hbm = f32[36,96,256]{2,1,0:T(8,128)} custom-call(bf16[32,240,128]{2,1,0:T(8,128)(2,1)S(1)} %all-to-all-done.1.back_ref, f32[1152,128]{1,0:T(8,128)S(1)} %get-tuple-element.19.early0, f32[1152,128]{1,0:T(8,128)S(1)} %get-tuple-element.20.early1), custom_call_target="tpu_custom_call" | custom-call | tf_op jit(solution)/shard_map/begin/pallas_call | solution.py:564
  106.5 0.3 collective-permute-done.6.three_ref
  106.8 1.1 collective-permute-done.5.two_ref
  107.8 0.0 collective-permute-done.4.one_ref
  107.8 4.4 %close.1 = (f32[36,96,256]{2,1,0:T(8,128)}, f32[3,8,128]{2,1,0:T(8,128)}) custom-call(bf16[32,240,128]{2,1,0:T(8,128)(2,1)S(1)} %all-to-all-done.1.back_ref, f32[3456,128]{1,0:T(8,128)} %get-tuple-element.17.prop0_hbm, f32[3456,128]{1,0:T(8,128)} %get-tuple-element.18.prop1_hbm, f32[36,96,256]{2,1,0:T(8,128)} %begin.1.begun_hbm, ...), custom_call_target="tpu_custom_call", output_to_operand_aliasing={{0}: (3, {})} | custom-call | tf_op jit(solution)/shard_map/close/pallas_call | solution.py:621
  (11 shorter events, 0.1 us)
Async XLA Ops:
  1.9 3.1 %collective-permute-start = (f32[37,4,256]{2,1,0:T(4,128)S(1)}, f32[37,4,256]{2,1,0:T(4,128)S(1)}, u32[]{:S(2)}, u32[]{:S(2)}) collective-permute-start(f32[37,4,256]{2,1,0:T(4,128)S(1)} %get-tuple-element.12), channel_id=1, source_target_pairs={{0,1},{1,2},{2,3},{4,5},{5,6},{6,7},{8,9},{9,10},{10,11},{12,13},{... | collective-permute-start | bytes 454664 | tf_op jit(solution)/shard_map/ppermute | solution.py:648
  3.6 5.0 %collective-permute-start.1 = (f32[37,4,256]{2,1,0:T(4,128)S(1)}, f32[37,4,256]{2,1,0:T(4,128)S(1)}, u32[]{:S(2)}, u32[]{:S(2)}) collective-permute-start(f32[37,4,256]{2,1,0:T(4,128)S(1)} %get-tuple-element.13), channel_id=1, source_target_pairs={{1,0},{2,1},{3,2},{5,4},{6,5},{7,6},{9,8},{10,9},{11,10},{13,12},{... | collective-permute-start | bytes 454664 | tf_op jit(solution)/shard_map/ppermute | solution.py:649
  17.1 32.5 %copy-start = (f32[1152]{0:T(1024)S(1)}, f32[1152]{0:T(1024)}, u32[]{:S(2)}) copy-start(f32[1152]{0:T(1024)} %param.9) | copy-start | bytes 13828
  17.1 32.5 %all-to-all-start = ((bf16[32,216,128]{2,1,0:T(8,128)(2,1)}), bf16[32,216,128]{2,1,0:T(8,128)(2,1)S(1)}, u32[]{:S(2)}, u32[]{:S(2)}) async-start(bf16[32,216,128]{2,1,0:T(8,128)(2,1)} %get-tuple-element.16), calls=%async_computation | async-start | bytes 3538944 | tf_op jit(solution)/shard_map/all_to_all | solution.py:660
  62.9 9.8 %copy-start.2 = (s32[3,8,128]{2,1,0:T(8,128)S(1)}, s32[3,8,128]{2,1,0:T(8,128)}, u32[]{:S(2)}) copy-start(s32[3,8,128]{2,1,0:T(8,128)} %param.11) | copy-start | bytes 36868
  62.9 9.8 %copy-start.1 = (f32[3,8,128]{2,1,0:T(8,128)S(1)}, f32[3,8,128]{2,1,0:T(8,128)}, u32[]{:S(2)}) copy-start(f32[3,8,128]{2,1,0:T(8,128)} %param.10) | copy-start | bytes 36868
  62.9 38.4 %all-to-all-start.1 = ((bf16[32,240,128]{2,1,0:T(8,128)(2,1)}), bf16[32,240,128]{2,1,0:T(8,128)(2,1)S(1)}, u32[]{:S(2)}, u32[]{:S(2)}) async-start(bf16[32,240,128]{2,1,0:T(8,128)(2,1)} %sources.1), calls=%async_computation.1 | async-start | bytes 3932160 | tf_op jit(solution)/shard_map/all_to_all | solution.py:680
  72.8 28.3 %collective-permute-start.2 = (f32[6,8,16]{2,1,0:T(8,128)S(1)}, f32[6,8,16]{2,1,0:T(8,128)S(1)}, u32[]{:S(2)}, u32[]{:S(2)}) collective-permute-start(f32[6,8,16]{2,1,0:T(8,128)S(1)} %get-tuple-element.24), channel_id=1, source_target_pairs={{0,4},{4,8},{8,12},{12,16},{16,20},{20,24},{24,28},{28,32},{32,36}... | collective-permute-start | bytes 9224 | tf_op jit(solution)/shard_map/ppermute | solution.py:648
  76.2 25.0 %collective-permute-start.3 = (f32[6,8,16]{2,1,0:T(8,128)S(1)}, f32[6,8,16]{2,1,0:T(8,128)S(1)}, u32[]{:S(2)}, u32[]{:S(2)}) collective-permute-start(f32[6,8,16]{2,1,0:T(8,128)S(1)} %get-tuple-element.25), channel_id=1, source_target_pairs={{4,0},{8,4},{12,8},{16,12},{20,16},{24,20},{28,24},{32,28},{36,32}... | collective-permute-start | bytes 9224 | tf_op jit(solution)/shard_map/ppermute | solution.py:649
  103.2 3.6 %collective-permute-start.6 = (f32[6,8,160]{2,1,0:T(8,128)S(1)}, f32[6,8,160]{2,1,0:T(8,128)S(1)}, u32[]{:S(2)}, u32[]{:S(2)}) collective-permute-start(f32[6,8,160]{2,1,0:T(8,128)S(1)} %fusion.own_ref), channel_id=1, source_target_pairs={{0,3},{1,2},{2,1},{3,0},{4,7},{5,6},{6,5},{7,4},{8,11},{9,10},{10,... | collective-permute-start | bytes 92168 | tf_op jit(solution)/shard_map/ppermute | solution.py:690
  103.3 4.6 %collective-permute-start.5 = (f32[6,8,160]{2,1,0:T(8,128)S(1)}, f32[6,8,160]{2,1,0:T(8,128)S(1)}, u32[]{:S(2)}, u32[]{:S(2)}) collective-permute-start(f32[6,8,160]{2,1,0:T(8,128)S(1)} %fusion.own_ref), channel_id=1, source_target_pairs={{0,2},{1,3},{2,0},{3,1},{4,6},{5,7},{6,4},{7,5},{8,10},{9,11},{10,... | collective-permute-start | bytes 92168 | tf_op jit(solution)/shard_map/ppermute | solution.py:690
  104.1 3.7 %collective-permute-start.4 = (f32[6,8,160]{2,1,0:T(8,128)S(1)}, f32[6,8,160]{2,1,0:T(8,128)S(1)}, u32[]{:S(2)}, u32[]{:S(2)}) collective-permute-start(f32[6,8,160]{2,1,0:T(8,128)S(1)} %fusion.own_ref), channel_id=1, source_target_pairs={{0,1},{1,0},{2,3},{3,2},{4,5},{5,4},{6,7},{7,6},{8,9},{9,8},{10,11... | collective-permute-start | bytes 92168 | tf_op jit(solution)/shard_map/ppermute | solution.py:690
